TPU v7x, 32 devices: a whole 2x2x4 slice. The times are simulated.
32 devices in a mesh: patch: 16 (over z, x, core), sec: 2 (over y).
Axes of the slice: x: 2, y: 2, z: 4, core: 2. Of those that a mesh axis runs over, the one named last changes fastest.
Arguments:
- concentration: float32 [16, 8, 128, 128], P('patch', 'sec'), may hold values from -1 to 1
- partner: int32 [16, 4], replicated, may hold values from 0 to 15, as said below
- face_id: int32 [16, 4], replicated, may hold values from 0 to 3, as said below
- flip: int32 [16, 4], replicated, may hold values from 0 to 1, as said below
Outputs:
- evolved: float32 [16, 8, 128, 128], P('patch', 'sec')
Inputs may be any that keep to these rules, and one draw needn't show every extreme that they name: Across face f of patch p lies face face_id[p, f] of patch partner[p, f], and across that face lies face f of patch p again; the four partners of a patch are four different patches, none of them p itself. `face_id`: see partner. `flip`: equal on the two sides of an interface.
All inputs are finite; a program needn't handle non-finite values.
Results may differ from a plain program's by a relative error of at most 0.0001.
Values sent between devices are 32-bit elements; how exact they have to be, the bound alone decides.
No kernel may reach another device: no remote copies, remote signals or barrier semaphores. Data moves between devices by JAX's collectives and lax.ppermute only.
A program may use at most 64 MiB of HBM per device.

v0:
```python
import jax
import jax.numpy as jnp
from jax import lax
from jax.sharding import PartitionSpec as P

ITERS = 3
STEPS = 2


MASS_BAND = (2416.0 / 5040.0, 1191.0 / 5040.0, 120.0 / 5040.0, 1.0 / 5040.0)
STIFF_BAND = (2.0 / 3.0, -0.125, -0.2, -1.0 / 120.0)
PENALTY = 2.0
TIME_STEP = 1.0
STABILIZER = 2.0
GRADIENT_ENERGY = 0.5


def padded_2(cells, sides, width):
    for axis, dim in sides:
        count = lax.axis_size(axis)
        ends = count - 1
        head = lax.slice_in_dim(cells, 0, width, axis=dim)
        tail = lax.slice_in_dim(cells, cells.shape[dim] - width, cells.shape[dim], axis=dim)
        cells = jnp.concatenate(
            [
                lax.ppermute(tail, axis, [(i, (i + 1) % count) for i in range(ends)]),
                cells,
                lax.ppermute(head, axis, [((i + 1) % count, i) for i in range(ends)]),
            ],
            axis=dim,
        )
    return cells


def banded_padded(padded, coefficients, along, length):
    summed = coefficients[0] * lax.slice_in_dim(padded, 3, 3 + length, axis=along)
    for offset in range(1, 4):
        lower = lax.slice_in_dim(padded, 3 - offset, 3 - offset + length, axis=along)
        upper = lax.slice_in_dim(padded, 3 + offset, 3 + offset + length, axis=along)
        summed = summed + coefficients[offset] * (lower + upper)
    return summed


def banded(field, coefficients, along):
    length = field.shape[along]
    widths = [(0, 0)] * field.ndim
    widths[along] = (3, 3)
    return banded_padded(jnp.pad(field, widths), coefficients, along, length)


def tensor_parts(mass_third, stiff_third, first_axis, second_axis):
    mass_both = banded(mass_third, MASS_BAND, second_axis)
    stiff_second = banded(mass_third, STIFF_BAND, second_axis)
    mixed_second = banded(stiff_third, MASS_BAND, second_axis)
    stiffness = banded(mass_both, STIFF_BAND, first_axis) + banded(
        stiff_second + mixed_second, MASS_BAND, first_axis
    )
    return (mass_both, stiffness)


def face_traces(field):
    return jnp.stack(
        [field[..., 0, :], field[..., -1, :], field[..., :, 0], field[..., :, -1]],
        axis=field.ndim - 3,
    )


def add_penalty(stiffness, mismatch, face_axis):
    pieces = [lax.index_in_dim(mismatch, number, face_axis, keepdims=False) for number in range(4)]
    stiffness = stiffness.at[..., 0, :].add(PENALTY * pieces[0])
    stiffness = stiffness.at[..., -1, :].add(PENALTY * pieces[1])
    stiffness = stiffness.at[..., :, 0].add(PENALTY * pieces[2])
    stiffness = stiffness.at[..., :, -1].add(PENALTY * pieces[3])
    return stiffness


def partner_traces(traces, partner_row, face_row, flip_row):
    all_traces = lax.all_gather(traces[None], "patch", axis=0, tiled=True)
    picked = all_traces[partner_row, face_row]
    return jnp.where(flip_row[:, None, None] == 1, picked[..., ::-1], picked)


def stiffness_local(field, tables, with_mass):
    length = field.shape[0]
    padded = padded_2(field, (("sec", 0),), 3)
    mass_third = banded_padded(padded, MASS_BAND, 0, length)
    stiff_third = banded_padded(padded, STIFF_BAND, 0, length)
    mass_both, stiffness = tensor_parts(mass_third, stiff_third, 1, 2)
    traces = face_traces(field)
    others = partner_traces(traces, tables[0], tables[1], tables[2])
    stiffness = add_penalty(stiffness, traces - others, 0)
    mass_full = banded(mass_both, MASS_BAND, 1) if with_mass else None
    return (mass_full, stiffness)


def operate(direction, tables):
    mass_full, stiff_one = stiffness_local(direction, tables, True)
    unused, stiff_two = stiffness_local(stiff_one, tables, False)
    return mass_full + TIME_STEP * STABILIZER * stiff_one + TIME_STEP * GRADIENT_ENERGY * stiff_two


def squares(residual):
    return lax.psum(jnp.sum(residual * residual), ("patch", "sec"))


def shards(concentration, partner, face_id, flip):
    patch_now = lax.axis_index("patch")
    tables = (
        lax.dynamic_index_in_dim(partner, patch_now, 0, keepdims=False),
        lax.dynamic_index_in_dim(face_id, patch_now, 0, keepdims=False),
        lax.dynamic_index_in_dim(flip, patch_now, 0, keepdims=False),
    )
    iterate = concentration[0]
    for section in range(STEPS):
        current = iterate
        unused, curvature = stiffness_local(current, tables, False)
        potential = current * current * current - current + GRADIENT_ENERGY * curvature
        unused, flux = stiffness_local(potential, tables, False)
        residual = -TIME_STEP * flux
        direction = residual
        norm_now = squares(residual)
        for iteration in range(ITERS):
            image = operate(direction, tables)
            step_size = norm_now / lax.psum(jnp.sum(direction * image), ("patch", "sec"))
            iterate = iterate + step_size * direction
            if iteration + 1 < ITERS:
                residual = residual - step_size * image
                norm_next = squares(residual)
                direction = residual + norm_next / norm_now * direction
                norm_now = norm_next
    return iterate[None]


def solution(mesh):
    placed = (P("patch", "sec", None, None), P(), P(), P())
    return jax.shard_map(
        shards, mesh=mesh, in_specs=placed, out_specs=P("patch", "sec", None, None), check_vma=False
    )
```

profile of v0, /device:TPU:0, one launch (start us, length us, event | category | flops | bytes accessed | tf_op | source)
XLA Modules:
  0.0 1100.8 jit_solution(2193271219574866490)
XLA Ops:
  2.5 4.9 collective-permute-start
  7.8 23.1 %all-gather = f32[64,4,128]{2,1,0:T(4,128)S(1)} all-gather(f32[4,4,128]{2,1,0:T(4,128)S(1)} %pad_maximum_fusion.32), channel_id=2, replica_groups=mesh['patch'=16,'sec'=2] {'patch'}, dimensions={0}, use_global_device_ids=true | all-gather | bytes 139264 | tf_op jit(solution)/shard_map/all_gather | solution.py:78
  39.5 10.8 scatter-add.215
  52.4 4.6 collective-permute-start.2
  57.0 17.7 %all-gather.1 = f32[64,4,128]{2,1,0:T(4,128)S(1)} all-gather(f32[4,4,128]{2,1,0:T(4,128)S(1)} %pad_maximum_fusion.33), channel_id=3, replica_groups=mesh['patch'=16,'sec'=2] {'patch'}, dimensions={0}, use_global_device_ids=true | all-gather | bytes 139264 | tf_op jit(solution)/shard_map/all_gather | solution.py:78
  81.7 4.6 collective-permute-start.4
  86.5 19.4 %all-gather.2 = f32[64,4,128]{2,1,0:T(4,128)S(1)} all-gather(f32[4,4,128]{2,1,0:T(4,128)S(1)} %pad_maximum_fusion.34), channel_id=4, replica_groups=mesh['patch'=16,'sec'=2] {'patch'}, dimensions={0}, use_global_device_ids=true | all-gather | bytes 139264 | tf_op jit(solution)/shard_map/all_gather | solution.py:78
  113.0 10.8 scatter-add.229
  125.5 4.6 collective-permute-start.6
  130.3 17.9 %all-gather.3 = f32[64,4,128]{2,1,0:T(4,128)S(1)} all-gather(f32[4,4,128]{2,1,0:T(4,128)S(1)} %pad_maximum_fusion.35), channel_id=5, replica_groups=mesh['patch'=16,'sec'=2] {'patch'}, dimensions={0}, use_global_device_ids=true | all-gather | bytes 139264 | tf_op jit(solution)/shard_map/all_gather | solution.py:78
  155.0 10.8 scatter-add.235
  167.4 37.5 %all-reduce.65 = (f32[]{:T(128)}, f32[]{:T(128)}) all-reduce(f32[]{:T(128)} %get-tuple-element.776, f32[]{:T(128)} %get-tuple-element.775), channel_id=1, replica_groups=mesh['patch'=16,'sec'=2] {'patch','sec'}, use_global_device_ids=true, to_apply=%region_1.2 | all-reduce | flops 2 | bytes 16 | tf_op jit(solution)/shard_map/psum | solution.py:103
  206.9 42.8 %psum.86 = f32[]{:T(128)} all-reduce(f32[]{:T(128)} %get-tuple-element.825), channel_id=1, replica_groups=mesh['patch'=16,'sec'=2] {'patch','sec'}, use_global_device_ids=true, to_apply=%region_5.6 | all-reduce | flops 1 | bytes 8 | tf_op jit(solution)/shard_map/psum | solution.py:103
  252.7 4.6 collective-permute-start.8
  257.5 20.9 %all-gather.4 = f32[64,4,128]{2,1,0:T(4,128)S(1)} all-gather(f32[4,4,128]{2,1,0:T(4,128)S(1)} %pad_maximum_fusion.36), channel_id=6, replica_groups=mesh['patch'=16,'sec'=2] {'patch'}, dimensions={0}, use_global_device_ids=true | all-gather | bytes 139264 | tf_op jit(solution)/shard_map/all_gather | solution.py:78
  285.3 10.8 scatter-add.241
  303.2 17.7 %all-gather.5 = f32[64,4,128]{2,1,0:T(4,128)S(1)} all-gather(f32[4,4,128]{2,1,0:T(4,128)S(1)} %pad_maximum_fusion.37), channel_id=7, replica_groups=mesh['patch'=16,'sec'=2] {'patch'}, dimensions={0}, use_global_device_ids=true | all-gather | bytes 139264 | tf_op jit(solution)/shard_map/all_gather | solution.py:78
  327.7 10.8 scatter-add.249
  340.0 37.4 %psum.87 = f32[]{:T(128)} all-reduce(f32[]{:T(128)} %get-tuple-element.817), channel_id=1, replica_groups=mesh['patch'=16,'sec'=2] {'patch','sec'}, use_global_device_ids=true, to_apply=%region_7.8 | all-reduce | flops 1 | bytes 8 | tf_op jit(solution)/shard_map/psum | solution.py:124
  379.5 42.8 %psum.88 = f32[]{:T(128)} all-reduce(f32[]{:T(128)} %multiply_reduce_fusion.7), channel_id=1, replica_groups=mesh['patch'=16,'sec'=2] {'patch','sec'}, use_global_device_ids=true, to_apply=%region_9.10 | all-reduce | flops 1 | bytes 8 | tf_op jit(solution)/shard_map/psum | solution.py:103
  425.3 4.6 collective-permute-start.12
  430.1 21.0 %all-gather.6 = f32[64,4,128]{2,1,0:T(4,128)S(1)} all-gather(f32[4,4,128]{2,1,0:T(4,128)S(1)} %pad_maximum_fusion.38), channel_id=8, replica_groups=mesh['patch'=16,'sec'=2] {'patch'}, dimensions={0}, use_global_device_ids=true | all-gather | bytes 139264 | tf_op jit(solution)/shard_map/all_gather | solution.py:78
  457.9 10.8 scatter-add.255
  475.8 18.0 %all-gather.7 = f32[64,4,128]{2,1,0:T(4,128)S(1)} all-gather(f32[4,4,128]{2,1,0:T(4,128)S(1)} %pad_maximum_fusion.39), channel_id=9, replica_groups=mesh['patch'=16,'sec'=2] {'patch'}, dimensions={0}, use_global_device_ids=true | all-gather | bytes 139264 | tf_op jit(solution)/shard_map/all_gather | solution.py:78
  500.6 10.8 scatter-add.261
  512.9 37.4 %psum.89 = f32[]{:T(128)} all-reduce(f32[]{:T(128)} %multiply_reduce_fusion.6), channel_id=1, replica_groups=mesh['patch'=16,'sec'=2] {'patch','sec'}, use_global_device_ids=true, to_apply=%region_11.12 | all-reduce | flops 1 | bytes 8 | tf_op jit(solution)/shard_map/psum | solution.py:124
  553.4 4.6 collective-permute-start.16
  558.3 21.6 %all-gather.8 = f32[64,4,128]{2,1,0:T(4,128)S(1)} all-gather(f32[4,4,128]{2,1,0:T(4,128)S(1)} %pad_maximum_fusion.40), channel_id=10, replica_groups=mesh['patch'=16,'sec'=2] {'patch'}, dimensions={0}, use_global_device_ids=true | all-gather | bytes 139264 | tf_op jit(solution)/shard_map/all_gather | solution.py:78
  586.7 10.8 scatter-add.269
  604.1 17.7 %all-gather.9 = f32[64,4,128]{2,1,0:T(4,128)S(1)} all-gather(f32[4,4,128]{2,1,0:T(4,128)S(1)} %pad_maximum_fusion.41), channel_id=11, replica_groups=mesh['patch'=16,'sec'=2] {'patch'}, dimensions={0}, use_global_device_ids=true | all-gather | bytes 139264 | tf_op jit(solution)/shard_map/all_gather | solution.py:78
  628.6 10.8 scatter-add.275
  646.2 19.7 %all-gather.10 = f32[64,4,128]{2,1,0:T(4,128)S(1)} all-gather(f32[4,4,128]{2,1,0:T(4,128)S(1)} %pad_maximum_fusion.42), channel_id=12, replica_groups=mesh['patch'=16,'sec'=2] {'patch'}, dimensions={0}, use_global_device_ids=true | all-gather | bytes 139264 | tf_op jit(solution)/shard_map/all_gather | solution.py:78
  673.6 10.8 scatter-add.281
  691.7 18.0 %all-gather.11 = f32[64,4,128]{2,1,0:T(4,128)S(1)} all-gather(f32[4,4,128]{2,1,0:T(4,128)S(1)} %pad_maximum_fusion.43), channel_id=13, replica_groups=mesh['patch'=16,'sec'=2] {'patch'}, dimensions={0}, use_global_device_ids=true | all-gather | bytes 139264 | tf_op jit(solution)/shard_map/all_gather | solution.py:78
  716.7 10.8 scatter-add.289
  728.6 37.5 %all-reduce.64 = (f32[]{:T(128)}, f32[]{:T(128)}) all-reduce(f32[]{:T(128)} %get-tuple-element.774, f32[]{:T(128)} %get-tuple-element.773), channel_id=1, replica_groups=mesh['patch'=16,'sec'=2] {'patch','sec'}, use_global_device_ids=true, to_apply=%region_13.14 | all-reduce | flops 2 | bytes 16 | tf_op jit(solution)/shard_map/psum | solution.py:103
  768.4 42.9 %psum.92 = f32[]{:T(128)} all-reduce(f32[]{:T(128)} %get-tuple-element.797), channel_id=1, replica_groups=mesh['patch'=16,'sec'=2] {'patch','sec'}, use_global_device_ids=true, to_apply=%region_17.18 | all-reduce | flops 1 | bytes 8 | tf_op jit(solution)/shard_map/psum | solution.py:103
  818.8 20.9 %all-gather.12 = f32[64,4,128]{2,1,0:T(4,128)S(1)} all-gather(f32[4,4,128]{2,1,0:T(4,128)S(1)} %pad_maximum_fusion.44), channel_id=14, replica_groups=mesh['patch'=16,'sec'=2] {'patch'}, dimensions={0}, use_global_device_ids=true | all-gather | bytes 139264 | tf_op jit(solution)/shard_map/all_gather | solution.py:78
  847.4 10.8 scatter-add.299
  859.6 4.6 collective-permute-start.26
  864.3 17.7 %all-gather.13 = f32[64,4,128]{2,1,0:T(4,128)S(1)} all-gather(f32[4,4,128]{2,1,0:T(4,128)S(1)} %pad_maximum_fusion.45), channel_id=15, replica_groups=mesh['patch'=16,'sec'=2] {'patch'}, dimensions={0}, use_global_device_ids=true | all-gather | bytes 139264 | tf_op jit(solution)/shard_map/all_gather | solution.py:78
  889.9 10.8 scatter-add.305
  901.6 37.4 %psum.93 = f32[]{:T(128)} all-reduce(f32[]{:T(128)} %multiply_reduce_fusion.2), channel_id=1, replica_groups=mesh['patch'=16,'sec'=2] {'patch','sec'}, use_global_device_ids=true, to_apply=%region_19.20 | all-reduce | flops 1 | bytes 8 | tf_op jit(solution)/shard_map/psum | solution.py:124
  941.1 42.8 %psum.94 = f32[]{:T(128)} all-reduce(f32[]{:T(128)} %get-tuple-element.789), channel_id=1, replica_groups=mesh['patch'=16,'sec'=2] {'patch','sec'}, use_global_device_ids=true, to_apply=%region_21.22 | all-reduce | flops 1 | bytes 8 | tf_op jit(solution)/shard_map/psum | solution.py:103
  991.4 21.0 %all-gather.14 = f32[64,4,128]{2,1,0:T(4,128)S(1)} all-gather(f32[4,4,128]{2,1,0:T(4,128)S(1)} %pad_maximum_fusion.46), channel_id=16, replica_groups=mesh['patch'=16,'sec'=2] {'patch'}, dimensions={0}, use_global_device_ids=true | all-gather | bytes 139264 | tf_op jit(solution)/shard_map/all_gather | solution.py:78
  1020.1 10.8 scatter-add.311
  1037.0 17.5 %all-gather.15 = f32[64,4,128]{2,1,0:T(4,128)S(1)} all-gather(f32[4,4,128]{2,1,0:T(4,128)S(1)} %pad_maximum_fusion.47), channel_id=17, replica_groups=mesh['patch'=16,'sec'=2] {'patch'}, dimensions={0}, use_global_device_ids=true | all-gather | bytes 139264 | tf_op jit(solution)/shard_map/all_gather | solution.py:78
  1060.6 37.4 %psum.95 = f32[]{:T(128)} all-reduce(f32[]{:T(128)} %multiply_reduce_fusion), channel_id=1, replica_groups=mesh['patch'=16,'sec'=2] {'patch','sec'}, use_global_device_ids=true, to_apply=%region_23.24 | all-reduce | flops 1 | bytes 8 | tf_op jit(solution)/shard_map/psum | solution.py:124
  (441 shorter events, 191.9 us)
Async XLA Ops:
  1.1 6.3 copy-start
  1.2 32.5 %collective-permute-start.1 = (f32[3,128,128]{1,0,2:T(4,128)S(1)}, f32[3,128,128]{1,0,2:T(4,128)S(1)}, u32[]{:S(2)}, u32[]{:S(2)}) collective-permute-start(f32[3,128,128]{1,0,2:T(4,128)S(1)} %get-tuple-element.957), channel_id=1, source_target_pairs={{1,0},{3,2},{5,4},{7,6},{9,8},{11,10},{13,12},{15,14},{17,16},{19,... | collective-permute-start | bytes 589832 | tf_op jit(solution)/shard_map/ppermute | solution.py:28
  2.5 31.2 %collective-permute-start = (f32[3,128,128]{1,0,2:T(4,128)S(1)}, f32[3,128,128]{1,0,2:T(4,128)S(1)}, u32[]{:S(2)}, u32[]{:S(2)}) collective-permute-start(f32[3,128,128]{1,0,2:T(4,128)S(1)} %get-tuple-element.956), channel_id=1, source_target_pairs={{0,1},{2,3},{4,5},{6,7},{8,9},{10,11},{12,13},{14,15},{16,17},{18,... | collective-permute-start | bytes 589832 | tf_op jit(solution)/shard_map/ppermute | solution.py:26
  30.9 0.7 copy-start.3
  30.9 0.7 copy-start.2
  32.4 0.7 copy-start.1
  51.1 24.5 %collective-permute-start.3 = (f32[3,128,128]{2,0,1:T(4,128)S(1)}, f32[3,128,128]{2,0,1:T(4,128)S(1)}, u32[]{:S(2)}, u32[]{:S(2)}) collective-permute-start(f32[3,128,128]{2,0,1:T(4,128)S(1)} %get-tuple-element.949), channel_id=1, source_target_pairs={{1,0},{3,2},{5,4},{7,6},{9,8},{11,10},{13,12},{15,14},{17,16},{19,... | collective-permute-start | bytes 589832 | tf_op jit(solution)/shard_map/ppermute | solution.py:28
  52.4 23.2 %collective-permute-start.2 = (f32[3,128,128]{2,0,1:T(4,128)S(1)}, f32[3,128,128]{2,0,1:T(4,128)S(1)}, u32[]{:S(2)}, u32[]{:S(2)}) collective-permute-start(f32[3,128,128]{2,0,1:T(4,128)S(1)} %get-tuple-element.948), channel_id=1, source_target_pairs={{0,1},{2,3},{4,5},{6,7},{8,9},{10,11},{12,13},{14,15},{16,17},{18,... | collective-permute-start | bytes 589832 | tf_op jit(solution)/shard_map/ppermute | solution.py:26
  80.4 26.3 %collective-permute-start.5 = (f32[3,128,128]{1,0,2:T(4,128)S(1)}, f32[3,128,128]{1,0,2:T(4,128)S(1)}, u32[]{:S(2)}, u32[]{:S(2)}) collective-permute-start(f32[3,128,128]{1,0,2:T(4,128)S(1)} %get-tuple-element.945), channel_id=1, source_target_pairs={{1,0},{3,2},{5,4},{7,6},{9,8},{11,10},{13,12},{15,14},{17,16},{19,... | collective-permute-start | bytes 589832 | tf_op jit(solution)/shard_map/ppermute | solution.py:28
  81.7 25.0 %collective-permute-start.4 = (f32[3,128,128]{1,0,2:T(4,128)S(1)}, f32[3,128,128]{1,0,2:T(4,128)S(1)}, u32[]{:S(2)}, u32[]{:S(2)}) collective-permute-start(f32[3,128,128]{1,0,2:T(4,128)S(1)} %get-tuple-element.944), channel_id=1, source_target_pairs={{0,1},{2,3},{4,5},{6,7},{8,9},{10,11},{12,13},{14,15},{16,17},{18,... | collective-permute-start | bytes 589832 | tf_op jit(solution)/shard_map/ppermute | solution.py:26
  124.2 25.1 %collective-permute-start.7 = (f32[3,128,128]{1,0,2:T(4,128)S(1)}, f32[3,128,128]{1,0,2:T(4,128)S(1)}, u32[]{:S(2)}, u32[]{:S(2)}) collective-permute-start(f32[3,128,128]{1,0,2:T(4,128)S(1)} %get-tuple-element.937), channel_id=1, source_target_pairs={{1,0},{3,2},{5,4},{7,6},{9,8},{11,10},{13,12},{15,14},{17,16},{19,... | collective-permute-start | bytes 589832 | tf_op jit(solution)/shard_map/ppermute | solution.py:28
  125.5 23.8 %collective-permute-start.6 = (f32[3,128,128]{1,0,2:T(4,128)S(1)}, f32[3,128,128]{1,0,2:T(4,128)S(1)}, u32[]{:S(2)}, u32[]{:S(2)}) collective-permute-start(f32[3,128,128]{1,0,2:T(4,128)S(1)} %get-tuple-element.936), channel_id=1, source_target_pairs={{0,1},{2,3},{4,5},{6,7},{8,9},{10,11},{12,13},{14,15},{16,17},{18,... | collective-permute-start | bytes 589832 | tf_op jit(solution)/shard_map/ppermute | solution.py:26
  251.4 28.1 %collective-permute-start.9 = (f32[3,128,128]{1,0,2:T(4,128)S(1)}, f32[3,128,128]{1,0,2:T(4,128)S(1)}, u32[]{:S(2)}, u32[]{:S(2)}) collective-permute-start(f32[3,128,128]{1,0,2:T(4,128)S(1)} %get-tuple-element.931), channel_id=1, source_target_pairs={{1,0},{3,2},{5,4},{7,6},{9,8},{11,10},{13,12},{15,14},{17,16},{19,... | collective-permute-start | bytes 589832 | tf_op jit(solution)/shard_map/ppermute | solution.py:28
  252.7 26.8 %collective-permute-start.8 = (f32[3,128,128]{1,0,2:T(4,128)S(1)}, f32[3,128,128]{1,0,2:T(4,128)S(1)}, u32[]{:S(2)}, u32[]{:S(2)}) collective-permute-start(f32[3,128,128]{1,0,2:T(4,128)S(1)} %get-tuple-element.930), channel_id=1, source_target_pairs={{0,1},{2,3},{4,5},{6,7},{8,9},{10,11},{12,13},{14,15},{16,17},{18,... | collective-permute-start | bytes 589832 | tf_op jit(solution)/shard_map/ppermute | solution.py:26
  297.1 24.9 %collective-permute-start.11 = (f32[3,128,128]{1,0,2:T(4,128)}, f32[3,128,128]{1,0,2:T(4,128)S(1)}, u32[]{:S(2)}, u32[]{:S(2)}) collective-permute-start(f32[3,128,128]{1,0,2:T(4,128)} %get-tuple-element.923), channel_id=1, source_target_pairs={{1,0},{3,2},{5,4},{7,6},{9,8},{11,10},{13,12},{15,14},{17,16},{19,... | collective-permute-start | bytes 589832 | tf_op jit(solution)/shard_map/ppermute | solution.py:28
  298.4 23.7 %collective-permute-start.10 = (f32[3,128,128]{1,0,2:T(4,128)S(1)}, f32[3,128,128]{1,0,2:T(4,128)S(1)}, u32[]{:S(2)}, u32[]{:S(2)}) collective-permute-start(f32[3,128,128]{1,0,2:T(4,128)S(1)} %get-tuple-element.922), channel_id=1, source_target_pairs={{0,1},{2,3},{4,5},{6,7},{8,9},{10,11},{12,13},{14,15},{16,17},{18,... | collective-permute-start | bytes 589832 | tf_op jit(solution)/shard_map/ppermute | solution.py:26
  424.0 28.2 %collective-permute-start.13 = (f32[3,128,128]{1,0,2:T(4,128)S(1)}, f32[3,128,128]{1,0,2:T(4,128)S(1)}, u32[]{:S(2)}, u32[]{:S(2)}) collective-permute-start(f32[3,128,128]{1,0,2:T(4,128)S(1)} %get-tuple-element.917), channel_id=1, source_target_pairs={{1,0},{3,2},{5,4},{7,6},{9,8},{11,10},{13,12},{15,14},{17,16},{19,... | collective-permute-start | bytes 589832 | tf_op jit(solution)/shard_map/ppermute | solution.py:28
  425.3 26.9 %collective-permute-start.12 = (f32[3,128,128]{1,0,2:T(4,128)S(1)}, f32[3,128,128]{1,0,2:T(4,128)S(1)}, u32[]{:S(2)}, u32[]{:S(2)}) collective-permute-start(f32[3,128,128]{1,0,2:T(4,128)S(1)} %get-tuple-element.916), channel_id=1, source_target_pairs={{0,1},{2,3},{4,5},{6,7},{8,9},{10,11},{12,13},{14,15},{16,17},{18,... | collective-permute-start | bytes 589832 | tf_op jit(solution)/shard_map/ppermute | solution.py:26
  469.7 25.2 %collective-permute-start.15 = (f32[3,128,128]{1,0,2:T(4,128)}, f32[3,128,128]{1,0,2:T(4,128)S(1)}, u32[]{:S(2)}, u32[]{:S(2)}) collective-permute-start(f32[3,128,128]{1,0,2:T(4,128)} %get-tuple-element.909), channel_id=1, source_target_pairs={{1,0},{3,2},{5,4},{7,6},{9,8},{11,10},{13,12},{15,14},{17,16},{19,... | collective-permute-start | bytes 589832 | tf_op jit(solution)/shard_map/ppermute | solution.py:28
  471.0 23.9 %collective-permute-start.14 = (f32[3,128,128]{1,0,2:T(4,128)S(1)}, f32[3,128,128]{1,0,2:T(4,128)S(1)}, u32[]{:S(2)}, u32[]{:S(2)}) collective-permute-start(f32[3,128,128]{1,0,2:T(4,128)S(1)} %get-tuple-element.908), channel_id=1, source_target_pairs={{0,1},{2,3},{4,5},{6,7},{8,9},{10,11},{12,13},{14,15},{16,17},{18,... | collective-permute-start | bytes 589832 | tf_op jit(solution)/shard_map/ppermute | solution.py:26
  552.1 28.9 %collective-permute-start.17 = (f32[3,128,128]{1,0,2:T(4,128)S(1)}, f32[3,128,128]{1,0,2:T(4,128)S(1)}, u32[]{:S(2)}, u32[]{:S(2)}) collective-permute-start(f32[3,128,128]{1,0,2:T(4,128)S(1)} %get-tuple-element.903), channel_id=1, source_target_pairs={{1,0},{3,2},{5,4},{7,6},{9,8},{11,10},{13,12},{15,14},{17,16},{19,... | collective-permute-start | bytes 589832 | tf_op jit(solution)/shard_map/ppermute | solution.py:28
  553.4 27.6 %collective-permute-start.16 = (f32[3,128,128]{1,0,2:T(4,128)S(1)}, f32[3,128,128]{1,0,2:T(4,128)S(1)}, u32[]{:S(2)}, u32[]{:S(2)}) collective-permute-start(f32[3,128,128]{1,0,2:T(4,128)S(1)} %get-tuple-element.902), channel_id=1, source_target_pairs={{0,1},{2,3},{4,5},{6,7},{8,9},{10,11},{12,13},{14,15},{16,17},{18,... | collective-permute-start | bytes 589832 | tf_op jit(solution)/shard_map/ppermute | solution.py:26
  597.9 24.9 %collective-permute-start.19 = (f32[3,128,128]{1,0,2:T(4,128)S(1)}, f32[3,128,128]{1,0,2:T(4,128)S(1)}, u32[]{:S(2)}, u32[]{:S(2)}) collective-permute-start(f32[3,128,128]{1,0,2:T(4,128)S(1)} %get-tuple-element.895), channel_id=1, source_target_pairs={{1,0},{3,2},{5,4},{7,6},{9,8},{11,10},{13,12},{15,14},{17,16},{19,... | collective-permute-start | bytes 589832 | tf_op jit(solution)/shard_map/ppermute | solution.py:28
  599.2 23.7 %collective-permute-start.18 = (f32[3,128,128]{1,0,2:T(4,128)S(1)}, f32[3,128,128]{1,0,2:T(4,128)S(1)}, u32[]{:S(2)}, u32[]{:S(2)}) collective-permute-start(f32[3,128,128]{1,0,2:T(4,128)S(1)} %get-tuple-element.894), channel_id=1, source_target_pairs={{0,1},{2,3},{4,5},{6,7},{8,9},{10,11},{12,13},{14,15},{16,17},{18,... | collective-permute-start | bytes 589832 | tf_op jit(solution)/shard_map/ppermute | solution.py:26
  640.1 26.9 %collective-permute-start.21 = (f32[3,128,128]{1,0,2:T(4,128)S(1)}, f32[3,128,128]{1,0,2:T(4,128)S(1)}, u32[]{:S(2)}, u32[]{:S(2)}) collective-permute-start(f32[3,128,128]{1,0,2:T(4,128)S(1)} %get-tuple-element.887), channel_id=1, source_target_pairs={{1,0},{3,2},{5,4},{7,6},{9,8},{11,10},{13,12},{15,14},{17,16},{19,... | collective-permute-start | bytes 589832 | tf_op jit(solution)/shard_map/ppermute | solution.py:28
  641.4 25.6 %collective-permute-start.20 = (f32[3,128,128]{1,0,2:T(4,128)S(1)}, f32[3,128,128]{1,0,2:T(4,128)S(1)}, u32[]{:S(2)}, u32[]{:S(2)}) collective-permute-start(f32[3,128,128]{1,0,2:T(4,128)S(1)} %get-tuple-element.886), channel_id=1, source_target_pairs={{0,1},{2,3},{4,5},{6,7},{8,9},{10,11},{12,13},{14,15},{16,17},{18,... | collective-permute-start | bytes 589832 | tf_op jit(solution)/shard_map/ppermute | solution.py:26
  685.6 25.4 %collective-permute-start.23 = (f32[3,128,128]{1,0,2:T(4,128)}, f32[3,128,128]{1,0,2:T(4,128)S(1)}, u32[]{:S(2)}, u32[]{:S(2)}) collective-permute-start(f32[3,128,128]{1,0,2:T(4,128)} %get-tuple-element.879), channel_id=1, source_target_pairs={{1,0},{3,2},{5,4},{7,6},{9,8},{11,10},{13,12},{15,14},{17,16},{19,... | collective-permute-start | bytes 589832 | tf_op jit(solution)/shard_map/ppermute | solution.py:28
  686.9 24.1 %collective-permute-start.22 = (f32[3,128,128]{1,0,2:T(4,128)S(1)}, f32[3,128,128]{1,0,2:T(4,128)S(1)}, u32[]{:S(2)}, u32[]{:S(2)}) collective-permute-start(f32[3,128,128]{1,0,2:T(4,128)S(1)} %get-tuple-element.878), channel_id=1, source_target_pairs={{0,1},{2,3},{4,5},{6,7},{8,9},{10,11},{12,13},{14,15},{16,17},{18,... | collective-permute-start | bytes 589832 | tf_op jit(solution)/shard_map/ppermute | solution.py:26
  812.9 27.7 %collective-permute-start.25 = (f32[3,128,128]{2,0,1:T(4,128)S(1)}, f32[3,128,128]{2,0,1:T(4,128)S(1)}, u32[]{:S(2)}, u32[]{:S(2)}) collective-permute-start(f32[3,128,128]{2,0,1:T(4,128)S(1)} %get-tuple-element.871), channel_id=1, source_target_pairs={{1,0},{3,2},{5,4},{7,6},{9,8},{11,10},{13,12},{15,14},{17,16},{19,... | collective-permute-start | bytes 589832 | tf_op jit(solution)/shard_map/ppermute | solution.py:28
  814.2 26.4 %collective-permute-start.24 = (f32[3,128,128]{2,0,1:T(4,128)S(1)}, f32[3,128,128]{2,0,1:T(4,128)S(1)}, u32[]{:S(2)}, u32[]{:S(2)}) collective-permute-start(f32[3,128,128]{2,0,1:T(4,128)S(1)} %get-tuple-element.870), channel_id=1, source_target_pairs={{0,1},{2,3},{4,5},{6,7},{8,9},{10,11},{12,13},{14,15},{16,17},{18,... | collective-permute-start | bytes 589832 | tf_op jit(solution)/shard_map/ppermute | solution.py:26
  858.3 24.8 %collective-permute-start.27 = (f32[3,128,128]{2,0,1:T(4,128)S(1)}, f32[3,128,128]{2,0,1:T(4,128)S(1)}, u32[]{:S(2)}, u32[]{:S(2)}) collective-permute-start(f32[3,128,128]{2,0,1:T(4,128)S(1)} %get-tuple-element.863), channel_id=1, source_target_pairs={{1,0},{3,2},{5,4},{7,6},{9,8},{11,10},{13,12},{15,14},{17,16},{19,... | collective-permute-start | bytes 589832 | tf_op jit(solution)/shard_map/ppermute | solution.py:28
  859.6 23.5 %collective-permute-start.26 = (f32[3,128,128]{2,0,1:T(4,128)S(1)}, f32[3,128,128]{2,0,1:T(4,128)S(1)}, u32[]{:S(2)}, u32[]{:S(2)}) collective-permute-start(f32[3,128,128]{2,0,1:T(4,128)S(1)} %get-tuple-element.862), channel_id=1, source_target_pairs={{0,1},{2,3},{4,5},{6,7},{8,9},{10,11},{12,13},{14,15},{16,17},{18,... | collective-permute-start | bytes 589832 | tf_op jit(solution)/shard_map/ppermute | solution.py:26
  985.5 27.8 %collective-permute-start.29 = (f32[3,128,128]{2,0,1:T(4,128)S(1)}, f32[3,128,128]{2,0,1:T(4,128)S(1)}, u32[]{:S(2)}, u32[]{:S(2)}) collective-permute-start(f32[3,128,128]{2,0,1:T(4,128)S(1)} %get-tuple-element.855), channel_id=1, source_target_pairs={{1,0},{3,2},{5,4},{7,6},{9,8},{11,10},{13,12},{15,14},{17,16},{19,... | collective-permute-start | bytes 589832 | tf_op jit(solution)/shard_map/ppermute | solution.py:28
  986.8 26.5 %collective-permute-start.28 = (f32[3,128,128]{2,0,1:T(4,128)S(1)}, f32[3,128,128]{2,0,1:T(4,128)S(1)}, u32[]{:S(2)}, u32[]{:S(2)}) collective-permute-start(f32[3,128,128]{2,0,1:T(4,128)S(1)} %get-tuple-element.854), channel_id=1, source_target_pairs={{0,1},{2,3},{4,5},{6,7},{8,9},{10,11},{12,13},{14,15},{16,17},{18,... | collective-permute-start | bytes 589832 | tf_op jit(solution)/shard_map/ppermute | solution.py:26
  1031.0 24.2 %collective-permute-start.31 = (f32[3,128,128]{2,0,1:T(4,128)S(1)}, f32[3,128,128]{2,0,1:T(4,128)S(1)}, u32[]{:S(2)}, u32[]{:S(2)}) collective-permute-start(f32[3,128,128]{2,0,1:T(4,128)S(1)} %get-tuple-element.847), channel_id=1, source_target_pairs={{1,0},{3,2},{5,4},{7,6},{9,8},{11,10},{13,12},{15,14},{17,16},{19,... | collective-permute-start | bytes 589832 | tf_op jit(solution)/shard_map/ppermute | solution.py:28
  1032.3 22.9 %collective-permute-start.30 = (f32[3,128,128]{2,0,1:T(4,128)S(1)}, f32[3,128,128]{2,0,1:T(4,128)S(1)}, u32[]{:S(2)}, u32[]{:S(2)}) collective-permute-start(f32[3,128,128]{2,0,1:T(4,128)S(1)} %get-tuple-element.846), channel_id=1, source_target_pairs={{0,1},{2,3},{4,5},{6,7},{8,9},{10,11},{12,13},{14,15},{16,17},{18,... | collective-permute-start | bytes 589832 | tf_op jit(solution)/shard_map/ppermute | solution.py:26
where the time goes:
time: 1110 us; the launch traced here: 1100 us
  blocking collectives  705 us (64%)
  local copies, waits for them, and re-layouts  212 us (19%)
  starting transfers between devices  94.2 us (8%)
  other arithmetic  72.7 us (7%)
  between operations  15.9 us (1%)
    all_gather x16, blocking collectives, partner_traces(): all_traces = lax.all_gather(traces[None], 'patch', axis=0, tiled=True)  310 us
    psum x6, blocking collectives, squares(): return lax.psum(jnp.sum(residual * residual), ('patch', 'sec'))  246 us
    psum x4, blocking collectives, shards(): lax.psum(jnp.sum(direction * image), ('patch', 'sec'))  150 us
    scatter-add x13, local copies, waits for them, and re-layouts, add_penalty(): stiffness = stiffness.at[..., -1, :].add(PENALTY * pieces[1])  119 us
    ppermute x16, starting transfers between devices, padded_2(): lax.ppermute(tail, axis, [(i, (i + 1) % count) for i in range(ends)])  73.5 us
    add x42, other arithmetic, banded_padded(): summed = summed + coefficients[offset] * (lower + upper)  34.7 us
    scatter-add x10, local copies, waits for them, and re-layouts, add_penalty(): stiffness = stiffness.at[..., :, -1].add(PENALTY * pieces[3])  32.8 us
    scatter-add x11, local copies, waits for them, and re-layouts, add_penalty(): stiffness = stiffness.at[..., 0, :].add(PENALTY * pieces[0])  23.7 us
  transfers between devices with their start and end apart: 32, of which 0 were waited for; matrix products, arithmetic and copies ran while one was open for 2% of the time, Pallas kernels for 0%

commit v1 on v0

v1 whole, which is shorter than its diff:
```python
import functools

import jax
import jax.numpy as jnp
import numpy as np
from jax import lax
from jax.experimental import pallas as pl
from jax.experimental.pallas import tpu as pltpu
from jax.sharding import PartitionSpec as P

STEPS = 2
MASS_BAND = (2416.0 / 5040.0, 1191.0 / 5040.0, 120.0 / 5040.0, 1.0 / 5040.0)
STIFF_BAND = (2.0 / 3.0, -0.125, -0.2, -1.0 / 120.0)
SCALE = 5040.0
MASS_HIGH, MASS_LOW = (2416.0, 1192.0, 120.0, 1.0), (0.0, -1.0, 0.0, 0.0)
STIFF_HIGH, STIFF_LOW = (3360.0, -632.0, -1008.0, -42.0), (0.0, 2.0, 0.0, 0.0)
PENALTY = 2.0
TIME_STEP = 1.0
STABILIZER = 2.0
GRADIENT_ENERGY = 0.5
HALF = TIME_STEP * GRADIENT_ENERGY
TWICE = TIME_STEP * STABILIZER
EXACT = lax.Precision.HIGHEST
LANES = 128
PAD = 8
TABLE = 8
SUMS = 32


def band_matrix(band, size):
    out = np.zeros((size, size), np.float32)
    for offset, value in enumerate(band):
        for row in range(size - offset):
            out[row, row + offset] = value
            out[row + offset, row] = value
    return out


def dot(left, right):
    return jnp.dot(left, right, precision=EXACT, preferred_element_type=jnp.float32)


def right_matrix(mass_band, stiff_band):
    mass, stiff = band_matrix(mass_band, LANES), band_matrix(stiff_band, LANES)
    return np.block([[mass, stiff], [np.zeros_like(mass), mass]])


def constants(depth):
    high = right_matrix(MASS_HIGH, STIFF_HIGH).astype(jnp.bfloat16)
    low = right_matrix(MASS_LOW, STIFF_LOW).astype(jnp.bfloat16)
    plain = right_matrix(MASS_BAND, STIFF_BAND)[:LANES]
    reverse = np.ascontiguousarray(np.eye(LANES, dtype=np.float32)[::-1])
    four = np.eye(4, dtype=np.float32)
    third = np.concatenate(
        [
            np.kron(four, band_matrix(MASS_BAND, depth)),
            np.kron(four, band_matrix(STIFF_BAND, depth)),
        ],
        axis=1,
    )
    return high, low, plain, reverse, third


class Body:
    def __init__(self, sizes, refs):
        self.depth, self.patches, self.slabs = sizes
        self.tables, self.consts, self.scratch = refs[:3], refs[3:8], refs[8:]
        self.high, self.low, self.plain, self.reverse, self.third = self.consts
        self.near, self.strip, self.turned, self.stood = self.scratch
        self.me = lax.axis_index("patch")
        self.lane = lax.broadcasted_iota(jnp.int32, (self.depth, LANES), 1)
        self.first, self.last = self.lane == 0, self.lane == LANES - 1
        self.wide = lax.broadcasted_iota(jnp.int32, (LANES, LANES), 1)
        self.edge = (self.wide == 0) | (self.wide == LANES - 1)

    def partner(self, patch, face):
        return self.tables[0][patch, face]

    def face_id(self, patch, face):
        return self.tables[1][patch, face]

    def flip(self, patch, face):
        return self.tables[2][patch, face]

    def split(self, value):
        pieces = []
        for last in (False, False, True):
            piece = value.astype(jnp.bfloat16)
            pieces.append(piece)
            if not last:
                value = value - piece.astype(jnp.float32)
        return pieces

    def stiff0(self, layer, finish):
        depth = self.depth
        zeros = jnp.zeros((PAD, LANES), jnp.float32)
        for i in range(4):
            self.near[i, :PAD] = zeros
            self.near[i, PAD + LANES :] = zeros
        for z in range(depth):
            middle = layer(z)
            massed = (MASS_BAND[0] / SCALE) * middle
            stiffed = (STIFF_BAND[0] / SCALE) * middle
            for offset in (1, 2, 3):
                near = [layer(k) for k in (z - offset, z + offset) if 0 <= k < depth]
                if near:
                    both = near[0] if len(near) == 1 else near[0] + near[1]
                    massed = massed + (MASS_BAND[offset] / SCALE) * both
                    stiffed = stiffed + (STIFF_BAND[offset] / SCALE) * both
            pieces = self.split(jnp.concatenate([massed, stiffed], axis=1))
            mixed = None
            for matrix, parts in ((self.high, pieces), (self.low, pieces[:2])):
                for piece in parts:
                    term = jnp.dot(piece, matrix[...], preferred_element_type=jnp.float32)
                    mixed = term if mixed is None else mixed + term
            a, b = 2 * (z % 2), 2 * (z % 2) + 1
            self.near[a, PAD : PAD + LANES] = mixed[:, :LANES]
            self.near[b, PAD : PAD + LANES] = mixed[:, LANES:]
            stiff = STIFF_BAND[0] * mixed[:, :LANES] + MASS_BAND[0] * mixed[:, LANES:]
            mass = MASS_BAND[0] * mixed[:, :LANES]
            for o in (1, 2, 3):
                low, high = slice(PAD - o, PAD - o + LANES), slice(PAD + o, PAD + o + LANES)
                both = self.near[a, low] + self.near[a, high]
                stiff = stiff + STIFF_BAND[o] * both
                stiff = stiff + MASS_BAND[o] * (self.near[b, low] + self.near[b, high])
                mass = mass + MASS_BAND[o] * both
            finish(z, stiff, mass)

    def strips(self, field, count=4):
        depth = field.shape[0]
        group = min(depth, 8)
        rows0 = [field[:, d, :] for d in range(count)]
        rows1 = [field[:, LANES - 1 - d, :] for d in range(count)]
        wanted = list(range(4 - count, 4 + count))
        pieces = {i: [] for i in wanted}
        for start in range(0, depth, group):
            stacked = jnp.zeros((LANES, LANES), jnp.float32)
            for j in range(group):
                rolled = pltpu.roll(field[start + j], (8 * j + 4) % LANES, 1)
                stacked = jnp.where((self.wide >> 3) == j, rolled, stacked)
            self.strip[...] = jnp.transpose(stacked)
            for i in wanted:
                pieces[i].append(self.strip[pl.ds(i, group, stride=8), :])
        columns = {i: jnp.concatenate(p, axis=0) if len(p) > 1 else p[0] for i, p in pieces.items()}
        return [
            rows0,
            rows1,
            [columns[4 + d] for d in range(count)],
            [columns[3 - d] for d in range(count)],
        ]

    def traces(self, field):
        return [strip[0] for strip in self.strips(field, 1)]

    def jumps(self, mine, other):
        return [PENALTY * (a - b) for a, b in zip(mine, other)]

    def stand(self, jump):
        for start in range(0, self.depth, 8):
            self.turned[pl.ds(0, 8, stride=2), :] = jump[3][start : start + 8]
            self.turned[pl.ds(1, 8, stride=2), :] = jump[2][start : start + 8]
            self.stood[start // 8] = jnp.transpose(self.turned[...])

    def column(self, z):
        rolled = pltpu.roll(self.stood[z // 8], (LANES - 2 * (z % 8) - 1) % LANES, 1)
        return jnp.where(self.edge, rolled, 0.0)

    def add_rows(self, field, jump, factor):
        field[:, 0, :] = field[:, 0, :] + factor * jump[0]
        field[:, LANES - 1, :] = field[:, LANES - 1, :] + factor * jump[1]

    def stiff_trace(self, inner, jump):
        out = []
        for f in range(4):
            side = f & 1
            low, high = (2, 3) if f < 2 else (0, 1)
            at = side * (LANES - 1)
            ends = []
            for face, end in ((low, 0), (high, LANES - 1)):
                shift = (end - at) % LANES
                ends.append(pltpu.roll(jump[face], shift, 1) if shift else jump[face])
            out.append(inner[f] + jump[f] + self.ends(*ends))
        return out

    def slab(self, stiffs, masses, plain=None):
        n = 4 * self.depth
        rows = [stack(masses), stack(stiffs)] + ([] if plain is None else [stack(plain)])
        both = dot(stack(rows), self.plain[...])
        lower = both[n : 2 * n, :LANES] + both[:n, LANES:]
        if plain is not None:
            lower = lower + both[2 * n :, :LANES]
        out = dot(self.third[...], stack([lower, both[:n, :LANES]]))
        return unstack(out, self.depth)

    def depth_sum(self, strip, band):
        out = band[0] * strip[0]
        for d in (1, 2, 3):
            out = out + band[d] * strip[d]
        return out

    def corner_table(self, trace, inner=None):
        table = jnp.zeros((self.depth, LANES), jnp.float32)
        ends = (0, LANES - 1)
        if inner is not None:
            arms = dot(stack(trace), self.plain[...])
        for rs in range(2):
            for cs in range(2):
                slot = TABLE * (2 * rs + cs)
                values = [(trace[rs], ends[cs])]
                if inner is not None:
                    values.append((inner[rs], ends[cs]))
                    for face, end in ((rs, ends[cs]), (2 + cs, ends[rs])):
                        part = arms[face * self.depth : (face + 1) * self.depth]
                        values.append((part[:, :LANES], end))
                        values.append((part[:, LANES:], end))
                for kind, (value, end) in enumerate(values):
                    shift = (slot + kind - end) % LANES
                    rolled = pltpu.roll(value, shift, 1) if shift else value
                    table = jnp.where(self.lane == slot + kind, rolled, table)
        return table

    def send(self, payload, groups, table, copies=1):
        depth = self.depth
        at = len(groups) * depth
        for f in range(4):
            to = self.partner(self.me, f) * copies
            for i, group in enumerate(groups):
                for s in range(copies):
                    payload[to + s, i * depth : (i + 1) * depth, :] = group[f]
        for to in range(self.patches * copies):
            payload[to, at : at + depth, :] = table

    def take(self, recv, patch, lo, hi):
        copies = recv.shape[0] // self.patches
        out = recv[patch * copies, lo:hi, :]
        for s in range(1, copies):
            out = out + recv[patch * copies + s, lo:hi, :]
        return out

    def received(self, recv, count, at=0):
        depth = self.depth
        rows = count * depth
        raw = [self.take(recv, self.partner(self.me, f), at, at + rows) for f in range(4)]
        turned = dot(stack(raw), self.reverse[...])
        out = []
        for f in range(4):
            flipped = self.flip(self.me, f) == 1
            out.append(jnp.where(flipped, turned[f * rows : (f + 1) * rows], raw[f]))
        return [[out[f][i * depth : (i + 1) * depth] for f in range(4)] for i in range(count)]

    def corner(self, face, side):
        q, f1 = self.partner(self.me, face), self.face_id(self.me, face)
        eq = side ^ self.flip(self.me, face)
        s1 = f1 & 1
        upright = f1 < 2
        f2 = jnp.where(upright, 2 + eq, eq)
        kq = jnp.where(upright, 2 * s1 + eq, 2 * eq + s1)
        tq = jnp.where(upright, 4, 2)
        r, g = self.partner(q, f2), self.face_id(q, f2)
        s2 = s1 ^ self.flip(q, f2)
        flat = g < 2
        k = jnp.where(flat, 2 * (g & 1) + s2, 2 * s2 + (g & 1))
        t = jnp.where(flat, 2, 4)
        g2 = jnp.where(flat, 2 + s2, s2)
        r2, h = self.partner(r, g2), self.face_id(r, g2)
        s4 = (g & 1) ^ self.flip(r, g2)
        k2 = jnp.where(h < 2, 2 * (h & 1) + s4, 2 * s4 + (h & 1))
        return (q, kq, tq), (r, k, t), (r2, k2)

    def corners(self):
        return [[self.corner(f, s) for s in range(2)] for f in range(4)]

    def look(self, recv, at, patch, lane, side):
        shift = (side * (LANES - 1) + LANES - lane) & (LANES - 1)
        return pltpu.roll(self.take(recv, patch, at, at + self.depth), shift, 1)

    def ends(self, low, high):
        return jnp.where(self.first, low, jnp.where(self.last, high, 0.0))

    def other_stiff(self, recv, at, mine, theirs, inner, corners):
        out = []
        edge = self.first | self.last
        for f in range(4):
            across = []
            for s in range(2):
                r, k, t = corners[f][s][1]
                across.append(self.look(recv, at, r, TABLE * k, s))
            value = inner[f] + PENALTY * (theirs[f] - mine[f])
            far = PENALTY * (theirs[f] - self.ends(*across))
            out.append(value + jnp.where(edge, far, 0.0))
        return out


def stack(values):
    return jnp.concatenate(values, 0)


def unstack(value, depth):
    return [value[f * depth : (f + 1) * depth] for f in range(4)]


def cubic(x, s):
    return x * x * x - x + GRADIENT_ENERGY * s


def start_kernel(sizes, own, payload, *refs):
    body = Body(sizes, refs)
    rows = own.shape[0]
    layer = lax.broadcasted_iota(jnp.int32, (body.depth, LANES), 0)
    low = lax.axis_index("sec") * rows
    here = (layer >= low) & (layer < low + rows)

    def place(value):
        return jnp.where(here, stack([value] * body.slabs), 0.0)

    strips = body.strips(own)
    trace = [place(s[0]) for s in strips]
    inner = body.slab(
        [place(body.depth_sum(s, STIFF_BAND)) for s in strips],
        [place(body.depth_sum(s, MASS_BAND)) for s in strips],
    )
    body.send(payload, [trace, inner], body.corner_table(trace), body.slabs)


def flux_tail(body, current, mine, other, r0, v1, m1, tr, tv, payload, potential):
    jump = body.jumps(mine, other)
    body.stand(jump)

    def residual(z, stiff, mass):
        r0[z] = -TIME_STEP * (stiff + body.column(z))

    body.stiff0(lambda z: potential[z], residual)
    body.add_rows(r0, jump, -TIME_STEP)

    def image(z, stiff, mass):
        v1[z] = stiff
        m1[z] = mass

    body.stiff0(lambda z: r0[z], image)
    trace, inner = body.traces(r0), body.traces(v1)
    tr[...], tv[...] = stack(trace), stack(inner)
    body.send(payload, [trace, inner], body.corner_table(trace))


def first_kernel(sizes, recv, *refs):
    slabs, refs = refs[: sizes[2]], refs[sizes[2] :]
    c, sc, r0, v1, m1, tc, tr, tv, sides, payload, potential = refs[:11]
    body = Body(sizes, refs[11:])
    depth, count = body.depth, body.slabs
    rows = depth // count
    sec = lax.axis_index("sec")
    for k, slab in enumerate(slabs):
        c[pl.ds(lax.rem(sec + k, count) * rows, rows)] = slab[...]
    other, inner = body.received(recv, 2)
    mine = body.traces(c)
    jump = body.jumps(mine, other)
    body.stand(jump)

    def curve(z, stiff, mass):
        sc[z] = stiff + body.column(z)

    body.stiff0(lambda z: c[z], curve)
    body.add_rows(sc, jump, 1.0)
    for z in range(depth):
        potential[z] = cubic(c[z], sc[z])
    mine_s = body.traces(sc)
    other_s = body.other_stiff(recv, 2 * depth, mine, other, inner, body.corners())
    tc[0], tc[1] = stack(mine), stack(mine_s)
    sides[0], sides[1] = stack(other), stack(other_s)
    mine_p = [cubic(x, s) for x, s in zip(mine, mine_s)]
    other_p = [cubic(x, s) for x, s in zip(other, other_s)]
    flux_tail(body, c, mine_p, other_p, r0, v1, m1, tr, tv, payload, potential)


def second_kernel(sizes, r0, v1, m1, tr, tv, recv, u1, y, v2, m2, ty, tv2, tu, sides, payload,
                  *refs):
    body = Body(sizes, refs)
    depth = body.depth
    other, inner = body.received(recv, 2)
    mine = unstack(tr, depth)
    jump = body.jumps(mine, other)
    body.stand(jump)
    for z in range(depth):
        u1[z] = v1[z] + body.column(z)
    body.add_rows(u1, jump, 1.0)
    mine_s = body.stiff_trace(unstack(tv, depth), jump)
    other_s = body.other_stiff(recv, 2 * depth, mine, other, inner, body.corners())
    tu[...] = stack(mine_s)
    sides[0], sides[1] = stack(other), stack(other_s)
    jump = body.jumps(mine_s, other_s)
    body.stand(jump)

    def image(z, stiff, mass):
        y[z] = m1[z] + TWICE * u1[z] + HALF * (stiff + body.column(z))

    body.stiff0(lambda z: u1[z], image)
    body.add_rows(y, jump, HALF)
    sums = [[], [], []]

    def again(z, stiff, mass):
        v2[z] = stiff
        m2[z] = mass
        a, b = r0[z], y[z]
        for i, product in enumerate((a * a, a * b, b * b)):
            sums[i].append(jnp.sum(product, axis=0, keepdims=True))

    body.stiff0(lambda z: y[z], again)
    strips_y, strips = body.strips(y), body.strips(v2)
    trace, inner = [s[0] for s in strips_y], [s[0] for s in strips]
    ty[...], tv2[...] = stack(trace), stack(inner)
    mixed = body.slab(
        [HALF * body.depth_sum(s, STIFF_BAND) for s in strips],
        [HALF * body.depth_sum(s, MASS_BAND) for s in strips],
        [body.depth_sum(s, MASS_BAND) for s in strips_y],
    )
    outer = [TWICE * a + b for a, b in zip(inner, mixed)]
    table = body.corner_table(trace, inner)
    for i in range(3):
        total = jnp.sum(stack(sums[i]), axis=1, keepdims=True)
        table = jnp.where(body.lane == SUMS + i, total, table)
    body.send(payload, [trace, inner, outer], table)


def third_kernel(sizes, last, r0, y, v2, m2, ty, tv2, recv, *refs):
    if last:
        t, base, payload, u2, zf, mt = refs[:6]
        body = Body(sizes, refs[6:])
    else:
        t, base, u2, zf, tt, tu2, tz, sides, payload, mt = refs[:10]
        body = Body(sizes, refs[10:])
    depth, patches = body.depth, body.patches
    at = 3 * depth
    known = recv[0, at : at + depth, :]
    for p in range(1, patches):
        known = known + recv[p, at : at + depth, :]
    known = jnp.sum(known, axis=0, keepdims=True)
    m0, m1, m2s = [known[:, SUMS + i : SUMS + i + 1] for i in range(3)]
    a0 = m0 / m1
    other, inner, outer = body.received(recv, 3)
    corners = body.corners()
    mine = unstack(ty, depth)
    jump = body.jumps(mine, other)
    body.stand(jump)
    for z in range(depth):
        u2[z] = v2[z] + body.column(z)
    body.add_rows(u2, jump, 1.0)
    mine_s = body.stiff_trace(unstack(tv2, depth), jump)
    other_s = body.other_stiff(recv, at, mine, other, inner, corners)
    masses, stiffs, far = [], [], []
    for f in range(4):
        arm_m, arm_k, across = [], [], []
        for s in range(2):
            (q, kq, tq), (r, k, kind), (r2, k2) = corners[f][s]
            look = functools.partial(body.look, recv, at, side=s)
            arm_m.append(look(q, TABLE * kq + tq) - look(r, TABLE * k + kind))
            arm_k.append(look(q, TABLE * kq + tq + 1) - look(r, TABLE * k + kind + 1))
            value = look(r, TABLE * k)
            across.append(
                look(r, TABLE * k + 1)
                + PENALTY * (value - other[f])
                + PENALTY * (value - look(r2, TABLE * k2))
            )
        theirs = PENALTY * (other[f] - mine[f])
        masses.append(MASS_BAND[0] * theirs + PENALTY * body.ends(*arm_m))
        stiffs.append(STIFF_BAND[0] * theirs + PENALTY * body.ends(*arm_k))
        far.append(body.ends(*across))
    pushed = body.slab(stiffs, masses)
    edge = body.first | body.last
    other_t = []
    for f in range(4):
        again = pushed[f] + PENALTY * (other_s[f] - mine_s[f])
        again = again + jnp.where(edge, PENALTY * (other_s[f] - far[f]), 0.0)
        image = outer[f] + TWICE * (other_s[f] - inner[f]) + HALF * again
        other_t.append(other[f] - a0 * image)
    jump = body.jumps(mine_s, other_s)
    body.stand(jump)

    def turn(z, stiff, mass):
        t[z] = y[z] - a0 * (m2[z] + TWICE * u2[z] + HALF * (stiff + body.column(z)))

    body.stiff0(lambda z: u2[z], turn)
    body.add_rows(t, jump, -HALF * a0)
    mine_t = body.traces(t)
    jump = body.jumps(mine_t, other_t)
    body.stand(jump)

    def image(z, stiff, mass):
        zf[z] = stiff + body.column(z)
        mt[z] = mass

    body.stiff0(lambda z: t[z], image)
    body.add_rows(zf, jump, 1.0)
    sums = [jnp.zeros((8, LANES), jnp.float32)] * 6
    for z in range(depth):
        b, x, s = y[z], t[z], zf[z]
        a = r0[z] - a0 * b
        energy = x * (mt[z] + TWICE * s) + HALF * (s * s)
        for i, product in enumerate((a * a, a * x, a * b, x * x, x * b, energy)):
            sums[i] = sums[i] + jnp.sum(product.reshape(LANES // 8, 8, LANES), axis=0)
    moments = jnp.zeros((1, LANES), jnp.float32)
    lane = lax.broadcasted_iota(jnp.int32, (1, LANES), 1)
    for i, value in enumerate(sums):
        value = jnp.sum(jnp.sum(value, axis=0, keepdims=True), axis=1, keepdims=True)
        moments = jnp.where(lane == i, value, moments)
    for i, value in enumerate((a0, m0, m1, m2s)):
        base[i : i + 1, :] = jnp.broadcast_to(value, (1, LANES))
    for to in range(patches):
        payload[to, :1, :] = moments
    if not last:
        trace = body.traces(zf)
        tt[...], tu2[...], tz[...] = stack(mine_t), stack(mine_s), stack(trace)
        sides[0], sides[1], sides[2] = stack(other), stack(other_s), stack(other_t)
        for f in range(4):
            payload[body.partner(body.me, f), 8 : 8 + depth, :] = trace[f]


def weights(patches, base, recv):
    total = recv[0, :1, :]
    for p in range(1, patches):
        total = total + recv[p, :1, :]
    a0, m0, m1, m2 = [base[i : i + 1, :1] for i in range(4)]
    rr1, g1, g2, tt, ty, tat = [total[:, i : i + 1] for i in range(6)]
    b0 = rr1 / m0
    a1 = rr1 / (g1 + 2.0 * b0 * g2 + b0 * b0 * m1)
    rr2 = rr1 - 2.0 * a1 * (g1 + b0 * g2) + a1 * a1 * (tt + 2.0 * b0 * ty + b0 * b0 * m2)
    b1 = rr2 / rr1
    shift = a1 * b0 / a0
    c1, c0, c2 = 1.0 + b1 + shift, b1 * b0 - shift, -a1
    a2 = rr2 / (
        c1 * c1 * g1
        + c0 * c0 * m1
        + c2 * c2 * tat
        + 2.0 * (c1 * c0 * g2 + c1 * c2 * tt + c0 * c2 * ty)
    )
    return a0 + a1 * (1.0 + b0) + a2 * (c1 + c0), -a0 * (a1 + a2 * c1), a2 * c2


def next_kernel(sizes, c, r0, y, t, sc, u1, u2, zf, tc, tr, tu, ty, tu2, tt, tz,
                side_c, side_r, side_y, base, recv,
                cn, rn, v1, m1, trn, tvn, payload, potential, *refs):
    body = Body(sizes, refs)
    depth = body.depth
    x = weights(body.patches, base, recv)

    def mix(*values):
        return values[0] + x[0] * values[1] + x[1] * values[2] + x[2] * values[3]

    for z in range(depth):
        cn[z] = mix(c[z], r0[z], y[z], t[z])
        potential[z] = cubic(cn[z], mix(sc[z], u1[z], u2[z], zf[z]))
    (side_z,) = body.received(recv, 1, 8)
    mine = cubic(
        mix(tc[0], tr[...], ty[...], tt[...]), mix(tc[1], tu[...], tu2[...], tz[...])
    )
    other = cubic(
        mix(side_c[0], side_r[0], side_y[0], side_y[2]),
        mix(side_c[1], side_r[1], side_y[1], stack(side_z)),
    )
    flux_tail(body, cn, unstack(mine, depth), unstack(other, depth),
              rn, v1, m1, trn, tvn, payload, potential)


def last_kernel(patches, c, r0, y, t, base, recv, out):
    x0, x1, x2 = weights(patches, base, recv)
    rows = out.shape[0]
    low = lax.axis_index("sec") * rows
    for z in range(rows):
        k = low + z
        out[z] = c[k] + x0 * r0[k] + x1 * y[k] + x2 * t[k]


def shards(patches, slabs, concentration, partner, face_id, flip):
    own = concentration[0]
    rows = own.shape[0]
    depth = rows * slabs
    halves = [own]
    for k in range(1, slabs):
        halves.append(lax.ppermute(own, "sec", [((i + k) % slabs, i) for i in range(slabs)]))
    consts = [jnp.asarray(x) for x in constants(depth)]
    tables = [partner, face_id, flip]
    vmem, smem = pl.BlockSpec(memory_space=pltpu.VMEM), pl.BlockSpec(memory_space=pltpu.SMEM)
    params = pltpu.CompilerParams(vmem_limit_bytes=48 << 20)

    def shape(*dims):
        return jax.ShapeDtypeStruct(dims, jnp.float32)

    field, trace, base = shape(depth, LANES, LANES), shape(4 * depth, LANES), shape(8, LANES)

    def sides(count):
        return shape(count, 4 * depth, LANES)

    def load(count):
        return shape(patches, count, LANES)

    def call(kernel, outs, *args, fields=0):
        count = len(args)
        inside = [pltpu.VMEM((depth, LANES, LANES), jnp.float32)] * fields
        shared = [
            pltpu.VMEM((4, LANES + 2 * PAD, LANES), jnp.float32),
            pltpu.VMEM((LANES, LANES), jnp.float32),
            pltpu.VMEM((LANES, LANES), jnp.float32),
            pltpu.VMEM((-(-depth // 8), LANES, LANES), jnp.float32),
        ]

        def run(*refs):
            common, rest = refs[:8], refs[8:]
            cut = len(rest) - len(shared)
            kernel((depth, patches, slabs), *rest[:cut], *common, *rest[cut:])

        return pl.pallas_call(
            run,
            out_shape=outs,
            in_specs=[smem] * 3 + [vmem] * (len(consts) + count),
            out_specs=[vmem] * len(outs),
            scratch_shapes=inside + shared,
            compiler_params=params,
            name=kernel.__name__ if hasattr(kernel, "__name__") else "third_kernel",
        )(*tables, *consts, *args)

    def swap(payload, axes="patch"):
        return lax.all_to_all(payload, axes, 0, 0)

    (payload,) = call(start_kernel, [shape(patches * slabs, 3 * depth, LANES)], own)
    c, sc, r0, v1, m1, tc, tr, tv, side_c, payload = call(
        first_kernel,
        [field] * 5 + [sides(2), trace, trace, sides(2), load(3 * depth)],
        swap(payload, ("patch", "sec")), *halves,
        fields=1,
    )
    for step in range(STEPS):
        u1, y, v2, m2, ty, tv2, tu, side_r, payload = call(
            second_kernel,
            [field] * 4 + [trace] * 3 + [sides(2), load(4 * depth)],
            r0, v1, m1, tr, tv, swap(payload),
        )
        last = step + 1 == STEPS
        outs = [field, base]
        if last:
            outs += [load(1)]
        else:
            outs += [field] * 2 + [trace] * 3 + [sides(3), load(8 + depth)]
        t, base_now, *rest = call(
            lambda sizes, *refs, last=last: third_kernel(sizes, last, *refs),
            outs,
            r0, y, v2, m2, ty, tv2, swap(payload),
            fields=3 if last else 1,
        )
        if last:
            (payload,) = rest
            break
        u2, zf, tt, tu2, tz, side_y, payload = rest
        c, r0, v1, m1, tr, tv, payload = call(
            next_kernel,
            [field] * 4 + [trace] * 2 + [load(3 * depth)],
            c, r0, y, t, sc, u1, u2, zf, tc, tr, tu, ty, tu2, tt, tz,
            side_c, side_r, side_y, base_now, swap(payload),
            fields=1,
        )
    out = pl.pallas_call(
        functools.partial(last_kernel, patches),
        out_shape=shape(rows, LANES, LANES),
        in_specs=[vmem] * 6,
        out_specs=vmem,
        compiler_params=params,
    )(c, r0, y, t, base_now, swap(payload))
    return out[None]


def solution(mesh):
    placed = (P("patch", "sec", None, None), P(), P(), P())
    return jax.shard_map(
        functools.partial(shards, mesh.shape["patch"], mesh.shape["sec"]),
        mesh=mesh,
        in_specs=placed,
        out_specs=P("patch", "sec", None, None),
        check_vma=False,
    )
```

time: 1110 us -> 133 us (0.12)
  blocking collectives: 705 us -> 71 us
  local copies, waits for them, and re-layouts: 212 us -> 7.75 us
  starting transfers between devices: 94.2 us -> 9.14 us
  other arithmetic: 72.7 us -> 0 us
  Pallas kernels: 0 us -> 33.2 us
  between operations: 15.9 us -> 0.12 us
    psum x10 -> x0, blocking collectives: 396 us -> none  [the longest x6 246 us: squares(): return lax.psum(jnp.sum(residual * residual), ('patch', 'sec'))]
    all_gather x16 -> x0, blocking collectives: 310 us -> none  [partner_traces(): all_traces = lax.all_gather(traces[None], 'patch', axis=0, tiled=True)]
    scatter-add x38 -> x0, local copies, waits for them, and re-layouts: 181 us -> none  [the longest x13 119 us: add_penalty(): stiffness = stiffness.at[..., -1, :].add(PENALTY * pieces[1])]
    ppermute x32 -> x1, starting transfers between devices: 94.2 us -> 1.83 us  [shards(): lax.ppermute(own, 'sec', [((i + k) % slabs, i) for i in range(slabs)])]
    all_to_all x0 -> x6, blocking collectives: none -> 71 us  [swap(): return lax.all_to_all(payload, axes, 0, 0)]
    add x104 -> x0, other arithmetic: 60.4 us -> none  [the longest x42 34.7 us: banded_padded(): summed = summed + coefficients[offset] * (lower + upper)]
    pallas_call x0 -> x8, Pallas kernels: none -> 33.2 us  [the longest x7 32.2 us: call(): pl.pallas_call(run, out_shape=outs, in_specs=[smem] * 3 + [vmem] * (len(c...]
  transfers between devices with their start and end apart: 32 -> 2, of which waited for: 0 -> 2; matrix products, arithmetic and copies ran while one was open for 2% -> 0% of each run, Pallas kernels for 0% -> 0%
where the time goes in v1:
time: 133 us; the launch traced here: 132 us
  blocking collectives  71 us (53%)
  Pallas kernels  33.2 us (25%)
  waiting for transfers between devices  10.9 us (8%)
  starting transfers between devices  9.14 us (7%)
  local copies, waits for them, and re-layouts  7.75 us (6%)
    all_to_all x6, blocking collectives, swap(): return lax.all_to_all(payload, axes, 0, 0)  71 us
    pallas_call x7, Pallas kernels, call(): pl.pallas_call(run, out_shape=outs, in_specs=[smem] * 3 + [vmem] * (len(c...  32.2 us
    ppermute x1, waiting for transfers between devices, shards(): lax.ppermute(own, 'sec', [((i + k) % slabs, i) for i in range(slabs)])  10.6 us
    unnamed x33, local copies, waits for them, and re-layouts  7.75 us
    all_to_all x1, starting transfers between devices, swap(): return lax.all_to_all(payload, axes, 0, 0)  7.3 us
  transfers between devices with their start and end apart: 2, of which 2 were waited for; matrix products, arithmetic and copies ran while one was open for 0% of the time, Pallas kernels for 0%

profile of v1, /device:TPU:0, one launch (start us, length us, event | category | flops | bytes accessed | tf_op | source)
XLA Modules:
  0.0 132.2 jit_solution(16343405612236419037)
XLA Ops:
  0.0 0.0 copy-start.10
  0.0 0.8 copy.22.refs_0_
  0.8 0.0 copy-start.14
  0.8 0.8 copy.23.refs_1_
  1.5 0.0 copy-done.14
  1.6 0.1 copy.24.refs_2_
  1.6 0.0 copy-done.10
  1.6 0.0 copy-start
  1.6 0.9 copy-done
  2.5 0.0 copy-start.2
  2.5 0.9 copy-done.2
  3.4 0.0 copy-start.4
  3.4 0.9 copy-done.4
  4.4 0.0 copy-start.6
  4.4 0.8 copy-done.6
  5.2 0.0 copy-start.8
  5.2 0.9 copy-done.8
  6.1 2.2 %start_kernel.1 = f32[32,24,128]{2,1,0:T(8,128)} custom-call(s32[16,4]{1,0:T(8,128)S(1)} %copy.22.refs_0_, s32[16,4]{1,0:T(8,128)S(1)} %copy.23.refs_1_, s32[16,4]{1,0:T(8,128)S(1)} %copy.24.refs_2_, bf16[256,256]{1,0:T(8,128)(2,1)S(1)} %copy-done.4, bf16[256,256]{1,0:T(8,128)(2,1)S(1)} %copy-done.2, f32[128,256]{1,0:T(8,128)S(1)} %copy-done, ...), custom_call_target="tpu_custom_call" | custom-call | tf_op jit(solution)/shard_map/start_kernel/pallas_call | solution.py:610
  8.4 0.0 copy-start.9
  8.4 0.0 copy-start.1
  8.4 0.0 copy-start.7
  8.4 7.3 %all-to-all-start = ((f32[32,24,128]{2,1,0:T(8,128)}), f32[32,24,128]{2,1,0:T(8,128)S(1)}, u32[]{:S(2)}, u32[]{:S(2)}) async-start(f32[32,24,128]{2,1,0:T(8,128)} %start_kernel.1), calls=%async_computation | async-start | bytes 786432 | tf_op jit(solution)/shard_map/all_to_all | solution.py:621
  15.7 0.0 copy-done.9
  15.7 1.8 %collective-permute-start = (f32[4,128,128]{2,1,0:T(8,128)S(1)}, f32[4,128,128]{2,1,0:T(8,128)S(1)}, u32[]{:S(2)}, u32[]{:S(2)}) collective-permute-start(f32[4,128,128]{2,1,0:T(8,128)S(1)} %bitcast.3), channel_id=1, source_target_pairs={{1,0},{0,1},{3,2},{2,3},{5,4},{4,5},{7,6},{6,7},{9,8},{8,9},{11,10... | collective-permute-start | bytes 786440 | tf_op jit(solution)/shard_map/ppermute | solution.py:578
  17.6 10.6 %collective-permute-done.refs_10_ = f32[4,128,128]{2,1,0:T(8,128)S(1)} collective-permute-done((f32[4,128,128]{2,1,0:T(8,128)S(1)}, f32[4,128,128]{2,1,0:T(8,128)S(1)}, u32[]{:S(2)}, u32[]{:S(2)}) %collective-permute-start) | collective-permute-done | bytes 262176 | tf_op jit(solution)/shard_map/ppermute | solution.py:578
  28.1 0.3 all-to-all-done.refs_8_
  28.5 0.0 copy-done.1
  28.5 0.0 copy-done.3
  28.5 0.0 copy-done.5
  28.5 0.0 copy-done.7
  28.5 5.1 %first_kernel.1 = (f32[8,128,128]{2,1,0:T(8,128)S(1)}, f32[8,128,128]{2,1,0:T(8,128)S(1)}, f32[8,128,128]{2,1,0:T(8,128)S(1)}, f32[8,128,128]{2,1,0:T(8,128)S(1)...) custom-call(s32[16,4]{1,0:T(8,128)S(1)} %copy.22.refs_0_, ...), custom_call_target="tpu_custom_call" | custom-call | tf_op jit(solution)/shard_map/first_kernel/pallas_call | solution.py:610
  33.6 14.3 %all_to_all.35.refs_13_ = f32[16,24,128]{2,1,0:T(8,128)S(1)} all-to-all(f32[16,24,128]{2,1,0:T(8,128)S(1)} %get-tuple-element.55), channel_id=1, replica_groups=mesh['patch'=16,'sec'=2] {'patch'}, dimensions={0} | all-to-all | bytes 393216 | tf_op jit(solution)/shard_map/all_to_all | solution.py:621
  47.9 4.9 %second_kernel.2 = (f32[8,128,128]{2,1,0:T(8,128)S(1)}, f32[8,128,128]{2,1,0:T(8,128)S(1)}, f32[8,128,128]{2,1,0:T(8,128)S(1)}, f32[8,128,128]{2,1,0:T(8,128)S(1...) custom-call(s32[16,4]{1,0:T(8,128)S(1)} %copy.22.refs_0_, ...), custom_call_target="tpu_custom_call" | custom-call | tf_op jit(solution)/shard_map/second_kernel/pallas_call | solution.py:610
  52.8 0.0 copy-start.11
  52.8 12.6 %all_to_all.36.refs_14_ = f32[16,32,128]{2,1,0:T(8,128)S(1)} all-to-all(f32[16,32,128]{2,1,0:T(8,128)S(1)} %get-tuple-element.61), channel_id=1, replica_groups=mesh['patch'=16,'sec'=2] {'patch'}, dimensions={0} | all-to-all | bytes 524288 | tf_op jit(solution)/shard_map/all_to_all | solution.py:621
  65.5 4.9 %_lambda_.2 = (f32[8,128,128]{2,1,0:T(8,128)S(1)}, f32[8,128]{1,0:T(8,128)S(1)}, f32[8,128,128]{2,1,0:T(8,128)S(1)}, f32[8,128,128]{2,1,0:T(8,128)S(1)}, f32[32,...) custom-call(s32[16,4]{1,0:T(8,128)S(1)} %copy.22.refs_0_, ...), custom_call_target="tpu_custom_call" | custom-call | tf_op jit(solution)/shard_map/<lambda>/pallas_call | solution.py:610
  70.3 0.0 copy-done.11
  70.4 0.0 copy-start.12
  70.4 0.8 copy-done.12
  71.2 0.8 copy-done.13
  72.0 10.7 %all_to_all.37.refs_27_ = f32[16,16,128]{2,1,0:T(8,128)S(1)} all-to-all(f32[16,16,128]{2,1,0:T(8,128)S(1)} %get-tuple-element.76), channel_id=1, replica_groups=mesh['patch'=16,'sec'=2] {'patch'}, dimensions={0} | all-to-all | bytes 262144 | tf_op jit(solution)/shard_map/all_to_all | solution.py:621
  82.6 4.7 %next_kernel.1 = (f32[8,128,128]{2,1,0:T(8,128)S(1)}, f32[8,128,128]{2,1,0:T(8,128)S(1)}, f32[8,128,128]{2,1,0:T(8,128)S(1)}, f32[8,128,128]{2,1,0:T(8,128)S(1)}...) custom-call(s32[16,4]{1,0:T(8,128)S(1)} %copy.22.refs_0_, s32[16,4]{1,0:T(8,128)S(1)} %copy.23.refs_1_, ...), custom_call_target="tpu_custom_call" | custom-call | tf_op jit(solution)/shard_map/next_kernel/pallas_call | solution.py:610
  87.3 11.6 %all_to_all.38.refs_13_ = f32[16,24,128]{2,1,0:T(8,128)S(1)} all-to-all(f32[16,24,128]{2,1,0:T(8,128)S(1)} %get-tuple-element.83), channel_id=1, replica_groups=mesh['patch'=16,'sec'=2] {'patch'}, dimensions={0} | all-to-all | bytes 393216 | tf_op jit(solution)/shard_map/all_to_all | solution.py:621
  98.9 5.4 %second_kernel.3 = (f32[8,128,128]{2,1,0:T(8,128)}, f32[8,128,128]{2,1,0:T(8,128)S(1)}, f32[8,128,128]{2,1,0:T(8,128)S(1)}, f32[8,128,128]{2,1,0:T(8,128)S(1)}, ...) custom-call(s32[16,4]{1,0:T(8,128)S(1)} %copy.22.refs_0_, ...), custom_call_target="tpu_custom_call" | custom-call | tf_op jit(solution)/shard_map/second_kernel/pallas_call | solution.py:610
  104.3 12.6 %all_to_all.39.refs_14_ = f32[16,32,128]{2,1,0:T(8,128)S(1)} all-to-all(f32[16,32,128]{2,1,0:T(8,128)S(1)} %get-tuple-element.89), channel_id=1, replica_groups=mesh['patch'=16,'sec'=2] {'patch'}, dimensions={0} | all-to-all | bytes 524288 | tf_op jit(solution)/shard_map/all_to_all | solution.py:621
  117.0 5.0 %_lambda_.3 = (f32[8,128,128]{2,1,0:T(8,128)S(1)}, f32[8,128]{1,0:T(8,128)S(1)}, f32[16,1,128]{2,1,0:T(1,128)S(1)}) custom-call(s32[16,4]{1,0:T(8,128)S(1)} %copy.22.refs_0_, s32[16,4]{1,0:T(8,128)S(1)} %copy.23.refs_1_, s32[16,4]{1,0:T(8,128)S(1)} %copy.24.refs_2_, bf16[256,256]{1,0:T(8,128)(2,1)S(1)} %copy-done.5, bf16[256,256]{1,0:T(8,128)(2,1)S(1)} %copy-done.3, ...), custom_call_target="tpu_custom_call" | custom-call | tf_op jit(solution)/shard_map/<lambda>/pallas_call | solution.py:610
  121.9 9.2 %all_to_all.40.recv = f32[16,1,128]{2,1,0:T(1,128)S(1)} all-to-all(f32[16,1,128]{2,1,0:T(1,128)S(1)} %get-tuple-element.92), channel_id=1, replica_groups=mesh['patch'=16,'sec'=2] {'patch'}, dimensions={0} | all-to-all | bytes 16384 | tf_op jit(solution)/shard_map/all_to_all | solution.py:621
  131.1 1.1 shard_map.91
  (3 shorter events, 0.0 us)
Async XLA Ops:
  0.0 1.6 %copy-start.10 = (f32[32,64]{1,0:T(8,128)S(1)}, f32[32,64]{1,0:T(8,128)}, u32[]{:S(2)}) copy-start(f32[32,64]{1,0:T(8,128)} %constant.14.clone.refs_7_) | copy-start | bytes 24580
  0.8 0.8 copy-start.14
  1.6 0.9 copy-start
  2.5 0.9 copy-start.2
  3.4 0.9 copy-start.4
  4.4 0.8 copy-start.6
  5.2 0.9 copy-start.8
  8.4 7.3 %copy-start.9 = (f32[1,4,128,128]{3,2,1,0:T(8,128)S(1)}, f32[1,4,128,128]{3,2,1,0:T(8,128)}, u32[]{:S(2)}) copy-start(f32[1,4,128,128]{3,2,1,0:T(8,128)} %param.9) | copy-start | bytes 786436
  8.4 20.1 %copy-start.1 = (f32[128,256]{1,0:T(8,128)S(1)}, f32[128,256]{1,0:T(8,128)}, u32[]{:S(2)}) copy-start(f32[128,256]{1,0:T(8,128)} %constant.12.clone.refs_5_) | copy-start | bytes 393220
  8.4 20.1 %copy-start.3 = (bf16[256,256]{1,0:T(8,128)(2,1)S(1)}, bf16[256,256]{1,0:T(8,128)(2,1)}, u32[]{:S(2)}) copy-start(bf16[256,256]{1,0:T(8,128)(2,1)} %constant.11.clone.refs_4_) | copy-start | bytes 393220
  8.4 20.1 %copy-start.5 = (bf16[256,256]{1,0:T(8,128)(2,1)S(1)}, bf16[256,256]{1,0:T(8,128)(2,1)}, u32[]{:S(2)}) copy-start(bf16[256,256]{1,0:T(8,128)(2,1)} %constant.10.clone.refs_3_) | copy-start | bytes 393220
  8.4 20.1 %copy-start.7 = (f32[128,128]{1,0:T(8,128)S(1)}, f32[128,128]{1,0:T(8,128)}, u32[]{:S(2)}) copy-start(f32[128,128]{1,0:T(8,128)} %constant.13.clone.refs_6_) | copy-start | bytes 196612
  8.4 20.1 %all-to-all-start = ((f32[32,24,128]{2,1,0:T(8,128)}), f32[32,24,128]{2,1,0:T(8,128)S(1)}, u32[]{:S(2)}, u32[]{:S(2)}) async-start(f32[32,24,128]{2,1,0:T(8,128)} %start_kernel.1), calls=%async_computation | async-start | bytes 786432 | tf_op jit(solution)/shard_map/all_to_all | solution.py:621
  15.7 12.4 %collective-permute-start = (f32[4,128,128]{2,1,0:T(8,128)S(1)}, f32[4,128,128]{2,1,0:T(8,128)S(1)}, u32[]{:S(2)}, u32[]{:S(2)}) collective-permute-start(f32[4,128,128]{2,1,0:T(8,128)S(1)} %bitcast.3), channel_id=1, source_target_pairs={{1,0},{0,1},{3,2},{2,3},{5,4},{4,5},{7,6},{6,7},{9,8},{8,9},{11,10... | collective-permute-start | bytes 786440 | tf_op jit(solution)/shard_map/ppermute | solution.py:578
  52.8 17.5 %copy-start.11 = (f32[8,128,128]{2,1,0:T(8,128)}, f32[8,128,128]{2,1,0:T(8,128)S(1)}, u32[]{:S(2)}) copy-start(f32[8,128,128]{2,1,0:T(8,128)S(1)} %get-tuple-element.64.refs_13_) | copy-start | bytes 1572868
  70.4 0.8 copy-start.12
  71.2 0.8 copy-start.13

commit v2 on v1

--- a/solution.py
+++ b/solution.py
@@ -23,8 +23,10 @@
 EXACT = lax.Precision.HIGHEST
 LANES = 128
 PAD = 8
-TABLE = 8
-SUMS = 32
+KINDS = 6
+SUMS = 4 * KINDS
+NARROW, BROAD = 16, 32
+COST = 1 << 34
 
 
 def band_matrix(band, size):
@@ -45,42 +47,61 @@
     return np.block([[mass, stiff], [np.zeros_like(mass), mass]])
 
 
-def constants(depth):
+def constants():
     high = right_matrix(MASS_HIGH, STIFF_HIGH).astype(jnp.bfloat16)
     low = right_matrix(MASS_LOW, STIFF_LOW).astype(jnp.bfloat16)
-    plain = right_matrix(MASS_BAND, STIFF_BAND)[:LANES]
-    reverse = np.ascontiguousarray(np.eye(LANES, dtype=np.float32)[::-1])
-    four = np.eye(4, dtype=np.float32)
-    third = np.concatenate(
-        [
-            np.kron(four, band_matrix(MASS_BAND, depth)),
-            np.kron(four, band_matrix(STIFF_BAND, depth)),
-        ],
-        axis=1,
-    )
-    return high, low, plain, reverse, third
+    return high, low
+
+
+def banded(distance, band, inside=None):
+    out = jnp.zeros(distance.shape, jnp.float32)
+    for offset, value in enumerate(band):
+        hit = distance == offset
+        out = jnp.where(hit if inside is None else hit & inside, value, out)
+    return out
 
 
 class Body:
-    def __init__(self, sizes, refs):
+    def __init__(self, sizes, refs, copies=1):
         self.depth, self.patches, self.slabs = sizes
-        self.tables, self.consts, self.scratch = refs[:3], refs[3:8], refs[8:]
-        self.high, self.low, self.plain, self.reverse, self.third = self.consts
-        self.near, self.strip, self.turned, self.stood = self.scratch
+        self.copies = copies
+        self.tables, refs = refs[:3], refs[3:]
+        self.near, self.strip, self.turned, self.stood = refs[-4:]
+        if len(refs) > 4:
+            self.high, self.low = refs[:2]
         self.me = lax.axis_index("patch")
         self.lane = lax.broadcasted_iota(jnp.int32, (self.depth, LANES), 1)
         self.first, self.last = self.lane == 0, self.lane == LANES - 1
         self.wide = lax.broadcasted_iota(jnp.int32, (LANES, LANES), 1)
         self.edge = (self.wide == 0) | (self.wide == LANES - 1)
+        row = lax.broadcasted_iota(jnp.int32, (LANES, LANES), 0)
+        self.reverse = jnp.where(row + self.wide == LANES - 1, 1.0, 0.0)
+        distance = jnp.abs(row - self.wide)
+        self.plain = jnp.concatenate(
+            [banded(distance, MASS_BAND), banded(distance, STIFF_BAND)], axis=1
+        )
+        n = 4 * self.depth
+        row = lax.broadcasted_iota(jnp.int32, (n, 2 * n), 0)
+        column = lax.broadcasted_iota(jnp.int32, (n, 2 * n), 1)
+        left = column < n
+        column = jnp.where(left, column, column - n)
+        inside = row < 0
+        for low in range(0, n, self.depth):
+            top = low + self.depth
+            inside = inside | ((row >= low) & (row < top) & (column >= low) & (column < top))
+        distance = jnp.abs(row - column)
+        self.third = banded(distance, MASS_BAND, inside & left) + banded(
+            distance, STIFF_BAND, inside & ~left
+        )
 
     def partner(self, patch, face):
-        return self.tables[0][patch, face]
+        return self.tables[0][face, patch]
 
     def face_id(self, patch, face):
-        return self.tables[1][patch, face]
+        return self.tables[1][face, patch]
 
     def flip(self, patch, face):
-        return self.tables[2][patch, face]
+        return self.tables[2][face, patch]
 
     def split(self, value):
         pieces = []
@@ -185,11 +206,11 @@
     def slab(self, stiffs, masses, plain=None):
         n = 4 * self.depth
         rows = [stack(masses), stack(stiffs)] + ([] if plain is None else [stack(plain)])
-        both = dot(stack(rows), self.plain[...])
+        both = dot(stack(rows), self.plain)
         lower = both[n : 2 * n, :LANES] + both[:n, LANES:]
         if plain is not None:
             lower = lower + both[2 * n :, :LANES]
-        out = dot(self.third[...], stack([lower, both[:n, :LANES]]))
+        out = dot(self.third, stack([lower, both[:n, :LANES]]))
         return unstack(out, self.depth)
 
     def depth_sum(self, strip, band):
@@ -201,11 +222,12 @@
     def corner_table(self, trace, inner=None):
         table = jnp.zeros((self.depth, LANES), jnp.float32)
         ends = (0, LANES - 1)
+        kinds = 1 if inner is None else KINDS
         if inner is not None:
-            arms = dot(stack(trace), self.plain[...])
+            arms = dot(stack(trace), self.plain)
         for rs in range(2):
             for cs in range(2):
-                slot = TABLE * (2 * rs + cs)
+                slot = kinds * (2 * rs + cs)
                 values = [(trace[rs], ends[cs])]
                 if inner is not None:
                     values.append((inner[rs], ends[cs]))
@@ -219,29 +241,44 @@
                     table = jnp.where(self.lane == slot + kind, rolled, table)
         return table
 
-    def send(self, payload, groups, table, copies=1):
-        depth = self.depth
+    def pack(self, table, width):
+        count = width // NARROW
+        rows = []
+        for start in range(0, self.depth, 8):
+            for low in range(count):
+                total = None
+                for i in range(low, 8, count):
+                    layer = table[start + i : start + i + 1]
+                    part = pltpu.roll(layer, LANES - NARROW * i, 1) if i else layer
+                    total = part if total is None else total + part
+                rows.append(total)
+        return stack(rows) if len(rows) > 1 else rows[0]
+
+    def send(self, payload, groups, packed):
+        depth, copies = self.depth, self.copies
+        rows = payload.shape[0] // (self.patches * copies)
         at = len(groups) * depth
         for f in range(4):
             to = self.partner(self.me, f) * copies
             for i, group in enumerate(groups):
                 for s in range(copies):
-                    payload[to + s, i * depth : (i + 1) * depth, :] = group[f]
+                    payload[pl.ds((to + s) * rows + i * depth, depth), :] = group[f]
         for to in range(self.patches * copies):
-            payload[to, at : at + depth, :] = table
-
-    def take(self, recv, patch, lo, hi):
-        copies = recv.shape[0] // self.patches
-        out = recv[patch * copies, lo:hi, :]
-        for s in range(1, copies):
-            out = out + recv[patch * copies + s, lo:hi, :]
+            payload[to * rows + at : (to + 1) * rows, :] = packed
+
+    def take(self, recv, patch, lo, count):
+        rows = recv.shape[0] // (self.patches * self.copies)
+        out = None
+        for s in range(self.copies):
+            part = recv[pl.ds((patch * self.copies + s) * rows + lo, count), :]
+            out = part if out is None else out + part
         return out
 
     def received(self, recv, count, at=0):
         depth = self.depth
         rows = count * depth
-        raw = [self.take(recv, self.partner(self.me, f), at, at + rows) for f in range(4)]
-        turned = dot(stack(raw), self.reverse[...])
+        raw = [self.take(recv, self.partner(self.me, f), at, rows) for f in range(4)]
+        turned = dot(stack(raw), self.reverse)
         out = []
         for f in range(4):
             flipped = self.flip(self.me, f) == 1
@@ -270,21 +307,30 @@
     def corners(self):
         return [[self.corner(f, s) for s in range(2)] for f in range(4)]
 
-    def look(self, recv, at, patch, lane, side):
+    def look(self, recv, at, patch, lane, side, width):
+        count = width // NARROW
         shift = (side * (LANES - 1) + LANES - lane) & (LANES - 1)
-        return pltpu.roll(self.take(recv, patch, at, at + self.depth), shift, 1)
+        packed = self.take(recv, patch, at, self.depth // 8 * count)
+        odd = (lax.broadcasted_iota(jnp.int32, (8, LANES), 0) & 1) == 1
+        out = []
+        for k in range(0, self.depth // 8 * count, count):
+            spread = jnp.broadcast_to(packed[k : k + 1], (8, LANES))
+            if count == 2:
+                spread = jnp.where(odd, packed[k + 1 : k + 2], spread)
+            out.append(pltpu.roll(spread, 0, 1, stride=NARROW, stride_axis=0))
+        return pltpu.roll(stack(out) if len(out) > 1 else out[0], shift, 1)
 
     def ends(self, low, high):
         return jnp.where(self.first, low, jnp.where(self.last, high, 0.0))
 
-    def other_stiff(self, recv, at, mine, theirs, inner, corners):
+    def other_stiff(self, recv, at, mine, theirs, inner, corners, kinds, width):
         out = []
         edge = self.first | self.last
         for f in range(4):
             across = []
             for s in range(2):
                 r, k, t = corners[f][s][1]
-                across.append(self.look(recv, at, r, TABLE * k, s))
+                across.append(self.look(recv, at, r, kinds * k, s, width))
             value = inner[f] + PENALTY * (theirs[f] - mine[f])
             far = PENALTY * (theirs[f] - self.ends(*across))
             out.append(value + jnp.where(edge, far, 0.0))
@@ -304,7 +350,7 @@
 
 
 def start_kernel(sizes, own, payload, *refs):
-    body = Body(sizes, refs)
+    body = Body(sizes, refs, sizes[2])
     rows = own.shape[0]
     layer = lax.broadcasted_iota(jnp.int32, (body.depth, LANES), 0)
     low = lax.axis_index("sec") * rows
@@ -319,7 +365,7 @@
         [place(body.depth_sum(s, STIFF_BAND)) for s in strips],
         [place(body.depth_sum(s, MASS_BAND)) for s in strips],
     )
-    body.send(payload, [trace, inner], body.corner_table(trace), body.slabs)
+    body.send(payload, [trace, inner], body.pack(body.corner_table(trace), NARROW))
 
 
 def flux_tail(body, current, mine, other, r0, v1, m1, tr, tv, payload, potential):
@@ -339,13 +385,14 @@
     body.stiff0(lambda z: r0[z], image)
     trace, inner = body.traces(r0), body.traces(v1)
     tr[...], tv[...] = stack(trace), stack(inner)
-    body.send(payload, [trace, inner], body.corner_table(trace))
+    body.copies = 1
+    body.send(payload, [trace, inner], body.pack(body.corner_table(trace), NARROW))
 
 
 def first_kernel(sizes, recv, *refs):
     slabs, refs = refs[: sizes[2]], refs[sizes[2] :]
     c, sc, r0, v1, m1, tc, tr, tv, sides, payload, potential = refs[:11]
-    body = Body(sizes, refs[11:])
+    body = Body(sizes, refs[11:], sizes[2])
     depth, count = body.depth, body.slabs
     rows = depth // count
     sec = lax.axis_index("sec")
@@ -364,7 +411,9 @@
     for z in range(depth):
         potential[z] = cubic(c[z], sc[z])
     mine_s = body.traces(sc)
-    other_s = body.other_stiff(recv, 2 * depth, mine, other, inner, body.corners())
+    other_s = body.other_stiff(
+        recv, 2 * depth, mine, other, inner, body.corners(), 1, NARROW
+    )
     tc[0], tc[1] = stack(mine), stack(mine_s)
     sides[0], sides[1] = stack(other), stack(other_s)
     mine_p = [cubic(x, s) for x, s in zip(mine, mine_s)]
@@ -384,7 +433,9 @@
         u1[z] = v1[z] + body.column(z)
     body.add_rows(u1, jump, 1.0)
     mine_s = body.stiff_trace(unstack(tv, depth), jump)
-    other_s = body.other_stiff(recv, 2 * depth, mine, other, inner, body.corners())
+    other_s = body.other_stiff(
+        recv, 2 * depth, mine, other, inner, body.corners(), 1, NARROW
+    )
     tu[...] = stack(mine_s)
     sides[0], sides[1] = stack(other), stack(other_s)
     jump = body.jumps(mine_s, other_s)
@@ -418,7 +469,7 @@
     for i in range(3):
         total = jnp.sum(stack(sums[i]), axis=1, keepdims=True)
         table = jnp.where(body.lane == SUMS + i, total, table)
-    body.send(payload, [trace, inner, outer], table)
+    body.send(payload, [trace, inner, outer], body.pack(table, BROAD))
 
 
 def third_kernel(sizes, last, r0, y, v2, m2, ty, tv2, recv, *refs):
@@ -430,11 +481,16 @@
         body = Body(sizes, refs[10:])
     depth, patches = body.depth, body.patches
     at = 3 * depth
-    known = recv[0, at : at + depth, :]
+    packed = depth * BROAD // LANES
+    known = recv[at : at + packed, :]
     for p in range(1, patches):
-        known = known + recv[p, at : at + depth, :]
-    known = jnp.sum(known, axis=0, keepdims=True)
-    m0, m1, m2s = [known[:, SUMS + i : SUMS + i + 1] for i in range(3)]
+        known = known + recv[p * (at + packed) + at : (p + 1) * (at + packed), :]
+    odd = lax.broadcasted_iota(jnp.int32, (packed, LANES), 0) & 1
+    slot = lax.broadcasted_iota(jnp.int32, (packed, LANES), 1) + NARROW * odd
+    slot = slot & (BROAD - 1)
+    m0, m1, m2s = [
+        jnp.sum(jnp.where(slot == SUMS + i, known, 0.0), keepdims=True) for i in range(3)
+    ]
     a0 = m0 / m1
     other, inner, outer = body.received(recv, 3)
     corners = body.corners()
@@ -445,20 +501,20 @@
         u2[z] = v2[z] + body.column(z)
     body.add_rows(u2, jump, 1.0)
     mine_s = body.stiff_trace(unstack(tv2, depth), jump)
-    other_s = body.other_stiff(recv, at, mine, other, inner, corners)
+    other_s = body.other_stiff(recv, at, mine, other, inner, corners, KINDS, BROAD)
     masses, stiffs, far = [], [], []
     for f in range(4):
         arm_m, arm_k, across = [], [], []
         for s in range(2):
             (q, kq, tq), (r, k, kind), (r2, k2) = corners[f][s]
-            look = functools.partial(body.look, recv, at, side=s)
-            arm_m.append(look(q, TABLE * kq + tq) - look(r, TABLE * k + kind))
-            arm_k.append(look(q, TABLE * kq + tq + 1) - look(r, TABLE * k + kind + 1))
-            value = look(r, TABLE * k)
+            look = functools.partial(body.look, recv, at, side=s, width=BROAD)
+            arm_m.append(look(q, KINDS * kq + tq) - look(r, KINDS * k + kind))
+            arm_k.append(look(q, KINDS * kq + tq + 1) - look(r, KINDS * k + kind + 1))
+            value = look(r, KINDS * k)
             across.append(
-                look(r, TABLE * k + 1)
+                look(r, KINDS * k + 1)
                 + PENALTY * (value - other[f])
-                + PENALTY * (value - look(r2, TABLE * k2))
+                + PENALTY * (value - look(r2, KINDS * k2))
             )
         theirs = PENALTY * (other[f] - mine[f])
         masses.append(MASS_BAND[0] * theirs + PENALTY * body.ends(*arm_m))
@@ -504,20 +560,22 @@
         moments = jnp.where(lane == i, value, moments)
     for i, value in enumerate((a0, m0, m1, m2s)):
         base[i : i + 1, :] = jnp.broadcast_to(value, (1, LANES))
+    rows = payload.shape[0] // patches
     for to in range(patches):
-        payload[to, :1, :] = moments
+        payload[to * rows : to * rows + 1, :] = moments
     if not last:
         trace = body.traces(zf)
         tt[...], tu2[...], tz[...] = stack(mine_t), stack(mine_s), stack(trace)
         sides[0], sides[1], sides[2] = stack(other), stack(other_s), stack(other_t)
         for f in range(4):
-            payload[body.partner(body.me, f), 8 : 8 + depth, :] = trace[f]
+            payload[pl.ds(body.partner(body.me, f) * rows + 1, depth), :] = trace[f]
 
 
 def weights(patches, base, recv):
-    total = recv[0, :1, :]
+    rows = recv.shape[0] // patches
+    total = recv[:1, :]
     for p in range(1, patches):
-        total = total + recv[p, :1, :]
+        total = total + recv[p * rows : p * rows + 1, :]
     a0, m0, m1, m2 = [base[i : i + 1, :1] for i in range(4)]
     rr1, g1, g2, tt, ty, tat = [total[:, i : i + 1] for i in range(6)]
     b0 = rr1 / m0
@@ -548,7 +606,7 @@
     for z in range(depth):
         cn[z] = mix(c[z], r0[z], y[z], t[z])
         potential[z] = cubic(cn[z], mix(sc[z], u1[z], u2[z], zf[z]))
-    (side_z,) = body.received(recv, 1, 8)
+    (side_z,) = body.received(recv, 1, 1)
     mine = cubic(
         mix(tc[0], tr[...], ty[...], tt[...]), mix(tc[1], tu[...], tu2[...], tz[...])
     )
@@ -576,10 +634,10 @@
     halves = [own]
     for k in range(1, slabs):
         halves.append(lax.ppermute(own, "sec", [((i + k) % slabs, i) for i in range(slabs)]))
-    consts = [jnp.asarray(x) for x in constants(depth)]
-    tables = [partner, face_id, flip]
+    matrices = [jnp.asarray(x) for x in constants()]
+    tables = [partner.T, face_id.T, flip.T]
     vmem, smem = pl.BlockSpec(memory_space=pltpu.VMEM), pl.BlockSpec(memory_space=pltpu.SMEM)
-    params = pltpu.CompilerParams(vmem_limit_bytes=48 << 20)
+    params = pltpu.CompilerParams(vmem_limit_bytes=(4 + depth) << 20)
 
     def shape(*dims):
         return jax.ShapeDtypeStruct(dims, jnp.float32)
@@ -590,10 +648,10 @@
         return shape(count, 4 * depth, LANES)
 
     def load(count):
-        return shape(patches, count, LANES)
-
-    def call(kernel, outs, *args, fields=0):
-        count = len(args)
+        return shape(patches * count, LANES)
+
+    def call(kernel, outs, *args, fields=0, consts=matrices, cost=None):
+        count, head = len(args), 3 + len(consts)
         inside = [pltpu.VMEM((depth, LANES, LANES), jnp.float32)] * fields
         shared = [
             pltpu.VMEM((4, LANES + 2 * PAD, LANES), jnp.float32),
@@ -603,7 +661,7 @@
         ]
 
         def run(*refs):
-            common, rest = refs[:8], refs[8:]
+            common, rest = refs[:head], refs[head:]
             cut = len(rest) - len(shared)
             kernel((depth, patches, slabs), *rest[:cut], *common, *rest[cut:])
 
@@ -614,23 +672,33 @@
             out_specs=[vmem] * len(outs),
             scratch_shapes=inside + shared,
             compiler_params=params,
+            cost_estimate=cost,
             name=kernel.__name__ if hasattr(kernel, "__name__") else "third_kernel",
         )(*tables, *consts, *args)
 
-    def swap(payload, axes="patch"):
-        return lax.all_to_all(payload, axes, 0, 0)
-
-    (payload,) = call(start_kernel, [shape(patches * slabs, 3 * depth, LANES)], own)
+    def swap(payload, axes="patch", parts=patches):
+        rows = payload.shape[0] // parts
+        moved = lax.all_to_all(payload.reshape(parts, 1, rows * LANES), axes, 0, 0)
+        return moved.reshape(parts * rows, LANES)
+
+    narrow, broad = depth * NARROW // LANES, depth * BROAD // LANES
+    (payload,) = call(
+        start_kernel,
+        [load(slabs * (2 * depth + narrow))],
+        own,
+        consts=[],
+        cost=pl.CostEstimate(flops=COST, bytes_accessed=4 * own.size, transcendentals=0),
+    )
     c, sc, r0, v1, m1, tc, tr, tv, side_c, payload = call(
         first_kernel,
-        [field] * 5 + [sides(2), trace, trace, sides(2), load(3 * depth)],
-        swap(payload, ("patch", "sec")), *halves,
+        [field] * 5 + [sides(2), trace, trace, sides(2), load(2 * depth + narrow)],
+        swap(payload, ("patch", "sec"), patches * slabs), *halves,
         fields=1,
     )
     for step in range(STEPS):
         u1, y, v2, m2, ty, tv2, tu, side_r, payload = call(
             second_kernel,
-            [field] * 4 + [trace] * 3 + [sides(2), load(4 * depth)],
+            [field] * 4 + [trace] * 3 + [sides(2), load(3 * depth + broad)],
             r0, v1, m1, tr, tv, swap(payload),
         )
         last = step + 1 == STEPS
@@ -638,7 +706,7 @@
         if last:
             outs += [load(1)]
         else:
-            outs += [field] * 2 + [trace] * 3 + [sides(3), load(8 + depth)]
+            outs += [field] * 2 + [trace] * 3 + [sides(3), load(1 + depth)]
         t, base_now, *rest = call(
             lambda sizes, *refs, last=last: third_kernel(sizes, last, *refs),
             outs,
@@ -651,7 +719,7 @@
         u2, zf, tt, tu2, tz, side_y, payload = rest
         c, r0, v1, m1, tr, tv, payload = call(
             next_kernel,
-            [field] * 4 + [trace] * 2 + [load(3 * depth)],
+            [field] * 4 + [trace] * 2 + [load(2 * depth + narrow)],
             c, r0, y, t, sc, u1, u2, zf, tc, tr, tu, ty, tu2, tt, tz,
             side_c, side_r, side_y, base_now, swap(payload),
             fields=1,

time: 133 us -> 118 us (0.89)
  local copies, waits for them, and re-layouts: 7.75 us -> 1.67 us
  blocking collectives: 71 us -> 66.3 us
  Pallas kernels: 33.2 us -> 31 us
    unnamed x33 -> x14, local copies, waits for them, and re-layouts: 7.75 us -> 1.67 us
    all_to_all x6, blocking collectives: 71 us -> 66.3 us  [swap(): moved = lax.all_to_all(payload.reshape(parts, 1, rows * LANES), axes, 0, 0)]
    pallas_call x7, Pallas kernels: 32.2 us -> 30 us  [call(): pl.pallas_call(run, out_shape=outs, in_specs=[smem] * 3 + [vmem] * (len(c...]
  transfers between devices with their start and end apart: 2 -> 2, of which waited for: 2 -> 1; matrix products, arithmetic and copies ran while one was open for 0% -> 0% of each run, Pallas kernels for 0% -> 0%
where the time goes in v2:
time: 118 us
  blocking collectives  66.3 us (56%)
  Pallas kernels  31 us (26%)
  waiting for transfers between devices  9.62 us (8%)
  starting transfers between devices  9.13 us (8%)
  local copies, waits for them, and re-layouts  1.67 us (1%)
    all_to_all x6, blocking collectives, swap(): moved = lax.all_to_all(payload.reshape(parts, 1, rows * LANES), axes, 0, 0)  66.3 us
    pallas_call x7, Pallas kernels, call(): pl.pallas_call(run, out_shape=outs, in_specs=[smem] * 3 + [vmem] * (len(c...  30 us
    ppermute x1, waiting for transfers between devices, shards(): lax.ppermute(own, 'sec', [((i + k) % slabs, i) for i in range(slabs)])  9.62 us
    all_to_all x1, starting transfers between devices, swap(): moved = lax.all_to_all(payload.reshape(parts, 1, rows * LANES), axes, 0, 0)  7.3 us
  transfers between devices with their start and end apart: 2, of which 1 were waited for; matrix products, arithmetic and copies ran while one was open for 0% of the time, Pallas kernels for 0%

profile of v2, /device:TPU:0, one launch (start us, length us, event | category | flops | bytes accessed | tf_op | source)
XLA Modules:
  0.0 117.9 jit_solution(5689286535364326153)
XLA Ops:
  0.0 0.0 copy-start.6
  0.0 0.0 copy-start.5
  0.0 0.0 copy-start.4
  0.0 0.7 copy-done.6
  0.7 0.0 copy-done.5
  0.7 0.0 copy-done.4
  0.7 0.0 copy-start.2
  0.7 0.9 copy-done.2
  1.7 1.9 %start_kernel.1 = f32[544,128]{1,0:T(8,128)} custom-call(s32[4,16]{1,0:T(4,128)S(1)} %bitcast.35, s32[4,16]{1,0:T(4,128)S(1)} %bitcast.42, s32[4,16]{1,0:T(4,128)S(1)} %bitcast.49, f32[4,128,128]{2,1,0:T(8,128)S(1)} %bitcast.27), custom_call_target="tpu_custom_call" | custom-call | flops 17179869184 | bytes 262144 | tf_op jit(solution)/shard_map/start_kernel/pallas_call | solution.py:668
  3.6 0.0 copy-start.3
  3.6 0.0 copy-start
  3.6 0.0 copy-start.1
  3.6 7.3 %all-to-all-start = ((f32[32,1,2176]{2,1,0:T(1,128)}), f32[32,1,2176]{2,1,0:T(1,128)S(1)}, u32[]{:S(2)}, u32[]{:S(2)}) async-start(f32[32,1,2176]{2,1,0:T(1,128)} %bitcast.4), calls=%async_computation | async-start | bytes 557056 | tf_op jit(solution)/shard_map/all_to_all | solution.py:681
  10.9 0.0 copy-done.3
  10.9 1.8 %collective-permute-start = (f32[4,128,128]{2,1,0:T(8,128)S(1)}, f32[4,128,128]{2,1,0:T(8,128)S(1)}, u32[]{:S(2)}, u32[]{:S(2)}) collective-permute-start(f32[4,128,128]{2,1,0:T(8,128)S(1)} %bitcast.28), channel_id=1, source_target_pairs={{1,0},{0,1},{3,2},{2,3},{5,4},{4,5},{7,6},{6,7},{9,8},{8,9},{11,10... | collective-permute-start | bytes 786440 | tf_op jit(solution)/shard_map/ppermute | solution.py:636
  12.7 9.6 %collective-permute-done.refs_7_ = f32[4,128,128]{2,1,0:T(8,128)S(1)} collective-permute-done((f32[4,128,128]{2,1,0:T(8,128)S(1)}, f32[4,128,128]{2,1,0:T(8,128)S(1)}, u32[]{:S(2)}, u32[]{:S(2)}) %collective-permute-start) | collective-permute-done | bytes 262176 | tf_op jit(solution)/shard_map/ppermute | solution.py:636
  22.3 0.0 all-to-all-done
  22.3 0.0 copy-done
  22.3 0.0 copy-done.1
  22.3 4.9 %first_kernel.1 = (f32[8,128,128]{2,1,0:T(8,128)S(1)}, f32[8,128,128]{2,1,0:T(8,128)S(1)}, f32[8,128,128]{2,1,0:T(8,128)S(1)}, f32[8,128,128]{2,1,0:T(8,128)S(1)...) custom-call(s32[4,16]{1,0:T(4,128)S(1)} %bitcast.36, ...), custom_call_target="tpu_custom_call" | custom-call | tf_op jit(solution)/shard_map/first_kernel/pallas_call | solution.py:668
  27.2 13.4 %all_to_all.35 = f32[16,1,2176]{2,1,0:T(1,128)S(1)} all-to-all(f32[16,1,2176]{2,1,0:T(1,128)S(1)} %bitcast.33), channel_id=1, replica_groups=mesh['patch'=16,'sec'=2] {'patch'}, dimensions={0} | all-to-all | bytes 278528 | tf_op jit(solution)/shard_map/all_to_all | solution.py:681
  40.6 4.5 %second_kernel.2 = (f32[8,128,128]{2,1,0:T(8,128)S(1)}, f32[8,128,128]{2,1,0:T(8,128)S(1)}, f32[8,128,128]{2,1,0:T(8,128)S(1)}, f32[8,128,128]{2,1,0:T(8,128)S(1...) custom-call(s32[4,16]{1,0:T(4,128)S(1)} %bitcast.37, ...), custom_call_target="tpu_custom_call" | custom-call | tf_op jit(solution)/shard_map/second_kernel/pallas_call | solution.py:668
  45.1 11.8 %all_to_all.36 = f32[16,1,3328]{2,1,0:T(1,128)S(1)} all-to-all(f32[16,1,3328]{2,1,0:T(1,128)S(1)} %bitcast.31), channel_id=1, replica_groups=mesh['patch'=16,'sec'=2] {'patch'}, dimensions={0} | all-to-all | bytes 425984 | tf_op jit(solution)/shard_map/all_to_all | solution.py:681
  57.0 4.9 %_lambda_.2 = (f32[8,128,128]{2,1,0:T(8,128)S(1)}, f32[8,128]{1,0:T(8,128)S(1)}, f32[8,128,128]{2,1,0:T(8,128)S(1)}, f32[8,128,128]{2,1,0:T(8,128)S(1)}, f32[32,...) custom-call(s32[4,16]{1,0:T(4,128)S(1)} %bitcast.38, ...), custom_call_target="tpu_custom_call" | custom-call | tf_op jit(solution)/shard_map/<lambda>/pallas_call | solution.py:668
  61.8 9.6 %all_to_all.37 = f32[16,1,1152]{2,1,0:T(1,128)S(1)} all-to-all(f32[16,1,1152]{2,1,0:T(1,128)S(1)} %bitcast.34), channel_id=1, replica_groups=mesh['patch'=16,'sec'=2] {'patch'}, dimensions={0} | all-to-all | bytes 147456 | tf_op jit(solution)/shard_map/all_to_all | solution.py:681
  71.4 3.9 %next_kernel.1 = (f32[8,128,128]{2,1,0:T(8,128)S(1)}, f32[8,128,128]{2,1,0:T(8,128)S(1)}, f32[8,128,128]{2,1,0:T(8,128)S(1)}, f32[8,128,128]{2,1,0:T(8,128)S(1)}...) custom-call(s32[4,16]{1,0:T(4,128)S(1)} %bitcast.39, s32[4,16]{1,0:T(4,128)S(1)} %bitcast.46, ...), custom_call_target="tpu_custom_call" | custom-call | tf_op jit(solution)/shard_map/next_kernel/pallas_call | solution.py:668
  75.3 10.7 %all_to_all.38 = f32[16,1,2176]{2,1,0:T(1,128)S(1)} all-to-all(f32[16,1,2176]{2,1,0:T(1,128)S(1)} %bitcast.32), channel_id=1, replica_groups=mesh['patch'=16,'sec'=2] {'patch'}, dimensions={0} | all-to-all | bytes 278528 | tf_op jit(solution)/shard_map/all_to_all | solution.py:681
  86.0 5.2 %second_kernel.3 = (f32[8,128,128]{2,1,0:T(8,128)}, f32[8,128,128]{2,1,0:T(8,128)S(1)}, f32[8,128,128]{2,1,0:T(8,128)S(1)}, f32[8,128,128]{2,1,0:T(8,128)S(1)}, ...) custom-call(s32[4,16]{1,0:T(4,128)S(1)} %bitcast.40, ...), custom_call_target="tpu_custom_call" | custom-call | tf_op jit(solution)/shard_map/second_kernel/pallas_call | solution.py:668
  91.2 11.8 %all_to_all.39 = f32[16,1,3328]{2,1,0:T(1,128)S(1)} all-to-all(f32[16,1,3328]{2,1,0:T(1,128)S(1)} %bitcast.30), channel_id=1, replica_groups=mesh['patch'=16,'sec'=2] {'patch'}, dimensions={0} | all-to-all | bytes 425984 | tf_op jit(solution)/shard_map/all_to_all | solution.py:681
  103.1 4.8 %_lambda_.3 = (f32[8,128,128]{2,1,0:T(8,128)S(1)}, f32[8,128]{1,0:T(8,128)S(1)}, f32[16,128]{1,0:T(8,128)S(1)}) custom-call(s32[4,16]{1,0:T(4,128)S(1)} %bitcast.41, s32[4,16]{1,0:T(4,128)S(1)} %bitcast.48, s32[4,16]{1,0:T(4,128)S(1)} %bitcast.55, bf16[256,256]{1,0:T(8,128)(2,1)S(1)} %copy-done.1, bf16[256,256]{1,0:T(8,128)(2,1)S(1)} %copy-done, ...), custom_call_target="tpu_custom_call" | custom-call | tf_op jit(solution)/shard_map/<lambda>/pallas_call | solution.py:668
  107.8 9.0 %all_to_all.40 = f32[16,1,128]{2,1,0:T(1,128)S(1)} all-to-all(f32[16,1,128]{2,1,0:T(1,128)S(1)} %bitcast.57), channel_id=1, replica_groups=mesh['patch'=16,'sec'=2] {'patch'}, dimensions={0} | all-to-all | bytes 16384 | tf_op jit(solution)/shard_map/all_to_all | solution.py:681
  116.8 1.1 shard_map.64
Async XLA Ops:
  0.0 0.7 copy-start.6
  0.0 0.7 copy-start.5
  0.0 0.7 copy-start.4
  0.7 0.9 copy-start.2
  3.6 7.3 %copy-start.3 = (f32[1,4,128,128]{3,2,1,0:T(8,128)S(1)}, f32[1,4,128,128]{3,2,1,0:T(8,128)}, u32[]{:S(2)}) copy-start(f32[1,4,128,128]{3,2,1,0:T(8,128)} %param.6) | copy-start | bytes 786436
  3.6 18.8 %copy-start = (bf16[256,256]{1,0:T(8,128)(2,1)S(1)}, bf16[256,256]{1,0:T(8,128)(2,1)}, u32[]{:S(2)}) copy-start(bf16[256,256]{1,0:T(8,128)(2,1)} %constant.5.clone.refs_4_) | copy-start | bytes 393220
  3.6 18.8 %copy-start.1 = (bf16[256,256]{1,0:T(8,128)(2,1)S(1)}, bf16[256,256]{1,0:T(8,128)(2,1)}, u32[]{:S(2)}) copy-start(bf16[256,256]{1,0:T(8,128)(2,1)} %constant.4.clone.refs_3_) | copy-start | bytes 393220
  3.6 18.8 %all-to-all-start = ((f32[32,1,2176]{2,1,0:T(1,128)}), f32[32,1,2176]{2,1,0:T(1,128)S(1)}, u32[]{:S(2)}, u32[]{:S(2)}) async-start(f32[32,1,2176]{2,1,0:T(1,128)} %bitcast.4), calls=%async_computation | async-start | bytes 557056 | tf_op jit(solution)/shard_map/all_to_all | solution.py:681
  10.9 11.5 %collective-permute-start = (f32[4,128,128]{2,1,0:T(8,128)S(1)}, f32[4,128,128]{2,1,0:T(8,128)S(1)}, u32[]{:S(2)}, u32[]{:S(2)}) collective-permute-start(f32[4,128,128]{2,1,0:T(8,128)S(1)} %bitcast.28), channel_id=1, source_target_pairs={{1,0},{0,1},{3,2},{2,3},{5,4},{4,5},{7,6},{6,7},{9,8},{8,9},{11,10... | collective-permute-start | bytes 786440 | tf_op jit(solution)/shard_map/ppermute | solution.py:636

commit v3 on v2

--- a/solution.py
+++ b/solution.py
@@ -255,14 +255,15 @@
         return stack(rows) if len(rows) > 1 else rows[0]
 
     def send(self, payload, groups, packed):
-        depth, copies = self.depth, self.copies
+        copies = self.copies
         rows = payload.shape[0] // (self.patches * copies)
-        at = len(groups) * depth
         for f in range(4):
-            to = self.partner(self.me, f) * copies
-            for i, group in enumerate(groups):
+            to, at = self.partner(self.me, f) * copies, 0
+            for group in groups:
+                high = group[f].shape[0]
                 for s in range(copies):
-                    payload[pl.ds((to + s) * rows + i * depth, depth), :] = group[f]
+                    payload[pl.ds((to + s) * rows + at, high), :] = group[f]
+                at += high
         for to in range(self.patches * copies):
             payload[to * rows + at : (to + 1) * rows, :] = packed
 
@@ -275,9 +276,14 @@
         return out
 
     def received(self, recv, count, at=0):
+        rows = count * self.depth
+        return self.oriented(
+            [self.take(recv, self.partner(self.me, f), at, rows) for f in range(4)], count
+        )
+
+    def oriented(self, raw, count):
         depth = self.depth
         rows = count * depth
-        raw = [self.take(recv, self.partner(self.me, f), at, rows) for f in range(4)]
         turned = dot(stack(raw), self.reverse)
         out = []
         for f in range(4):
@@ -360,12 +366,13 @@
         return jnp.where(here, stack([value] * body.slabs), 0.0)
 
     strips = body.strips(own)
-    trace = [place(s[0]) for s in strips]
+    trace = [s[0] for s in strips]
     inner = body.slab(
         [place(body.depth_sum(s, STIFF_BAND)) for s in strips],
         [place(body.depth_sum(s, MASS_BAND)) for s in strips],
     )
-    body.send(payload, [trace, inner], body.pack(body.corner_table(trace), NARROW))
+    table = body.corner_table([place(a) for a in trace])
+    body.send(payload, [trace, inner], body.pack(table, NARROW))
 
 
 def flux_tail(body, current, mine, other, r0, v1, m1, tr, tv, payload, potential):
@@ -389,32 +396,45 @@
     body.send(payload, [trace, inner], body.pack(body.corner_table(trace), NARROW))
 
 
-def first_kernel(sizes, recv, *refs):
+def middle_kernel(sizes, *refs):
     slabs, refs = refs[: sizes[2]], refs[sizes[2] :]
-    c, sc, r0, v1, m1, tc, tr, tv, sides, payload, potential = refs[:11]
-    body = Body(sizes, refs[11:], sizes[2])
+    c, v0, tc, tv = refs[:4]
+    body = Body(sizes, refs[4:])
+    count = body.slabs
+    rows = body.depth // count
+    for k, slab in enumerate(slabs):
+        c[pl.ds(lax.rem(lax.axis_index("sec") + k, count) * rows, rows)] = slab[...]
+
+    def image(z, stiff, mass):
+        v0[z] = stiff
+
+    body.stiff0(lambda z: c[z], image)
+    tc[...], tv[...] = stack(body.traces(c)), stack(body.traces(v0))
+
+
+def first_kernel(sizes, c, v0, tc, tv0, recv, sc, r0, v1, m1, ts, tr, tv, sides, payload,
+                 potential, *refs):
+    body = Body(sizes, refs, sizes[2])
     depth, count = body.depth, body.slabs
     rows = depth // count
-    sec = lax.axis_index("sec")
-    for k, slab in enumerate(slabs):
-        c[pl.ds(lax.rem(sec + k, count) * rows, rows)] = slab[...]
-    other, inner = body.received(recv, 2)
-    mine = body.traces(c)
+    high = recv.shape[0] // (body.patches * count)
+    raw = []
+    for f in range(4):
+        q = body.partner(body.me, f)
+        parts = [recv[pl.ds((q * count + s) * high, rows), :] for s in range(count)]
+        raw.append(stack(parts + [body.take(recv, q, rows, depth)]))
+    other, inner = body.oriented(raw, 2)
+    mine = unstack(tc, depth)
     jump = body.jumps(mine, other)
     body.stand(jump)
-
-    def curve(z, stiff, mass):
-        sc[z] = stiff + body.column(z)
-
-    body.stiff0(lambda z: c[z], curve)
+    for z in range(depth):
+        sc[z] = v0[z] + body.column(z)
     body.add_rows(sc, jump, 1.0)
     for z in range(depth):
         potential[z] = cubic(c[z], sc[z])
-    mine_s = body.traces(sc)
-    other_s = body.other_stiff(
-        recv, 2 * depth, mine, other, inner, body.corners(), 1, NARROW
-    )
-    tc[0], tc[1] = stack(mine), stack(mine_s)
+    mine_s = body.stiff_trace(unstack(tv0, depth), jump)
+    other_s = body.other_stiff(recv, rows + depth, mine, other, inner, body.corners(), 1, NARROW)
+    ts[...] = stack(mine_s)
     sides[0], sides[1] = stack(other), stack(other_s)
     mine_p = [cubic(x, s) for x, s in zip(mine, mine_s)]
     other_p = [cubic(x, s) for x, s in zip(other, other_s)]
@@ -593,7 +613,7 @@
     return a0 + a1 * (1.0 + b0) + a2 * (c1 + c0), -a0 * (a1 + a2 * c1), a2 * c2
 
 
-def next_kernel(sizes, c, r0, y, t, sc, u1, u2, zf, tc, tr, tu, ty, tu2, tt, tz,
+def next_kernel(sizes, c, r0, y, t, sc, u1, u2, zf, tc, ts, tr, tu, ty, tu2, tt, tz,
                 side_c, side_r, side_y, base, recv,
                 cn, rn, v1, m1, trn, tvn, payload, potential, *refs):
     body = Body(sizes, refs)
@@ -608,7 +628,7 @@
         potential[z] = cubic(cn[z], mix(sc[z], u1[z], u2[z], zf[z]))
     (side_z,) = body.received(recv, 1, 1)
     mine = cubic(
-        mix(tc[0], tr[...], ty[...], tt[...]), mix(tc[1], tu[...], tu2[...], tz[...])
+        mix(tc[...], tr[...], ty[...], tt[...]), mix(ts[...], tu[...], tu2[...], tz[...])
     )
     other = cubic(
         mix(side_c[0], side_r[0], side_y[0], side_y[2]),
@@ -684,15 +704,21 @@
     narrow, broad = depth * NARROW // LANES, depth * BROAD // LANES
     (payload,) = call(
         start_kernel,
-        [load(slabs * (2 * depth + narrow))],
+        [load(slabs * (rows + depth + narrow))],
         own,
         consts=[],
         cost=pl.CostEstimate(flops=COST, bytes_accessed=4 * own.size, transcendentals=0),
     )
-    c, sc, r0, v1, m1, tc, tr, tv, side_c, payload = call(
+    c, v0, tc, tv0 = call(
+        middle_kernel,
+        [field, field, trace, trace],
+        *halves,
+        cost=pl.CostEstimate(flops=COST, bytes_accessed=4 * own.size, transcendentals=0),
+    )
+    sc, r0, v1, m1, ts, tr, tv, side_c, payload = call(
         first_kernel,
-        [field] * 5 + [sides(2), trace, trace, sides(2), load(2 * depth + narrow)],
-        swap(payload, ("patch", "sec"), patches * slabs), *halves,
+        [field] * 4 + [trace] * 3 + [sides(2), load(2 * depth + narrow)],
+        c, v0, tc, tv0, swap(payload, ("patch", "sec"), patches * slabs),
         fields=1,
     )
     for step in range(STEPS):
@@ -720,7 +746,7 @@
         c, r0, v1, m1, tr, tv, payload = call(
             next_kernel,
             [field] * 4 + [trace] * 2 + [load(2 * depth + narrow)],
-            c, r0, y, t, sc, u1, u2, zf, tc, tr, tu, ty, tu2, tt, tz,
+            c, r0, y, t, sc, u1, u2, zf, tc, ts, tr, tu, ty, tu2, tt, tz,
             side_c, side_r, side_y, base_now, swap(payload),
             fields=1,
         )

time: 118 us -> 113 us (0.958)
  blocking collectives: 66.3 us -> 63.6 us
  waiting for transfers between devices: 9.62 us -> 7.83 us
  starting transfers between devices: 9.13 us -> 7.86 us
    ppermute x1, waiting for transfers between devices: 9.62 us -> 0.01 us  [shards(): lax.ppermute(own, 'sec', [((i + k) % slabs, i) for i in range(slabs)])]
    all_to_all x1, waiting for transfers between devices: 0.01 us -> 7.83 us  [swap(): moved = lax.all_to_all(payload.reshape(parts, 1, rows * LANES), axes, 0, 0)]
    all_to_all x6, blocking collectives: 66.3 us -> 63.6 us  [swap(): moved = lax.all_to_all(payload.reshape(parts, 1, rows * LANES), axes, 0, 0)]
    all_to_all x1, starting transfers between devices: 7.3 us -> 4.89 us  [swap(): moved = lax.all_to_all(payload.reshape(parts, 1, rows * LANES), axes, 0, 0)]
    pallas_call x7 -> x8, Pallas kernels: 30 us -> 30.9 us  [call(): pl.pallas_call(run, out_shape=outs, in_specs=[smem] * 3 + [vmem] * (len(c...]
  transfers between devices with their start and end apart: 2 -> 2, of which waited for: 1 -> 1; matrix products, arithmetic and copies ran while one was open for 0% -> 0% of each run, Pallas kernels for 0% -> 3%
where the time goes in v3:
time: 113 us
  blocking collectives  63.6 us (56%)
  Pallas kernels  31.9 us (28%)
  starting transfers between devices  7.86 us (7%)
  waiting for transfers between devices  7.83 us (7%)
  local copies, waits for them, and re-layouts  1.66 us (1%)
    all_to_all x6, blocking collectives, swap(): moved = lax.all_to_all(payload.reshape(parts, 1, rows * LANES), axes, 0, 0)  63.6 us
    pallas_call x8, Pallas kernels, call(): pl.pallas_call(run, out_shape=outs, in_specs=[smem] * 3 + [vmem] * (len(c...  30.9 us
    all_to_all x1, waiting for transfers between devices, swap(): moved = lax.all_to_all(payload.reshape(parts, 1, rows * LANES), axes, 0, 0)  7.83 us
    all_to_all x1, starting transfers between devices, swap(): moved = lax.all_to_all(payload.reshape(parts, 1, rows * LANES), axes, 0, 0)  4.89 us
    ppermute x1, starting transfers between devices, shards(): lax.ppermute(own, 'sec', [((i + k) % slabs, i) for i in range(slabs)])  2.97 us
  transfers between devices with their start and end apart: 2, of which 1 were waited for; matrix products, arithmetic and copies ran while one was open for 0% of the time, Pallas kernels for 3%

profile of v3, /device:TPU:0, one launch (start us, length us, event | category | flops | bytes accessed | tf_op | source)
XLA Modules:
  0.0 113.0 jit_solution(7869822206500152978)
XLA Ops:
  0.0 0.0 copy-start.4
  0.0 3.0 %collective-permute-start = (f32[4,128,128]{2,1,0:T(8,128)}, f32[4,128,128]{2,1,0:T(8,128)S(1)}, u32[]{:S(2)}, u32[]{:S(2)}) collective-permute-start(f32[4,128,128]{2,1,0:T(8,128)} %bitcast.58), channel_id=1, source_target_pairs={{1,0},{0,1},{3,2},{2,3},{5,4},{4,5},{7,6},{6,7},{9,8},{8,9},{11,10... | collective-permute-start | bytes 786440 | tf_op jit(solution)/shard_map/ppermute | solution.py:656
  3.0 0.0 copy-start.3
  3.0 0.0 copy-start.2
  3.0 0.0 copy-done.4
  3.0 0.7 copy-done.3
  3.7 0.0 copy-done.2
  3.7 0.0 copy-start.5
  3.7 0.9 copy-done.5
  4.6 0.0 copy-start.6
  4.6 1.9 %start_kernel.1 = f32[416,128]{1,0:T(8,128)} custom-call(s32[4,16]{1,0:T(4,128)S(1)} %bitcast.32, s32[4,16]{1,0:T(4,128)S(1)} %bitcast.40, s32[4,16]{1,0:T(4,128)S(1)} %bitcast.48, f32[4,128,128]{2,1,0:T(8,128)S(1)} %bitcast.59), custom_call_target="tpu_custom_call" | custom-call | flops 17179869184 | bytes 262144 | tf_op jit(solution)/shard_map/start_kernel/pallas_call | solution.py:688
  6.5 0.0 copy-start
  6.5 0.0 copy-start.1
  6.5 4.9 %all-to-all-start = ((f32[32,1,1664]{2,1,0:T(1,128)}), f32[32,1,1664]{2,1,0:T(1,128)S(1)}, u32[]{:S(2)}, u32[]{:S(2)}) async-start(f32[32,1,1664]{2,1,0:T(1,128)} %bitcast.4), calls=%async_computation | async-start | bytes 425984 | tf_op jit(solution)/shard_map/all_to_all | solution.py:701
  11.4 0.0 collective-permute-done.refs_6_
  11.4 0.0 copy-done.6
  11.4 0.0 copy-done
  11.4 0.0 copy-done.1
  11.4 2.1 %middle_kernel.1 = (f32[8,128,128]{2,1,0:T(8,128)S(1)}, f32[8,128,128]{2,1,0:T(8,128)S(1)}, f32[32,128]{1,0:T(8,128)S(1)}, f32[32,128]{1,0:T(8,128)S(1)}) custom-call(s32[4,16]{1,0:T(4,128)S(1)} %bitcast.33, s32[4,16]{1,0:T(4,128)S(1)} %bitcast.41, s32[4,16]{1,0:T(4,128)S(1)} %bitcast.49, bf16[256,256]{1,0:T(8,128)(2,1)S(1)} %copy-done.1, ...), custom_call_target="tpu_custom_call" | custom-call | flops 17179869184 | bytes 262144 | tf_op jit(solution)/shard_map/middle_kernel/pallas_call | solution.py:688
  13.5 7.8 %all-to-all-done = f32[32,1,1664]{2,1,0:T(1,128)S(1)} async-done(((f32[32,1,1664]{2,1,0:T(1,128)}), f32[32,1,1664]{2,1,0:T(1,128)S(1)}, u32[]{:S(2)}, u32[]{:S(2)}) %all-to-all-start) | async-done | bytes 213024 | tf_op jit(solution)/shard_map/all_to_all | solution.py:701
  21.3 3.8 %first_kernel.1 = (f32[8,128,128]{2,1,0:T(8,128)S(1)}, f32[8,128,128]{2,1,0:T(8,128)S(1)}, f32[8,128,128]{2,1,0:T(8,128)S(1)}, f32[8,128,128]{2,1,0:T(8,128)S(1)...) custom-call(s32[4,16]{1,0:T(4,128)S(1)} %bitcast.34, ...), custom_call_target="tpu_custom_call" | custom-call | tf_op jit(solution)/shard_map/first_kernel/pallas_call | solution.py:688
  25.1 10.7 %all_to_all.35 = f32[16,1,2176]{2,1,0:T(1,128)S(1)} all-to-all(f32[16,1,2176]{2,1,0:T(1,128)S(1)} %bitcast.30), channel_id=1, replica_groups=mesh['patch'=16,'sec'=2] {'patch'}, dimensions={0} | all-to-all | bytes 278528 | tf_op jit(solution)/shard_map/all_to_all | solution.py:701
  35.8 4.5 %second_kernel.2 = (f32[8,128,128]{2,1,0:T(8,128)S(1)}, f32[8,128,128]{2,1,0:T(8,128)S(1)}, f32[8,128,128]{2,1,0:T(8,128)S(1)}, f32[8,128,128]{2,1,0:T(8,128)S(1...) custom-call(s32[4,16]{1,0:T(4,128)S(1)} %bitcast.35, ...), custom_call_target="tpu_custom_call" | custom-call | tf_op jit(solution)/shard_map/second_kernel/pallas_call | solution.py:688
  40.3 11.8 %all_to_all.36 = f32[16,1,3328]{2,1,0:T(1,128)S(1)} all-to-all(f32[16,1,3328]{2,1,0:T(1,128)S(1)} %bitcast.28), channel_id=1, replica_groups=mesh['patch'=16,'sec'=2] {'patch'}, dimensions={0} | all-to-all | bytes 425984 | tf_op jit(solution)/shard_map/all_to_all | solution.py:701
  52.2 4.7 %_lambda_.2 = (f32[8,128,128]{2,1,0:T(8,128)S(1)}, f32[8,128]{1,0:T(8,128)S(1)}, f32[8,128,128]{2,1,0:T(8,128)S(1)}, f32[8,128,128]{2,1,0:T(8,128)S(1)}, f32[32,...) custom-call(s32[4,16]{1,0:T(4,128)S(1)} %bitcast.36, ...), custom_call_target="tpu_custom_call" | custom-call | tf_op jit(solution)/shard_map/<lambda>/pallas_call | solution.py:688
  56.9 9.6 %all_to_all.37 = f32[16,1,1152]{2,1,0:T(1,128)S(1)} all-to-all(f32[16,1,1152]{2,1,0:T(1,128)S(1)} %bitcast.31), channel_id=1, replica_groups=mesh['patch'=16,'sec'=2] {'patch'}, dimensions={0} | all-to-all | bytes 147456 | tf_op jit(solution)/shard_map/all_to_all | solution.py:701
  66.5 3.9 %next_kernel.1 = (f32[8,128,128]{2,1,0:T(8,128)S(1)}, f32[8,128,128]{2,1,0:T(8,128)S(1)}, f32[8,128,128]{2,1,0:T(8,128)S(1)}, f32[8,128,128]{2,1,0:T(8,128)S(1)}...) custom-call(s32[4,16]{1,0:T(4,128)S(1)} %bitcast.37, s32[4,16]{1,0:T(4,128)S(1)} %bitcast.45, ...), custom_call_target="tpu_custom_call" | custom-call | tf_op jit(solution)/shard_map/next_kernel/pallas_call | solution.py:688
  70.4 10.7 %all_to_all.38 = f32[16,1,2176]{2,1,0:T(1,128)S(1)} all-to-all(f32[16,1,2176]{2,1,0:T(1,128)S(1)} %bitcast.29), channel_id=1, replica_groups=mesh['patch'=16,'sec'=2] {'patch'}, dimensions={0} | all-to-all | bytes 278528 | tf_op jit(solution)/shard_map/all_to_all | solution.py:701
  81.1 5.2 %second_kernel.3 = (f32[8,128,128]{2,1,0:T(8,128)}, f32[8,128,128]{2,1,0:T(8,128)S(1)}, f32[8,128,128]{2,1,0:T(8,128)S(1)}, f32[8,128,128]{2,1,0:T(8,128)S(1)}, ...) custom-call(s32[4,16]{1,0:T(4,128)S(1)} %bitcast.38, ...), custom_call_target="tpu_custom_call" | custom-call | tf_op jit(solution)/shard_map/second_kernel/pallas_call | solution.py:688
  86.3 11.8 %all_to_all.39 = f32[16,1,3328]{2,1,0:T(1,128)S(1)} all-to-all(f32[16,1,3328]{2,1,0:T(1,128)S(1)} %bitcast.27), channel_id=1, replica_groups=mesh['patch'=16,'sec'=2] {'patch'}, dimensions={0} | all-to-all | bytes 425984 | tf_op jit(solution)/shard_map/all_to_all | solution.py:701
  98.1 4.8 %_lambda_.3 = (f32[8,128,128]{2,1,0:T(8,128)S(1)}, f32[8,128]{1,0:T(8,128)S(1)}, f32[16,128]{1,0:T(8,128)S(1)}) custom-call(s32[4,16]{1,0:T(4,128)S(1)} %bitcast.39, s32[4,16]{1,0:T(4,128)S(1)} %bitcast.47, s32[4,16]{1,0:T(4,128)S(1)} %bitcast.55, bf16[256,256]{1,0:T(8,128)(2,1)S(1)} %copy-done.1, bf16[256,256]{1,0:T(8,128)(2,1)S(1)} %copy-done, ...), custom_call_target="tpu_custom_call" | custom-call | tf_op jit(solution)/shard_map/<lambda>/pallas_call | solution.py:688
  102.9 9.0 %all_to_all.40 = f32[16,1,128]{2,1,0:T(1,128)S(1)} all-to-all(f32[16,1,128]{2,1,0:T(1,128)S(1)} %bitcast.57), channel_id=1, replica_groups=mesh['patch'=16,'sec'=2] {'patch'}, dimensions={0} | all-to-all | bytes 16384 | tf_op jit(solution)/shard_map/all_to_all | solution.py:701
  111.9 1.1 shard_map.64
Async XLA Ops:
  0.0 3.0 %copy-start.4 = (s32[16,4]{0,1:T(4,128)S(1)}, s32[16,4]{0,1:T(4,128)}, u32[]{:S(2)}) copy-start(s32[16,4]{0,1:T(4,128)} %param.9) | copy-start | bytes 772
  0.0 11.4 %collective-permute-start = (f32[4,128,128]{2,1,0:T(8,128)}, f32[4,128,128]{2,1,0:T(8,128)S(1)}, u32[]{:S(2)}, u32[]{:S(2)}) collective-permute-start(f32[4,128,128]{2,1,0:T(8,128)} %bitcast.58), channel_id=1, source_target_pairs={{1,0},{0,1},{3,2},{2,3},{5,4},{4,5},{7,6},{6,7},{9,8},{8,9},{11,10... | collective-permute-start | bytes 786440 | tf_op jit(solution)/shard_map/ppermute | solution.py:656
  3.0 0.7 copy-start.3
  3.0 0.7 copy-start.2
  3.7 0.9 copy-start.5
  4.6 6.8 %copy-start.6 = (f32[1,4,128,128]{3,2,1,0:T(8,128)S(1)}, f32[1,4,128,128]{3,2,1,0:T(8,128)}, u32[]{:S(2)}) copy-start(f32[1,4,128,128]{3,2,1,0:T(8,128)} %param.6) | copy-start | bytes 786436
  6.5 4.9 %copy-start = (bf16[256,256]{1,0:T(8,128)(2,1)S(1)}, bf16[256,256]{1,0:T(8,128)(2,1)}, u32[]{:S(2)}) copy-start(bf16[256,256]{1,0:T(8,128)(2,1)} %constant.5.clone.refs_4_) | copy-start | bytes 393220
  6.5 4.9 %copy-start.1 = (bf16[256,256]{1,0:T(8,128)(2,1)S(1)}, bf16[256,256]{1,0:T(8,128)(2,1)}, u32[]{:S(2)}) copy-start(bf16[256,256]{1,0:T(8,128)(2,1)} %constant.4.clone.refs_3_) | copy-start | bytes 393220
  6.5 14.8 %all-to-all-start = ((f32[32,1,1664]{2,1,0:T(1,128)}), f32[32,1,1664]{2,1,0:T(1,128)S(1)}, u32[]{:S(2)}, u32[]{:S(2)}) async-start(f32[32,1,1664]{2,1,0:T(1,128)} %bitcast.4), calls=%async_computation | async-start | bytes 425984 | tf_op jit(solution)/shard_map/all_to_all | solution.py:701

commit v4 on v3

--- a/solution.py
+++ b/solution.py
@@ -59,6 +59,13 @@
         hit = distance == offset
         out = jnp.where(hit if inside is None else hit & inside, value, out)
     return out
+
+
+def face_weights():
+    mass, stiff = band_matrix(MASS_BAND, 16), band_matrix(STIFF_BAND, 16)
+    mass, stiff = mass.astype(np.float64), stiff.astype(np.float64)
+    pairs = ((stiff, stiff), (stiff, mass), (mass, stiff), (mass, mass))
+    return [[float(x) for x in (a @ b)[0, :7]] for a, b in pairs]
 
 
 class Body:
@@ -150,24 +157,26 @@
     def strips(self, field, count=4):
         depth = field.shape[0]
         group = min(depth, 8)
+        half = 8 if count > 4 else 4
+        width, bits = 2 * half, (half * 2).bit_length() - 1
         rows0 = [field[:, d, :] for d in range(count)]
         rows1 = [field[:, LANES - 1 - d, :] for d in range(count)]
-        wanted = list(range(4 - count, 4 + count))
+        wanted = list(range(half - count, half + count))
         pieces = {i: [] for i in wanted}
         for start in range(0, depth, group):
             stacked = jnp.zeros((LANES, LANES), jnp.float32)
             for j in range(group):
-                rolled = pltpu.roll(field[start + j], (8 * j + 4) % LANES, 1)
-                stacked = jnp.where((self.wide >> 3) == j, rolled, stacked)
+                rolled = pltpu.roll(field[start + j], (width * j + half) % LANES, 1)
+                stacked = jnp.where((self.wide >> bits) == j, rolled, stacked)
             self.strip[...] = jnp.transpose(stacked)
             for i in wanted:
-                pieces[i].append(self.strip[pl.ds(i, group, stride=8), :])
+                pieces[i].append(self.strip[pl.ds(i, group, stride=width), :])
         columns = {i: jnp.concatenate(p, axis=0) if len(p) > 1 else p[0] for i, p in pieces.items()}
         return [
             rows0,
             rows1,
-            [columns[4 + d] for d in range(count)],
-            [columns[3 - d] for d in range(count)],
+            [columns[half + d] for d in range(count)],
+            [columns[half - 1 - d] for d in range(count)],
         ]
 
     def traces(self, field):
@@ -203,21 +212,37 @@
             out.append(inner[f] + jump[f] + self.ends(*ends))
         return out
 
-    def slab(self, stiffs, masses, plain=None):
+    def slabs_of(self, sets):
         n = 4 * self.depth
-        rows = [stack(masses), stack(stiffs)] + ([] if plain is None else [stack(plain)])
+        rows = [stack(values) for values in sum(sets, ())]
         both = dot(stack(rows), self.plain)
-        lower = both[n : 2 * n, :LANES] + both[:n, LANES:]
-        if plain is not None:
-            lower = lower + both[2 * n :, :LANES]
-        out = dot(self.third, stack([lower, both[:n, :LANES]]))
-        return unstack(out, self.depth)
+        at, uppers, lowers = 0, [], []
+        for values in sets:
+            masses, stiffs = both[at + n : at + 2 * n], both[at : at + n, :LANES]
+            lower = stiffs + masses[:, LANES:]
+            if len(values) == 3:
+                lower = lower + both[at + 2 * n : at + 3 * n, :LANES]
+            uppers.append(lower)
+            lowers.append(masses[:, :LANES])
+            at += n * len(values)
+        if len(sets) > 1:
+            uppers, lowers = [jnp.concatenate(x, axis=1) for x in (uppers, lowers)]
+        else:
+            uppers, lowers = uppers[0], lowers[0]
+        out = dot(self.third, stack([uppers, lowers]))
+        return [unstack(out[:, k * LANES : (k + 1) * LANES], self.depth) for k in range(len(sets))]
+
+    def slab(self, *lists):
+        return self.slabs_of([lists])[0]
 
     def depth_sum(self, strip, band):
         out = band[0] * strip[0]
-        for d in (1, 2, 3):
+        for d in range(1, len(band)):
             out = out + band[d] * strip[d]
         return out
+
+    def depth_sums(self, strips, band):
+        return [self.depth_sum(strip, band) for strip in strips]
 
     def corner_table(self, trace, inner=None):
         table = jnp.zeros((self.depth, LANES), jnp.float32)
@@ -375,7 +400,7 @@
     body.send(payload, [trace, inner], body.pack(table, NARROW))
 
 
-def flux_tail(body, current, mine, other, r0, v1, m1, tr, tv, payload, potential):
+def flux_tail(body, mine, other, r0, tr, tv, payload, potential):
     jump = body.jumps(mine, other)
     body.stand(jump)
 
@@ -384,16 +409,22 @@
 
     body.stiff0(lambda z: potential[z], residual)
     body.add_rows(r0, jump, -TIME_STEP)
-
-    def image(z, stiff, mass):
-        v1[z] = stiff
-        m1[z] = mass
-
-    body.stiff0(lambda z: r0[z], image)
-    trace, inner = body.traces(r0), body.traces(v1)
+    strips = body.strips(r0)
+    trace = [s[0] for s in strips]
+    inner = body.slab(body.depth_sums(strips, STIFF_BAND), body.depth_sums(strips, MASS_BAND))
     tr[...], tv[...] = stack(trace), stack(inner)
     body.copies = 1
     body.send(payload, [trace, inner], body.pack(body.corner_table(trace), NARROW))
+
+
+def image_kernel(sizes, field, v, m, *refs):
+    body = Body(sizes, refs)
+
+    def image(z, stiff, mass):
+        v[z] = stiff
+        m[z] = mass
+
+    body.stiff0(lambda z: field[z], image)
 
 
 def middle_kernel(sizes, *refs):
@@ -412,7 +443,7 @@
     tc[...], tv[...] = stack(body.traces(c)), stack(body.traces(v0))
 
 
-def first_kernel(sizes, c, v0, tc, tv0, recv, sc, r0, v1, m1, ts, tr, tv, sides, payload,
+def first_kernel(sizes, c, v0, tc, tv0, recv, sc, r0, ts, tr, tv, sides, payload,
                  potential, *refs):
     body = Body(sizes, refs, sizes[2])
     depth, count = body.depth, body.slabs
@@ -438,10 +469,10 @@
     sides[0], sides[1] = stack(other), stack(other_s)
     mine_p = [cubic(x, s) for x, s in zip(mine, mine_s)]
     other_p = [cubic(x, s) for x, s in zip(other, other_s)]
-    flux_tail(body, c, mine_p, other_p, r0, v1, m1, tr, tv, payload, potential)
-
-
-def second_kernel(sizes, r0, v1, m1, tr, tv, recv, u1, y, v2, m2, ty, tv2, tu, sides, payload,
+    flux_tail(body, mine_p, other_p, r0, tr, tv, payload, potential)
+
+
+def second_kernel(sizes, r0, v1, m1, tr, tv, recv, u1, y, ty, tv2, tu, sides, payload,
                   *refs):
     body = Body(sizes, refs)
     depth = body.depth
@@ -467,23 +498,19 @@
     body.stiff0(lambda z: u1[z], image)
     body.add_rows(y, jump, HALF)
     sums = [[], [], []]
-
-    def again(z, stiff, mass):
-        v2[z] = stiff
-        m2[z] = mass
+    for z in range(depth):
         a, b = r0[z], y[z]
         for i, product in enumerate((a * a, a * b, b * b)):
             sums[i].append(jnp.sum(product, axis=0, keepdims=True))
-
-    body.stiff0(lambda z: y[z], again)
-    strips_y, strips = body.strips(y), body.strips(v2)
-    trace, inner = [s[0] for s in strips_y], [s[0] for s in strips]
+    strips = body.strips(y, 7)
+    trace = [s[0] for s in strips]
+    masses = body.depth_sums(strips, MASS_BAND)
+    kk, km, mk, mm = [body.depth_sums(strips, band) for band in face_weights()]
+    inner, ahead, across = body.slabs_of(
+        [(body.depth_sums(strips, STIFF_BAND), masses), (kk, km), (mk, mm)]
+    )
     ty[...], tv2[...] = stack(trace), stack(inner)
-    mixed = body.slab(
-        [HALF * body.depth_sum(s, STIFF_BAND) for s in strips],
-        [HALF * body.depth_sum(s, MASS_BAND) for s in strips],
-        [body.depth_sum(s, MASS_BAND) for s in strips_y],
-    )
+    mixed = body.slab([HALF * a for a in ahead], [HALF * a for a in across], masses)
     outer = [TWICE * a + b for a, b in zip(inner, mixed)]
     table = body.corner_table(trace, inner)
     for i in range(3):
@@ -615,7 +642,7 @@
 
 def next_kernel(sizes, c, r0, y, t, sc, u1, u2, zf, tc, ts, tr, tu, ty, tu2, tt, tz,
                 side_c, side_r, side_y, base, recv,
-                cn, rn, v1, m1, trn, tvn, payload, potential, *refs):
+                cn, rn, trn, tvn, payload, potential, *refs):
     body = Body(sizes, refs)
     depth = body.depth
     x = weights(body.patches, base, recv)
@@ -634,8 +661,7 @@
         mix(side_c[0], side_r[0], side_y[0], side_y[2]),
         mix(side_c[1], side_r[1], side_y[1], stack(side_z)),
     )
-    flux_tail(body, cn, unstack(mine, depth), unstack(other, depth),
-              rn, v1, m1, trn, tvn, payload, potential)
+    flux_tail(body, unstack(mine, depth), unstack(other, depth), rn, trn, tvn, payload, potential)
 
 
 def last_kernel(patches, c, r0, y, t, base, recv, out):
@@ -701,32 +727,35 @@
         moved = lax.all_to_all(payload.reshape(parts, 1, rows * LANES), axes, 0, 0)
         return moved.reshape(parts * rows, LANES)
 
+    cost = pl.CostEstimate(flops=COST, bytes_accessed=4 * own.size, transcendentals=0)
     narrow, broad = depth * NARROW // LANES, depth * BROAD // LANES
     (payload,) = call(
         start_kernel,
         [load(slabs * (rows + depth + narrow))],
         own,
         consts=[],
-        cost=pl.CostEstimate(flops=COST, bytes_accessed=4 * own.size, transcendentals=0),
+        cost=cost,
     )
     c, v0, tc, tv0 = call(
         middle_kernel,
         [field, field, trace, trace],
         *halves,
-        cost=pl.CostEstimate(flops=COST, bytes_accessed=4 * own.size, transcendentals=0),
-    )
-    sc, r0, v1, m1, ts, tr, tv, side_c, payload = call(
+        cost=cost,
+    )
+    sc, r0, ts, tr, tv, side_c, payload = call(
         first_kernel,
-        [field] * 4 + [trace] * 3 + [sides(2), load(2 * depth + narrow)],
+        [field] * 2 + [trace] * 3 + [sides(2), load(2 * depth + narrow)],
         c, v0, tc, tv0, swap(payload, ("patch", "sec"), patches * slabs),
         fields=1,
     )
     for step in range(STEPS):
-        u1, y, v2, m2, ty, tv2, tu, side_r, payload = call(
+        v1, m1 = call(image_kernel, [field] * 2, r0, cost=cost)
+        u1, y, ty, tv2, tu, side_r, payload = call(
             second_kernel,
-            [field] * 4 + [trace] * 3 + [sides(2), load(3 * depth + broad)],
+            [field] * 2 + [trace] * 3 + [sides(2), load(3 * depth + broad)],
             r0, v1, m1, tr, tv, swap(payload),
         )
+        v2, m2 = call(image_kernel, [field] * 2, y, cost=cost)
         last = step + 1 == STEPS
         outs = [field, base]
         if last:
@@ -743,9 +772,9 @@
             (payload,) = rest
             break
         u2, zf, tt, tu2, tz, side_y, payload = rest
-        c, r0, v1, m1, tr, tv, payload = call(
+        c, r0, tr, tv, payload = call(
             next_kernel,
-            [field] * 4 + [trace] * 2 + [load(2 * depth + narrow)],
+            [field] * 2 + [trace] * 2 + [load(2 * depth + narrow)],
             c, r0, y, t, sc, u1, u2, zf, tc, ts, tr, tu, ty, tu2, tt, tz,
             side_c, side_r, side_y, base_now, swap(payload),
             fields=1,

time: 113 us -> 124 us (1.097)
  blocking collectives: 63.6 us -> 18.6 us
  waiting for transfers between devices: 7.83 us -> 30.8 us
  starting transfers between devices: 7.86 us -> 22.3 us
  local copies, waits for them, and re-layouts: 1.66 us -> 12.4 us
  Pallas kernels: 31.9 us -> 39.1 us
    all_to_all x6 -> x2, blocking collectives: 63.6 us -> 18.6 us  [swap(): moved = lax.all_to_all(payload.reshape(parts, 1, rows * LANES), axes, 0, 0)]
    all_to_all x1 -> x5, waiting for transfers between devices: 7.83 us -> 30.8 us  [swap(): moved = lax.all_to_all(payload.reshape(parts, 1, rows * LANES), axes, 0, 0)]
    all_to_all x1 -> x5, starting transfers between devices: 4.89 us -> 19.4 us  [swap(): moved = lax.all_to_all(payload.reshape(parts, 1, rows * LANES), axes, 0, 0)]
    unnamed x14 -> x46, local copies, waits for them, and re-layouts: 1.66 us -> 12.4 us
    pallas_call x8 -> x12, Pallas kernels: 30.9 us -> 38 us  [call(): pl.pallas_call(run, out_shape=outs, in_specs=[smem] * 3 + [vmem] * (len(c...]
  transfers between devices with their start and end apart: 2 -> 6, of which waited for: 1 -> 5; matrix products, arithmetic and copies ran while one was open for 0% -> 0% of each run, Pallas kernels for 3% -> 10%
where the time goes in v4:
time: 124 us; the launch traced here: 123 us
  Pallas kernels  39.1 us (32%)
  waiting for transfers between devices  30.8 us (25%)
  starting transfers between devices  22.3 us (18%)
  blocking collectives  18.6 us (15%)
  local copies, waits for them, and re-layouts  12.4 us (10%)
    pallas_call x12, Pallas kernels, call(): pl.pallas_call(run, out_shape=outs, in_specs=[smem] * 3 + [vmem] * (len(c...  38 us
    all_to_all x5, waiting for transfers between devices, swap(): moved = lax.all_to_all(payload.reshape(parts, 1, rows * LANES), axes, 0, 0)  30.8 us
    all_to_all x5, starting transfers between devices, swap(): moved = lax.all_to_all(payload.reshape(parts, 1, rows * LANES), axes, 0, 0)  19.4 us
    all_to_all x2, blocking collectives, swap(): moved = lax.all_to_all(payload.reshape(parts, 1, rows * LANES), axes, 0, 0)  18.6 us
    unnamed x46, local copies, waits for them, and re-layouts  12.4 us
    ppermute x1, starting transfers between devices, shards(): lax.ppermute(own, 'sec', [((i + k) % slabs, i) for i in range(slabs)])  2.97 us
  transfers between devices with their start and end apart: 6, of which 5 were waited for; matrix products, arithmetic and copies ran while one was open for 0% of the time, Pallas kernels for 10%

profile of v4, /device:TPU:0, one launch (start us, length us, event | category | flops | bytes accessed | tf_op | source)
XLA Modules:
  0.0 123.3 jit_solution(16681767803799758383)
XLA Ops:
  0.0 3.0 %collective-permute-start = (f32[4,128,128]{2,1,0:T(8,128)}, f32[4,128,128]{2,1,0:T(8,128)S(1)}, u32[]{:S(2)}, u32[]{:S(2)}) collective-permute-start(f32[4,128,128]{2,1,0:T(8,128)} %bitcast.66), channel_id=1, source_target_pairs={{1,0},{0,1},{3,2},{2,3},{5,4},{4,5},{7,6},{6,7},{9,8},{8,9},{11,10... | collective-permute-start | bytes 786440 | tf_op jit(solution)/shard_map/ppermute | solution.py:682
  3.0 0.0 copy-done.14
  3.0 0.7 copy-done.13
  3.7 0.0 copy-done.12
  3.7 0.9 copy-done.21
  4.6 1.9 %start_kernel.1 = f32[416,128]{1,0:T(8,128)} custom-call(s32[4,16]{1,0:T(4,128)S(1)} %bitcast.28, s32[4,16]{1,0:T(4,128)S(1)} %bitcast.40, s32[4,16]{1,0:T(4,128)S(1)} %bitcast.52, f32[4,128,128]{2,1,0:T(8,128)S(1)} %bitcast.67), custom_call_target="tpu_custom_call" | custom-call | flops 17179869184 | bytes 262144 | tf_op jit(solution)/shard_map/start_kernel/pallas_call | solution.py:714
  6.5 4.9 %all-to-all-start = ((f32[32,1,1664]{2,1,0:T(1,128)}), f32[32,1,1664]{2,1,0:T(1,128)S(1)}, u32[]{:S(2)}, u32[]{:S(2)}) async-start(f32[32,1,1664]{2,1,0:T(1,128)} %bitcast.4), calls=%async_computation | async-start | bytes 425984 | tf_op jit(solution)/shard_map/all_to_all | solution.py:727
  11.4 0.0 collective-permute-done.refs_6_
  11.4 0.0 copy-done.22
  11.4 0.0 copy-done
  11.4 0.0 copy-done.1
  11.4 2.0 %middle_kernel.1 = (f32[8,128,128]{2,1,0:T(8,128)S(1)}, f32[8,128,128]{2,1,0:T(8,128)S(1)}, f32[32,128]{1,0:T(8,128)S(1)}, f32[32,128]{1,0:T(8,128)S(1)}) custom-call(s32[4,16]{1,0:T(4,128)S(1)} %bitcast.29, s32[4,16]{1,0:T(4,128)S(1)} %bitcast.41, s32[4,16]{1,0:T(4,128)S(1)} %bitcast.53, bf16[256,256]{1,0:T(8,128)(2,1)S(1)} %copy-done.1, ...), custom_call_target="tpu_custom_call" | custom-call | flops 17179869184 | bytes 262144 | tf_op jit(solution)/shard_map/middle_kernel/pallas_call | solution.py:714
  13.5 7.8 %all-to-all-done = f32[32,1,1664]{2,1,0:T(1,128)S(1)} async-done(((f32[32,1,1664]{2,1,0:T(1,128)}), f32[32,1,1664]{2,1,0:T(1,128)S(1)}, u32[]{:S(2)}, u32[]{:S(2)}) %all-to-all-start) | async-done | bytes 213024 | tf_op jit(solution)/shard_map/all_to_all | solution.py:727
  21.3 3.6 %first_kernel.1 = (f32[8,128,128]{2,1,0:T(8,128)S(1)}, f32[8,128,128]{2,1,0:T(8,128)S(1)}, f32[32,128]{1,0:T(8,128)S(1)}, f32[32,128]{1,0:T(8,128)S(1)}, f32[32,...) custom-call(s32[4,16]{1,0:T(4,128)S(1)} %bitcast.30, s32[4,16]{1,0:T(4,128)S(1)} %bitcast.42, ...), custom_call_target="tpu_custom_call" | custom-call | tf_op jit(solution)/shard_map/first_kernel/pallas_call | solution.py:714
  25.0 3.5 %all-to-all-start.1 = ((f32[16,1,2176]{2,1,0:T(1,128)}), f32[16,1,2176]{2,1,0:T(1,128)S(1)}, u32[]{:S(2)}, u32[]{:S(2)}) async-start(f32[16,1,2176]{2,1,0:T(1,128)} %bitcast.6), calls=%async_computation.1 | async-start | bytes 278528 | tf_op jit(solution)/shard_map/all_to_all | solution.py:727
  28.5 2.0 %image_kernel.4 = (f32[8,128,128]{2,1,0:T(8,128)S(1)}, f32[8,128,128]{2,1,0:T(8,128)S(1)}) custom-call(s32[4,16]{1,0:T(4,128)S(1)} %bitcast.31, s32[4,16]{1,0:T(4,128)S(1)} %bitcast.43, s32[4,16]{1,0:T(4,128)S(1)} %bitcast.55, bf16[256,256]{1,0:T(8,128)(2,1)S(1)} %copy-done.1, bf16[256,256]{1,0:T(8,128)(2,1)S(1)} %copy-done, ...), custom_call_target="tpu_custom_call" | custom-call | flops 17179869184 | bytes 262144 | tf_op jit(solution)/shard_map/image_kernel/pallas_call | solution.py:714
  30.4 0.0 copy-start.2
  30.5 0.8 copy-done.2
  31.2 0.8 copy-done.4
  32.1 4.4 %all-to-all-done.1 = f32[16,1,2176]{2,1,0:T(1,128)S(1)} async-done(((f32[16,1,2176]{2,1,0:T(1,128)}), f32[16,1,2176]{2,1,0:T(1,128)S(1)}, u32[]{:S(2)}, u32[]{:S(2)}) %all-to-all-start.1) | async-done | bytes 139296 | tf_op jit(solution)/shard_map/all_to_all | solution.py:727
  36.5 1.0 copy-done.3
  37.5 1.0 copy-done.5
  38.6 4.7 %second_kernel.2 = (f32[8,128,128]{2,1,0:T(8,128)S(1)}, f32[8,128,128]{2,1,0:T(8,128)S(1)}, f32[32,128]{1,0:T(8,128)S(1)}, f32[32,128]{1,0:T(8,128)S(1)}, f32[32...) custom-call(s32[4,16]{1,0:T(4,128)S(1)} %bitcast.32, s32[4,16]{1,0:T(4,128)S(1)} %bitcast.44, ...), custom_call_target="tpu_custom_call" | custom-call | tf_op jit(solution)/shard_map/second_kernel/pallas_call | solution.py:714
  43.3 0.6 copy-done.15
  43.9 3.7 %all-to-all-start.2 = ((f32[16,1,3328]{2,1,0:T(1,128)}), f32[16,1,3328]{2,1,0:T(1,128)S(1)}, u32[]{:S(2)}, u32[]{:S(2)}) async-start(f32[16,1,3328]{2,1,0:T(1,128)} %bitcast.8), calls=%async_computation.2 | async-start | bytes 425984 | tf_op jit(solution)/shard_map/all_to_all | solution.py:727
  47.6 2.0 %image_kernel.5 = (f32[8,128,128]{2,1,0:T(8,128)S(1)}, f32[8,128,128]{2,1,0:T(8,128)S(1)}) custom-call(s32[4,16]{1,0:T(4,128)S(1)} %bitcast.33, s32[4,16]{1,0:T(4,128)S(1)} %bitcast.45, s32[4,16]{1,0:T(4,128)S(1)} %bitcast.57, bf16[256,256]{1,0:T(8,128)(2,1)S(1)} %copy-done.1, bf16[256,256]{1,0:T(8,128)(2,1)S(1)} %copy-done, ...), custom_call_target="tpu_custom_call" | custom-call | flops 17179869184 | bytes 262144 | tf_op jit(solution)/shard_map/image_kernel/pallas_call | solution.py:714
  49.6 0.8 copy-done.8
  50.4 0.8 copy-done.10
  51.2 5.5 %all-to-all-done.2 = f32[16,1,3328]{2,1,0:T(1,128)S(1)} async-done(((f32[16,1,3328]{2,1,0:T(1,128)}), f32[16,1,3328]{2,1,0:T(1,128)S(1)}, u32[]{:S(2)}, u32[]{:S(2)}) %all-to-all-start.2) | async-done | bytes 213024 | tf_op jit(solution)/shard_map/all_to_all | solution.py:727
  56.6 1.0 copy-done.9
  57.7 1.0 copy-done.11
  58.7 4.8 %_lambda_.2 = (f32[8,128,128]{2,1,0:T(8,128)S(1)}, f32[8,128]{1,0:T(8,128)S(1)}, f32[8,128,128]{2,1,0:T(8,128)S(1)}, f32[8,128,128]{2,1,0:T(8,128)S(1)}, f32[32,...) custom-call(s32[4,16]{1,0:T(4,128)S(1)} %bitcast.34, ...), custom_call_target="tpu_custom_call" | custom-call | tf_op jit(solution)/shard_map/<lambda>/pallas_call | solution.py:714
  63.6 9.6 %all_to_all.35 = f32[16,1,1152]{2,1,0:T(1,128)S(1)} all-to-all(f32[16,1,1152]{2,1,0:T(1,128)S(1)} %bitcast.27), channel_id=1, replica_groups=mesh['patch'=16,'sec'=2] {'patch'}, dimensions={0} | all-to-all | bytes 147456 | tf_op jit(solution)/shard_map/all_to_all | solution.py:727
  73.2 0.7 copy-done.16
  73.9 3.7 %next_kernel.1 = (f32[8,128,128]{2,1,0:T(8,128)S(1)}, f32[8,128,128]{2,1,0:T(8,128)S(1)}, f32[32,128]{1,0:T(8,128)S(1)}, f32[32,128]{1,0:T(8,128)S(1)}, f32[272,128]{1,0:T(8,128)}) custom-call(s32[4,16]{1,0:T(4,128)S(1)} %bitcast.35, s32[4,16]{1,0:T(4,128)S(1)} %bitcast.47, s32[4,16]{1,0:T(4,128)S(1)} %bitcast.59, bf16[256,256]{1,0:T(8,128)(2,1)S(1)} %copy-done.1, ...), custom_call_target="tpu_custom_call" | custom-call | tf_op jit(solution)/shard_map/next_kernel/pallas_call | solution.py:714
  77.6 0.8 copy-done.6
  78.4 0.6 copy-done.17
  79.0 0.6 copy-done.19
  79.6 3.5 %all-to-all-start.4 = ((f32[16,1,2176]{2,1,0:T(1,128)}), f32[16,1,2176]{2,1,0:T(1,128)S(1)}, u32[]{:S(2)}, u32[]{:S(2)}) async-start(f32[16,1,2176]{2,1,0:T(1,128)} %bitcast.12), calls=%async_computation.4 | async-start | bytes 278528 | tf_op jit(solution)/shard_map/all_to_all | solution.py:727
  83.1 2.0 %image_kernel.6 = (f32[8,128,128]{2,1,0:T(8,128)S(1)}, f32[8,128,128]{2,1,0:T(8,128)S(1)}) custom-call(s32[4,16]{1,0:T(4,128)S(1)} %bitcast.36, s32[4,16]{1,0:T(4,128)S(1)} %bitcast.48, s32[4,16]{1,0:T(4,128)S(1)} %bitcast.60, bf16[256,256]{1,0:T(8,128)(2,1)S(1)} %copy-done.1, bf16[256,256]{1,0:T(8,128)(2,1)S(1)} %copy-done, ...), custom_call_target="tpu_custom_call" | custom-call | flops 17179869184 | bytes 262144 | tf_op jit(solution)/shard_map/image_kernel/pallas_call | solution.py:714
  85.1 6.0 %all-to-all-done.4 = f32[16,1,2176]{2,1,0:T(1,128)S(1)} async-done(((f32[16,1,2176]{2,1,0:T(1,128)}), f32[16,1,2176]{2,1,0:T(1,128)S(1)}, u32[]{:S(2)}, u32[]{:S(2)}) %all-to-all-start.4) | async-done | bytes 139296 | tf_op jit(solution)/shard_map/all_to_all | solution.py:727
  91.1 4.7 %second_kernel.3 = (f32[8,128,128]{2,1,0:T(8,128)}, f32[8,128,128]{2,1,0:T(8,128)S(1)}, f32[32,128]{1,0:T(8,128)S(1)}, f32[32,128]{1,0:T(8,128)S(1)}, f32[32,128...) custom-call(s32[4,16]{1,0:T(4,128)S(1)} %bitcast.37, s32[4,16]{1,0:T(4,128)S(1)} %bitcast.49, ...), custom_call_target="tpu_custom_call" | custom-call | tf_op jit(solution)/shard_map/second_kernel/pallas_call | solution.py:714
  95.9 3.7 %all-to-all-start.5 = ((f32[16,1,3328]{2,1,0:T(1,128)}), f32[16,1,3328]{2,1,0:T(1,128)S(1)}, u32[]{:S(2)}, u32[]{:S(2)}) async-start(f32[16,1,3328]{2,1,0:T(1,128)} %bitcast.14), calls=%async_computation.5 | async-start | bytes 425984 | tf_op jit(solution)/shard_map/all_to_all | solution.py:727
  99.6 2.0 %image_kernel.7 = (f32[8,128,128]{2,1,0:T(8,128)S(1)}, f32[8,128,128]{2,1,0:T(8,128)S(1)}) custom-call(s32[4,16]{1,0:T(4,128)S(1)} %bitcast.38, s32[4,16]{1,0:T(4,128)S(1)} %bitcast.50, s32[4,16]{1,0:T(4,128)S(1)} %bitcast.62, bf16[256,256]{1,0:T(8,128)(2,1)S(1)} %copy-done.1, bf16[256,256]{1,0:T(8,128)(2,1)S(1)} %copy-done, ...), custom_call_target="tpu_custom_call" | custom-call | flops 17179869184 | bytes 262144 | tf_op jit(solution)/shard_map/image_kernel/pallas_call | solution.py:714
  101.6 7.0 %all-to-all-done.5 = f32[16,1,3328]{2,1,0:T(1,128)S(1)} async-done(((f32[16,1,3328]{2,1,0:T(1,128)}), f32[16,1,3328]{2,1,0:T(1,128)S(1)}, u32[]{:S(2)}, u32[]{:S(2)}) %all-to-all-start.5) | async-done | bytes 213024 | tf_op jit(solution)/shard_map/all_to_all | solution.py:727
  108.6 4.7 %_lambda_.3 = (f32[8,128,128]{2,1,0:T(8,128)S(1)}, f32[8,128]{1,0:T(8,128)S(1)}, f32[16,128]{1,0:T(8,128)S(1)}) custom-call(s32[4,16]{1,0:T(4,128)S(1)} %bitcast.39, s32[4,16]{1,0:T(4,128)S(1)} %bitcast.51, s32[4,16]{1,0:T(4,128)S(1)} %bitcast.63, bf16[256,256]{1,0:T(8,128)(2,1)S(1)} %copy-done.1, bf16[256,256]{1,0:T(8,128)(2,1)S(1)} %copy-done, ...), custom_call_target="tpu_custom_call" | custom-call | tf_op jit(solution)/shard_map/<lambda>/pallas_call | solution.py:714
  113.3 9.0 %all_to_all.36 = f32[16,1,128]{2,1,0:T(1,128)S(1)} all-to-all(f32[16,1,128]{2,1,0:T(1,128)S(1)} %bitcast.65), channel_id=1, replica_groups=mesh['patch'=16,'sec'=2] {'patch'}, dimensions={0} | all-to-all | bytes 16384 | tf_op jit(solution)/shard_map/all_to_all | solution.py:727
  122.3 1.1 shard_map.64
  (25 shorter events, 0.0 us)
Async XLA Ops:
  0.0 3.0 %copy-start.14 = (s32[16,4]{0,1:T(4,128)S(1)}, s32[16,4]{0,1:T(4,128)}, u32[]{:S(2)}) copy-start(s32[16,4]{0,1:T(4,128)} %param.9) | copy-start | bytes 772
  0.0 11.4 %collective-permute-start = (f32[4,128,128]{2,1,0:T(8,128)}, f32[4,128,128]{2,1,0:T(8,128)S(1)}, u32[]{:S(2)}, u32[]{:S(2)}) collective-permute-start(f32[4,128,128]{2,1,0:T(8,128)} %bitcast.66), channel_id=1, source_target_pairs={{1,0},{0,1},{3,2},{2,3},{5,4},{4,5},{7,6},{6,7},{9,8},{8,9},{11,10... | collective-permute-start | bytes 786440 | tf_op jit(solution)/shard_map/ppermute | solution.py:682
  3.0 0.7 copy-start.13
  3.0 0.7 copy-start.12
  3.7 0.9 copy-start.21
  4.6 6.8 %copy-start.22 = (f32[1,4,128,128]{3,2,1,0:T(8,128)S(1)}, f32[1,4,128,128]{3,2,1,0:T(8,128)}, u32[]{:S(2)}) copy-start(f32[1,4,128,128]{3,2,1,0:T(8,128)} %param.6) | copy-start | bytes 786436
  6.5 4.9 %copy-start = (bf16[256,256]{1,0:T(8,128)(2,1)S(1)}, bf16[256,256]{1,0:T(8,128)(2,1)}, u32[]{:S(2)}) copy-start(bf16[256,256]{1,0:T(8,128)(2,1)} %constant.5.clone.refs_4_) | copy-start | bytes 393220
  6.5 4.9 %copy-start.1 = (bf16[256,256]{1,0:T(8,128)(2,1)S(1)}, bf16[256,256]{1,0:T(8,128)(2,1)}, u32[]{:S(2)}) copy-start(bf16[256,256]{1,0:T(8,128)(2,1)} %constant.4.clone.refs_3_) | copy-start | bytes 393220
  6.5 14.8 %all-to-all-start = ((f32[32,1,1664]{2,1,0:T(1,128)}), f32[32,1,1664]{2,1,0:T(1,128)S(1)}, u32[]{:S(2)}, u32[]{:S(2)}) async-start(f32[32,1,1664]{2,1,0:T(1,128)} %bitcast.4), calls=%async_computation | async-start | bytes 425984 | tf_op jit(solution)/shard_map/all_to_all | solution.py:727
  25.0 11.6 %all-to-all-start.1 = ((f32[16,1,2176]{2,1,0:T(1,128)}), f32[16,1,2176]{2,1,0:T(1,128)S(1)}, u32[]{:S(2)}, u32[]{:S(2)}) async-start(f32[16,1,2176]{2,1,0:T(1,128)} %bitcast.6), calls=%async_computation.1 | async-start | bytes 278528 | tf_op jit(solution)/shard_map/all_to_all | solution.py:727
  30.4 0.8 copy-start.2
  31.2 0.8 copy-start.4
  36.5 1.0 copy-start.3
  37.5 1.0 copy-start.5
  43.3 0.6 copy-start.15
  43.9 12.7 %all-to-all-start.2 = ((f32[16,1,3328]{2,1,0:T(1,128)}), f32[16,1,3328]{2,1,0:T(1,128)S(1)}, u32[]{:S(2)}, u32[]{:S(2)}) async-start(f32[16,1,3328]{2,1,0:T(1,128)} %bitcast.8), calls=%async_computation.2 | async-start | bytes 425984 | tf_op jit(solution)/shard_map/all_to_all | solution.py:727
  49.6 0.8 copy-start.8
  50.4 0.8 copy-start.10
  56.6 1.0 copy-start.9
  57.7 1.0 copy-start.11
  73.2 0.7 copy-start.16
  77.6 0.8 copy-start.6
  78.4 0.6 copy-start.17
  79.0 0.6 copy-start.19
  79.6 11.6 %all-to-all-start.4 = ((f32[16,1,2176]{2,1,0:T(1,128)}), f32[16,1,2176]{2,1,0:T(1,128)S(1)}, u32[]{:S(2)}, u32[]{:S(2)}) async-start(f32[16,1,2176]{2,1,0:T(1,128)} %bitcast.12), calls=%async_computation.4 | async-start | bytes 278528 | tf_op jit(solution)/shard_map/all_to_all | solution.py:727
  83.1 8.0 %copy-start.18 = (f32[32,128]{1,0:T(8,128)S(1)}, f32[32,128]{1,0:T(8,128)}, u32[]{:S(2)}) copy-start(f32[32,128]{1,0:T(8,128)} %copy-done.17) | copy-start | bytes 49156
  83.1 8.0 %copy-start.20 = (f32[32,128]{1,0:T(8,128)S(1)}, f32[32,128]{1,0:T(8,128)}, u32[]{:S(2)}) copy-start(f32[32,128]{1,0:T(8,128)} %copy-done.19) | copy-start | bytes 49156
  95.9 12.7 %all-to-all-start.5 = ((f32[16,1,3328]{2,1,0:T(1,128)}), f32[16,1,3328]{2,1,0:T(1,128)S(1)}, u32[]{:S(2)}, u32[]{:S(2)}) async-start(f32[16,1,3328]{2,1,0:T(1,128)} %bitcast.14), calls=%async_computation.5 | async-start | bytes 425984 | tf_op jit(solution)/shard_map/all_to_all | solution.py:727
  108.6 13.7 %copy-start.7 = (f32[8,128,128]{2,1,0:T(8,128)S(1)}, f32[8,128,128]{2,1,0:T(8,128)}, u32[]{:S(2)}) copy-start(f32[8,128,128]{2,1,0:T(8,128)} %copy-done.6) | copy-start | bytes 1572868

commit v5 on v3

--- a/solution.py
+++ b/solution.py
@@ -50,7 +50,7 @@
 def constants():
     high = right_matrix(MASS_HIGH, STIFF_HIGH).astype(jnp.bfloat16)
     low = right_matrix(MASS_LOW, STIFF_LOW).astype(jnp.bfloat16)
-    return high, low
+    return (np.concatenate([high, high, high, low, low]),)
 
 
 def banded(distance, band, inside=None):
@@ -68,7 +68,7 @@
         self.tables, refs = refs[:3], refs[3:]
         self.near, self.strip, self.turned, self.stood = refs[-4:]
         if len(refs) > 4:
-            self.high, self.low = refs[:2]
+            self.pieces = refs[0]
         self.me = lax.axis_index("patch")
         self.lane = lax.broadcasted_iota(jnp.int32, (self.depth, LANES), 1)
         self.first, self.last = self.lane == 0, self.lane == LANES - 1
@@ -79,19 +79,6 @@
         distance = jnp.abs(row - self.wide)
         self.plain = jnp.concatenate(
             [banded(distance, MASS_BAND), banded(distance, STIFF_BAND)], axis=1
-        )
-        n = 4 * self.depth
-        row = lax.broadcasted_iota(jnp.int32, (n, 2 * n), 0)
-        column = lax.broadcasted_iota(jnp.int32, (n, 2 * n), 1)
-        left = column < n
-        column = jnp.where(left, column, column - n)
-        inside = row < 0
-        for low in range(0, n, self.depth):
-            top = low + self.depth
-            inside = inside | ((row >= low) & (row < top) & (column >= low) & (column < top))
-        distance = jnp.abs(row - column)
-        self.third = banded(distance, MASS_BAND, inside & left) + banded(
-            distance, STIFF_BAND, inside & ~left
         )
 
     def partner(self, patch, face):
@@ -129,11 +116,8 @@
                     massed = massed + (MASS_BAND[offset] / SCALE) * both
                     stiffed = stiffed + (STIFF_BAND[offset] / SCALE) * both
             pieces = self.split(jnp.concatenate([massed, stiffed], axis=1))
-            mixed = None
-            for matrix, parts in ((self.high, pieces), (self.low, pieces[:2])):
-                for piece in parts:
-                    term = jnp.dot(piece, matrix[...], preferred_element_type=jnp.float32)
-                    mixed = term if mixed is None else mixed + term
+            pieces = jnp.concatenate(pieces + pieces[:2], axis=1)
+            mixed = jnp.dot(pieces, self.pieces[...], preferred_element_type=jnp.float32)
             a, b = 2 * (z % 2), 2 * (z % 2) + 1
             self.near[a, PAD : PAD + LANES] = mixed[:, :LANES]
             self.near[b, PAD : PAD + LANES] = mixed[:, LANES:]
@@ -147,21 +131,22 @@
                 mass = mass + MASS_BAND[o] * both
             finish(z, stiff, mass)
 
-    def strips(self, field, count=4):
+    def strips(self, field, slot=None, count=4):
         depth = field.shape[0]
         group = min(depth, 8)
+        if slot is None:
+            slot = 0
+            for z in range(depth):
+                rolled = pltpu.roll(field[z], (8 * (z % 8) + 4) % LANES, 1)
+                pltpu.store(self.strip.at[slot, z // 8], rolled, mask=(self.wide >> 3) == z % 8)
         rows0 = [field[:, d, :] for d in range(count)]
         rows1 = [field[:, LANES - 1 - d, :] for d in range(count)]
         wanted = list(range(4 - count, 4 + count))
         pieces = {i: [] for i in wanted}
         for start in range(0, depth, group):
-            stacked = jnp.zeros((LANES, LANES), jnp.float32)
-            for j in range(group):
-                rolled = pltpu.roll(field[start + j], (8 * j + 4) % LANES, 1)
-                stacked = jnp.where((self.wide >> 3) == j, rolled, stacked)
-            self.strip[...] = jnp.transpose(stacked)
+            self.turned[...] = jnp.transpose(self.strip[slot, start // 8])
             for i in wanted:
-                pieces[i].append(self.strip[pl.ds(i, group, stride=8), :])
+                pieces[i].append(self.turned[pl.ds(i, group, stride=8), :])
         columns = {i: jnp.concatenate(p, axis=0) if len(p) > 1 else p[0] for i, p in pieces.items()}
         return [
             rows0,
@@ -170,25 +155,43 @@
             [columns[3 - d] for d in range(count)],
         ]
 
-    def traces(self, field):
-        return [strip[0] for strip in self.strips(field, 1)]
+    def traces(self, field, slot=None):
+        return [strip[0] for strip in self.strips(field, slot, 1)]
 
     def jumps(self, mine, other):
         return [PENALTY * (a - b) for a, b in zip(mine, other)]
 
-    def stand(self, jump):
+    def stand(self, jump, slot=0):
         for start in range(0, self.depth, 8):
             self.turned[pl.ds(0, 8, stride=2), :] = jump[3][start : start + 8]
             self.turned[pl.ds(1, 8, stride=2), :] = jump[2][start : start + 8]
-            self.stood[start // 8] = jnp.transpose(self.turned[...])
-
-    def column(self, z):
-        rolled = pltpu.roll(self.stood[z // 8], (LANES - 2 * (z % 8) - 1) % LANES, 1)
+            self.stood[slot, start // 8] = jnp.transpose(self.turned[...])
+
+    def column(self, z, slot=0):
+        rolled = pltpu.roll(self.stood[slot, z // 8], (LANES - 2 * (z % 8) - 1) % LANES, 1)
         return jnp.where(self.edge, rolled, 0.0)
 
-    def add_rows(self, field, jump, factor):
-        field[:, 0, :] = field[:, 0, :] + factor * jump[0]
-        field[:, LANES - 1, :] = field[:, LANES - 1, :] + factor * jump[1]
+    def emit(self, field, z, value, jump=None, factor=1.0, slot=None):
+        field[z] = value
+        if jump is not None:
+            field[z, :1, :] = field[z, :1, :] + factor * jump[0][z : z + 1]
+            at = LANES - 1
+            field[z, at:, :] = field[z, at:, :] + factor * jump[1][z : z + 1]
+        if slot is not None:
+            rolled = pltpu.roll(field[z], (8 * (z % 8) + 4) % LANES, 1)
+            mask = (self.wide >> 3) == z % 8
+            pltpu.store(self.strip.at[slot, z // 8], rolled, mask=mask)
+
+    def lazy(self, field, make):
+        made = set()
+
+        def layer(z):
+            if z not in made:
+                made.add(z)
+                make(z)
+            return field[z]
+
+        return layer
 
     def stiff_trace(self, inner, jump):
         out = []
@@ -203,15 +206,27 @@
             out.append(inner[f] + jump[f] + self.ends(*ends))
         return out
 
-    def slab(self, stiffs, masses, plain=None):
+    def third_axis(self, value, band):
+        layer = lax.broadcasted_iota(jnp.int32, value.shape, 0)
+        out = band[0] * value
+        for o in (1, 2, 3):
+            low = jnp.where(layer >= o, pltpu.roll(value, o, 0), 0.0)
+            high = jnp.where(layer < self.depth - o, pltpu.roll(value, self.depth - o, 0), 0.0)
+            out = out + band[o] * (low + high)
+        return out
+
+    def slab(self, stiffs, masses, plain=None, arms=None):
         n = 4 * self.depth
-        rows = [stack(masses), stack(stiffs)] + ([] if plain is None else [stack(plain)])
+        rows = [stack(x) for x in (masses, stiffs, plain, arms) if x is not None]
         both = dot(stack(rows), self.plain)
         lower = both[n : 2 * n, :LANES] + both[:n, LANES:]
         if plain is not None:
-            lower = lower + both[2 * n :, :LANES]
-        out = dot(self.third, stack([lower, both[:n, :LANES]]))
-        return unstack(out, self.depth)
+            lower = lower + both[2 * n : 3 * n, :LANES]
+        out = [
+            self.third_axis(a, MASS_BAND) + self.third_axis(b, STIFF_BAND)
+            for a, b in zip(unstack(lower, self.depth), unstack(both[:n, :LANES], self.depth))
+        ]
+        return out if arms is None else (out, both[3 * n :])
 
     def depth_sum(self, strip, band):
         out = band[0] * strip[0]
@@ -219,12 +234,10 @@
             out = out + band[d] * strip[d]
         return out
 
-    def corner_table(self, trace, inner=None):
+    def corner_table(self, trace, inner=None, arms=None):
         table = jnp.zeros((self.depth, LANES), jnp.float32)
         ends = (0, LANES - 1)
         kinds = 1 if inner is None else KINDS
-        if inner is not None:
-            arms = dot(stack(trace), self.plain)
         for rs in range(2):
             for cs in range(2):
                 slot = kinds * (2 * rs + cs)
@@ -375,22 +388,21 @@
     body.send(payload, [trace, inner], body.pack(table, NARROW))
 
 
-def flux_tail(body, current, mine, other, r0, v1, m1, tr, tv, payload, potential):
+def flux_tail(body, layer, mine, other, r0, v1, m1, tr, tv, payload):
     jump = body.jumps(mine, other)
-    body.stand(jump)
+    body.stand(jump, 1)
 
     def residual(z, stiff, mass):
-        r0[z] = -TIME_STEP * (stiff + body.column(z))
-
-    body.stiff0(lambda z: potential[z], residual)
-    body.add_rows(r0, jump, -TIME_STEP)
+        body.emit(r0, z, -TIME_STEP * (stiff + body.column(z, 1)), jump, -TIME_STEP, 0)
+
+    body.stiff0(layer, residual)
 
     def image(z, stiff, mass):
-        v1[z] = stiff
+        body.emit(v1, z, stiff, slot=1)
         m1[z] = mass
 
     body.stiff0(lambda z: r0[z], image)
-    trace, inner = body.traces(r0), body.traces(v1)
+    trace, inner = body.traces(r0, 0), body.traces(v1, 1)
     tr[...], tv[...] = stack(trace), stack(inner)
     body.copies = 1
     body.send(payload, [trace, inner], body.pack(body.corner_table(trace), NARROW))
@@ -427,18 +439,19 @@
     mine = unstack(tc, depth)
     jump = body.jumps(mine, other)
     body.stand(jump)
-    for z in range(depth):
-        sc[z] = v0[z] + body.column(z)
-    body.add_rows(sc, jump, 1.0)
-    for z in range(depth):
+
+    def make(z):
+        body.emit(sc, z, v0[z] + body.column(z), jump)
         potential[z] = cubic(c[z], sc[z])
+
     mine_s = body.stiff_trace(unstack(tv0, depth), jump)
     other_s = body.other_stiff(recv, rows + depth, mine, other, inner, body.corners(), 1, NARROW)
     ts[...] = stack(mine_s)
     sides[0], sides[1] = stack(other), stack(other_s)
     mine_p = [cubic(x, s) for x, s in zip(mine, mine_s)]
     other_p = [cubic(x, s) for x, s in zip(other, other_s)]
-    flux_tail(body, c, mine_p, other_p, r0, v1, m1, tr, tv, payload, potential)
+    layer = body.lazy(potential, make)
+    flux_tail(body, layer, mine_p, other_p, r0, v1, m1, tr, tv, payload)
 
 
 def second_kernel(sizes, r0, v1, m1, tr, tv, recv, u1, y, v2, m2, ty, tv2, tu, sides, payload,
@@ -449,9 +462,10 @@
     mine = unstack(tr, depth)
     jump = body.jumps(mine, other)
     body.stand(jump)
-    for z in range(depth):
-        u1[z] = v1[z] + body.column(z)
-    body.add_rows(u1, jump, 1.0)
+
+    def make(z, jump=jump):
+        body.emit(u1, z, v1[z] + body.column(z), jump)
+
     mine_s = body.stiff_trace(unstack(tv, depth), jump)
     other_s = body.other_stiff(
         recv, 2 * depth, mine, other, inner, body.corners(), 1, NARROW
@@ -459,33 +473,34 @@
     tu[...] = stack(mine_s)
     sides[0], sides[1] = stack(other), stack(other_s)
     jump = body.jumps(mine_s, other_s)
-    body.stand(jump)
+    body.stand(jump, 1)
 
     def image(z, stiff, mass):
-        y[z] = m1[z] + TWICE * u1[z] + HALF * (stiff + body.column(z))
-
-    body.stiff0(lambda z: u1[z], image)
-    body.add_rows(y, jump, HALF)
+        value = m1[z] + TWICE * u1[z] + HALF * (stiff + body.column(z, 1))
+        body.emit(y, z, value, jump, HALF, 0)
+
+    body.stiff0(body.lazy(u1, make), image)
     sums = [[], [], []]
 
     def again(z, stiff, mass):
-        v2[z] = stiff
+        body.emit(v2, z, stiff, slot=1)
         m2[z] = mass
         a, b = r0[z], y[z]
         for i, product in enumerate((a * a, a * b, b * b)):
             sums[i].append(jnp.sum(product, axis=0, keepdims=True))
 
     body.stiff0(lambda z: y[z], again)
-    strips_y, strips = body.strips(y), body.strips(v2)
+    strips_y, strips = body.strips(y, 0), body.strips(v2, 1)
     trace, inner = [s[0] for s in strips_y], [s[0] for s in strips]
     ty[...], tv2[...] = stack(trace), stack(inner)
-    mixed = body.slab(
+    mixed, arms = body.slab(
         [HALF * body.depth_sum(s, STIFF_BAND) for s in strips],
         [HALF * body.depth_sum(s, MASS_BAND) for s in strips],
         [body.depth_sum(s, MASS_BAND) for s in strips_y],
+        trace,
     )
     outer = [TWICE * a + b for a, b in zip(inner, mixed)]
-    table = body.corner_table(trace, inner)
+    table = body.corner_table(trace, inner, arms)
     for i in range(3):
         total = jnp.sum(stack(sums[i]), axis=1, keepdims=True)
         table = jnp.where(body.lane == SUMS + i, total, table)
@@ -494,11 +509,11 @@
 
 def third_kernel(sizes, last, r0, y, v2, m2, ty, tv2, recv, *refs):
     if last:
-        t, base, payload, u2, zf, mt = refs[:6]
-        body = Body(sizes, refs[6:])
+        t, base, payload, u2, zf = refs[:5]
+        body = Body(sizes, refs[5:])
     else:
-        t, base, u2, zf, tt, tu2, tz, sides, payload, mt = refs[:10]
-        body = Body(sizes, refs[10:])
+        t, base, u2, zf, tt, tu2, tz, sides, payload = refs[:9]
+        body = Body(sizes, refs[9:])
     depth, patches = body.depth, body.patches
     at = 3 * depth
     packed = depth * BROAD // LANES
@@ -517,9 +532,10 @@
     mine = unstack(ty, depth)
     jump = body.jumps(mine, other)
     body.stand(jump)
-    for z in range(depth):
-        u2[z] = v2[z] + body.column(z)
-    body.add_rows(u2, jump, 1.0)
+
+    def make(z, jump=jump):
+        body.emit(u2, z, v2[z] + body.column(z), jump)
+
     mine_s = body.stiff_trace(unstack(tv2, depth), jump)
     other_s = body.other_stiff(recv, at, mine, other, inner, corners, KINDS, BROAD)
     masses, stiffs, far = [], [], []
@@ -548,31 +564,28 @@
         again = again + jnp.where(edge, PENALTY * (other_s[f] - far[f]), 0.0)
         image = outer[f] + TWICE * (other_s[f] - inner[f]) + HALF * again
         other_t.append(other[f] - a0 * image)
-    jump = body.jumps(mine_s, other_s)
-    body.stand(jump)
+    jump_s = body.jumps(mine_s, other_s)
+    body.stand(jump_s, 1)
 
     def turn(z, stiff, mass):
-        t[z] = y[z] - a0 * (m2[z] + TWICE * u2[z] + HALF * (stiff + body.column(z)))
-
-    body.stiff0(lambda z: u2[z], turn)
-    body.add_rows(t, jump, -HALF * a0)
-    mine_t = body.traces(t)
-    jump = body.jumps(mine_t, other_t)
-    body.stand(jump)
+        image = m2[z] + TWICE * u2[z] + HALF * (stiff + body.column(z, 1))
+        body.emit(t, z, y[z] - a0 * image, jump_s, -HALF * a0, 0)
+
+    body.stiff0(body.lazy(u2, make), turn)
+    mine_t = body.traces(t, 0)
+    jump_t = body.jumps(mine_t, other_t)
+    body.stand(jump_t)
+    sums = [jnp.zeros((8, LANES), jnp.float32)] * 6
 
     def image(z, stiff, mass):
-        zf[z] = stiff + body.column(z)
-        mt[z] = mass
-
-    body.stiff0(lambda z: t[z], image)
-    body.add_rows(zf, jump, 1.0)
-    sums = [jnp.zeros((8, LANES), jnp.float32)] * 6
-    for z in range(depth):
+        body.emit(zf, z, stiff + body.column(z), jump_t, slot=None if last else 1)
         b, x, s = y[z], t[z], zf[z]
         a = r0[z] - a0 * b
-        energy = x * (mt[z] + TWICE * s) + HALF * (s * s)
+        energy = x * (mass + TWICE * s) + HALF * (s * s)
         for i, product in enumerate((a * a, a * x, a * b, x * x, x * b, energy)):
             sums[i] = sums[i] + jnp.sum(product.reshape(LANES // 8, 8, LANES), axis=0)
+
+    body.stiff0(lambda z: t[z], image)
     moments = jnp.zeros((1, LANES), jnp.float32)
     lane = lax.broadcasted_iota(jnp.int32, (1, LANES), 1)
     for i, value in enumerate(sums):
@@ -584,7 +597,7 @@
     for to in range(patches):
         payload[to * rows : to * rows + 1, :] = moments
     if not last:
-        trace = body.traces(zf)
+        trace = body.traces(zf, 1)
         tt[...], tu2[...], tz[...] = stack(mine_t), stack(mine_s), stack(trace)
         sides[0], sides[1], sides[2] = stack(other), stack(other_s), stack(other_t)
         for f in range(4):
@@ -623,9 +636,10 @@
     def mix(*values):
         return values[0] + x[0] * values[1] + x[1] * values[2] + x[2] * values[3]
 
-    for z in range(depth):
+    def make(z):
         cn[z] = mix(c[z], r0[z], y[z], t[z])
         potential[z] = cubic(cn[z], mix(sc[z], u1[z], u2[z], zf[z]))
+
     (side_z,) = body.received(recv, 1, 1)
     mine = cubic(
         mix(tc[...], tr[...], ty[...], tt[...]), mix(ts[...], tu[...], tu2[...], tz[...])
@@ -634,8 +648,9 @@
         mix(side_c[0], side_r[0], side_y[0], side_y[2]),
         mix(side_c[1], side_r[1], side_y[1], stack(side_z)),
     )
-    flux_tail(body, cn, unstack(mine, depth), unstack(other, depth),
-              rn, v1, m1, trn, tvn, payload, potential)
+    layer = body.lazy(potential, make)
+    mine, other = unstack(mine, depth), unstack(other, depth)
+    flux_tail(body, layer, mine, other, rn, v1, m1, trn, tvn, payload)
 
 
 def last_kernel(patches, c, r0, y, t, base, recv, out):
@@ -675,9 +690,9 @@
         inside = [pltpu.VMEM((depth, LANES, LANES), jnp.float32)] * fields
         shared = [
             pltpu.VMEM((4, LANES + 2 * PAD, LANES), jnp.float32),
+            pltpu.VMEM((2, -(-depth // 8), LANES, LANES), jnp.float32),
             pltpu.VMEM((LANES, LANES), jnp.float32),
-            pltpu.VMEM((LANES, LANES), jnp.float32),
-            pltpu.VMEM((-(-depth // 8), LANES, LANES), jnp.float32),
+            pltpu.VMEM((2, -(-depth // 8), LANES, LANES), jnp.float32),
         ]
 
         def run(*refs):
@@ -737,7 +752,7 @@
             lambda sizes, *refs, last=last: third_kernel(sizes, last, *refs),
             outs,
             r0, y, v2, m2, ty, tv2, swap(payload),
-            fields=3 if last else 1,
+            fields=2 if last else 0,
         )
         if last:
             (payload,) = rest

time: 113 us -> 113 us (level)
  no operation moved by 1% of the time
where the time goes in v5:
time: 113 us
  blocking collectives  63.6 us (56%)
  Pallas kernels  31.6 us (28%)
  starting transfers between devices  7.86 us (7%)
  waiting for transfers between devices  7.82 us (7%)
  local copies, waits for them, and re-layouts  1.65 us (1%)
    all_to_all x6, blocking collectives, swap(): moved = lax.all_to_all(payload.reshape(parts, 1, rows * LANES), axes, 0, 0)  63.6 us
    pallas_call x8, Pallas kernels, call(): pl.pallas_call(run, out_shape=outs, in_specs=[smem] * 3 + [vmem] * (len(c...  30.6 us
    all_to_all x1, waiting for transfers between devices, swap(): moved = lax.all_to_all(payload.reshape(parts, 1, rows * LANES), axes, 0, 0)  7.82 us
    all_to_all x1, starting transfers between devices, swap(): moved = lax.all_to_all(payload.reshape(parts, 1, rows * LANES), axes, 0, 0)  4.89 us
    ppermute x1, starting transfers between devices, shards(): lax.ppermute(own, 'sec', [((i + k) % slabs, i) for i in range(slabs)])  2.97 us
  transfers between devices with their start and end apart: 2, of which 1 were waited for; matrix products, arithmetic and copies ran while one was open for 0% of the time, Pallas kernels for 3%

profile of v5, /device:TPU:0, one launch (start us, length us, event | category | flops | bytes accessed | tf_op | source)
XLA Modules:
  0.0 112.6 jit_solution(2135939805289323469)
XLA Ops:
  0.0 0.0 copy-start.3
  0.0 3.0 %collective-permute-start = (f32[4,128,128]{2,1,0:T(8,128)}, f32[4,128,128]{2,1,0:T(8,128)S(1)}, u32[]{:S(2)}, u32[]{:S(2)}) collective-permute-start(f32[4,128,128]{2,1,0:T(8,128)} %bitcast.58), channel_id=1, source_target_pairs={{1,0},{0,1},{3,2},{2,3},{5,4},{4,5},{7,6},{6,7},{9,8},{8,9},{11,10... | collective-permute-start | bytes 786440 | tf_op jit(solution)/shard_map/ppermute | solution.py:671
  3.0 0.0 copy-start.2
  3.0 0.0 copy-start.1
  3.0 0.0 copy-done.3
  3.0 0.7 copy-done.2
  3.7 0.0 copy-done.1
  3.7 0.0 copy-start.4
  3.7 0.9 copy-done.4
  4.6 0.0 copy-start
  4.6 1.7 %start_kernel.1 = f32[416,128]{1,0:T(8,128)} custom-call(s32[4,16]{1,0:T(4,128)S(1)} %bitcast.32, s32[4,16]{1,0:T(4,128)S(1)} %bitcast.40, s32[4,16]{1,0:T(4,128)S(1)} %bitcast.48, f32[4,128,128]{2,1,0:T(8,128)S(1)} %bitcast.59), custom_call_target="tpu_custom_call" | custom-call | flops 17179869184 | bytes 262144 | tf_op jit(solution)/shard_map/start_kernel/pallas_call | solution.py:703
  6.4 0.0 copy-start.5
  6.4 4.9 %all-to-all-start = ((f32[32,1,1664]{2,1,0:T(1,128)}), f32[32,1,1664]{2,1,0:T(1,128)S(1)}, u32[]{:S(2)}, u32[]{:S(2)}) async-start(f32[32,1,1664]{2,1,0:T(1,128)} %bitcast.4), calls=%async_computation | async-start | bytes 425984 | tf_op jit(solution)/shard_map/all_to_all | solution.py:716
  11.3 0.0 collective-permute-done.refs_5_
  11.3 0.0 copy-done
  11.3 0.0 copy-done.5
  11.3 2.1 %middle_kernel.1 = (f32[8,128,128]{2,1,0:T(8,128)S(1)}, f32[8,128,128]{2,1,0:T(8,128)S(1)}, f32[32,128]{1,0:T(8,128)S(1)}, f32[32,128]{1,0:T(8,128)S(1)}) custom-call(s32[4,16]{1,0:T(4,128)S(1)} %bitcast.33, s32[4,16]{1,0:T(4,128)S(1)} %bitcast.41, s32[4,16]{1,0:T(4,128)S(1)} %bitcast.49, bf16[1280,256]{1,0:T(8,128)(2,1)S(1)} %copy-done, ...), custom_call_target="tpu_custom_call" | custom-call | flops 17179869184 | bytes 262144 | tf_op jit(solution)/shard_map/middle_kernel/pallas_call | solution.py:703
  13.4 7.8 %all-to-all-done = f32[32,1,1664]{2,1,0:T(1,128)S(1)} async-done(((f32[32,1,1664]{2,1,0:T(1,128)}), f32[32,1,1664]{2,1,0:T(1,128)S(1)}, u32[]{:S(2)}, u32[]{:S(2)}) %all-to-all-start) | async-done | bytes 213024 | tf_op jit(solution)/shard_map/all_to_all | solution.py:716
  21.2 3.8 %first_kernel.1 = (f32[8,128,128]{2,1,0:T(8,128)S(1)}, f32[8,128,128]{2,1,0:T(8,128)S(1)}, f32[8,128,128]{2,1,0:T(8,128)S(1)}, f32[8,128,128]{2,1,0:T(8,128)S(1)...) custom-call(s32[4,16]{1,0:T(4,128)S(1)} %bitcast.34, ...), custom_call_target="tpu_custom_call" | custom-call | tf_op jit(solution)/shard_map/first_kernel/pallas_call | solution.py:703
  25.0 10.7 %all_to_all.35 = f32[16,1,2176]{2,1,0:T(1,128)S(1)} all-to-all(f32[16,1,2176]{2,1,0:T(1,128)S(1)} %bitcast.30), channel_id=1, replica_groups=mesh['patch'=16,'sec'=2] {'patch'}, dimensions={0} | all-to-all | bytes 278528 | tf_op jit(solution)/shard_map/all_to_all | solution.py:716
  35.7 4.5 %second_kernel.2 = (f32[8,128,128]{2,1,0:T(8,128)S(1)}, f32[8,128,128]{2,1,0:T(8,128)S(1)}, f32[8,128,128]{2,1,0:T(8,128)S(1)}, f32[8,128,128]{2,1,0:T(8,128)S(1...) custom-call(s32[4,16]{1,0:T(4,128)S(1)} %bitcast.35, ...), custom_call_target="tpu_custom_call" | custom-call | tf_op jit(solution)/shard_map/second_kernel/pallas_call | solution.py:703
  40.2 11.8 %all_to_all.36 = f32[16,1,3328]{2,1,0:T(1,128)S(1)} all-to-all(f32[16,1,3328]{2,1,0:T(1,128)S(1)} %bitcast.28), channel_id=1, replica_groups=mesh['patch'=16,'sec'=2] {'patch'}, dimensions={0} | all-to-all | bytes 425984 | tf_op jit(solution)/shard_map/all_to_all | solution.py:716
  52.1 4.7 %_lambda_.2 = (f32[8,128,128]{2,1,0:T(8,128)S(1)}, f32[8,128]{1,0:T(8,128)S(1)}, f32[8,128,128]{2,1,0:T(8,128)S(1)}, f32[8,128,128]{2,1,0:T(8,128)S(1)}, f32[32,...) custom-call(s32[4,16]{1,0:T(4,128)S(1)} %bitcast.36, ...), custom_call_target="tpu_custom_call" | custom-call | tf_op jit(solution)/shard_map/<lambda>/pallas_call | solution.py:703
  56.7 9.6 %all_to_all.37 = f32[16,1,1152]{2,1,0:T(1,128)S(1)} all-to-all(f32[16,1,1152]{2,1,0:T(1,128)S(1)} %bitcast.31), channel_id=1, replica_groups=mesh['patch'=16,'sec'=2] {'patch'}, dimensions={0} | all-to-all | bytes 147456 | tf_op jit(solution)/shard_map/all_to_all | solution.py:716
  66.3 4.0 %next_kernel.1 = (f32[8,128,128]{2,1,0:T(8,128)S(1)}, f32[8,128,128]{2,1,0:T(8,128)S(1)}, f32[8,128,128]{2,1,0:T(8,128)S(1)}, f32[8,128,128]{2,1,0:T(8,128)S(1)}...) custom-call(s32[4,16]{1,0:T(4,128)S(1)} %bitcast.37, s32[4,16]{1,0:T(4,128)S(1)} %bitcast.45, ...), custom_call_target="tpu_custom_call" | custom-call | tf_op jit(solution)/shard_map/next_kernel/pallas_call | solution.py:703
  70.3 10.7 %all_to_all.38 = f32[16,1,2176]{2,1,0:T(1,128)S(1)} all-to-all(f32[16,1,2176]{2,1,0:T(1,128)S(1)} %bitcast.29), channel_id=1, replica_groups=mesh['patch'=16,'sec'=2] {'patch'}, dimensions={0} | all-to-all | bytes 278528 | tf_op jit(solution)/shard_map/all_to_all | solution.py:716
  81.0 5.0 %second_kernel.3 = (f32[8,128,128]{2,1,0:T(8,128)}, f32[8,128,128]{2,1,0:T(8,128)S(1)}, f32[8,128,128]{2,1,0:T(8,128)S(1)}, f32[8,128,128]{2,1,0:T(8,128)S(1)}, ...) custom-call(s32[4,16]{1,0:T(4,128)S(1)} %bitcast.38, ...), custom_call_target="tpu_custom_call" | custom-call | tf_op jit(solution)/shard_map/second_kernel/pallas_call | solution.py:703
  86.0 11.8 %all_to_all.39 = f32[16,1,3328]{2,1,0:T(1,128)S(1)} all-to-all(f32[16,1,3328]{2,1,0:T(1,128)S(1)} %bitcast.27), channel_id=1, replica_groups=mesh['patch'=16,'sec'=2] {'patch'}, dimensions={0} | all-to-all | bytes 425984 | tf_op jit(solution)/shard_map/all_to_all | solution.py:716
  97.9 4.7 %_lambda_.3 = (f32[8,128,128]{2,1,0:T(8,128)S(1)}, f32[8,128]{1,0:T(8,128)S(1)}, f32[16,128]{1,0:T(8,128)S(1)}) custom-call(s32[4,16]{1,0:T(4,128)S(1)} %bitcast.39, s32[4,16]{1,0:T(4,128)S(1)} %bitcast.47, s32[4,16]{1,0:T(4,128)S(1)} %bitcast.55, bf16[1280,256]{1,0:T(8,128)(2,1)S(1)} %copy-done, f32[8,128,128]{2,1,0:T(8,128)S(1)} %get-tuple-element.84.refs_4_.r0, ...), custom_call_target="tpu_custom_call" | custom-call | tf_op jit(solution)/shard_map/<lambda>/pallas_call | solution.py:703
  102.6 9.0 %all_to_all.40 = f32[16,1,128]{2,1,0:T(1,128)S(1)} all-to-all(f32[16,1,128]{2,1,0:T(1,128)S(1)} %bitcast.57), channel_id=1, replica_groups=mesh['patch'=16,'sec'=2] {'patch'}, dimensions={0} | all-to-all | bytes 16384 | tf_op jit(solution)/shard_map/all_to_all | solution.py:716
  111.5 1.1 shard_map.55
Async XLA Ops:
  0.0 3.0 %copy-start.3 = (s32[16,4]{0,1:T(4,128)S(1)}, s32[16,4]{0,1:T(4,128)}, u32[]{:S(2)}) copy-start(s32[16,4]{0,1:T(4,128)} %param.8) | copy-start | bytes 772
  0.0 11.3 %collective-permute-start = (f32[4,128,128]{2,1,0:T(8,128)}, f32[4,128,128]{2,1,0:T(8,128)S(1)}, u32[]{:S(2)}, u32[]{:S(2)}) collective-permute-start(f32[4,128,128]{2,1,0:T(8,128)} %bitcast.58), channel_id=1, source_target_pairs={{1,0},{0,1},{3,2},{2,3},{5,4},{4,5},{7,6},{6,7},{9,8},{8,9},{11,10... | collective-permute-start | bytes 786440 | tf_op jit(solution)/shard_map/ppermute | solution.py:671
  3.0 0.7 copy-start.2
  3.0 0.7 copy-start.1
  3.7 0.9 copy-start.4
  4.6 6.7 %copy-start = (bf16[1280,256]{1,0:T(8,128)(2,1)S(1)}, bf16[1280,256]{1,0:T(8,128)(2,1)}, u32[]{:S(2)}) copy-start(bf16[1280,256]{1,0:T(8,128)(2,1)} %constant.2.clone.refs_3_) | copy-start | bytes 1966084
  6.4 4.9 %copy-start.5 = (f32[1,4,128,128]{3,2,1,0:T(8,128)S(1)}, f32[1,4,128,128]{3,2,1,0:T(8,128)}, u32[]{:S(2)}) copy-start(f32[1,4,128,128]{3,2,1,0:T(8,128)} %param.5) | copy-start | bytes 786436
  6.4 14.8 %all-to-all-start = ((f32[32,1,1664]{2,1,0:T(1,128)}), f32[32,1,1664]{2,1,0:T(1,128)S(1)}, u32[]{:S(2)}, u32[]{:S(2)}) async-start(f32[32,1,1664]{2,1,0:T(1,128)} %bitcast.4), calls=%async_computation | async-start | bytes 425984 | tf_op jit(solution)/shard_map/all_to_all | solution.py:716

commit v6 on v5

--- a/solution.py
+++ b/solution.py
@@ -50,7 +50,7 @@
 def constants():
     high = right_matrix(MASS_HIGH, STIFF_HIGH).astype(jnp.bfloat16)
     low = right_matrix(MASS_LOW, STIFF_LOW).astype(jnp.bfloat16)
-    return (np.concatenate([high, high, high, low, low]),)
+    return (np.concatenate([high, high, high, low]),)
 
 
 def banded(distance, band, inside=None):
@@ -99,10 +99,10 @@
                 value = value - piece.astype(jnp.float32)
         return pieces
 
-    def stiff0(self, layer, finish):
+    def stiff0(self, layer, finish, with_mass=False):
         depth = self.depth
         zeros = jnp.zeros((PAD, LANES), jnp.float32)
-        for i in range(4):
+        for i in range(8):
             self.near[i, :PAD] = zeros
             self.near[i, PAD + LANES :] = zeros
         for z in range(depth):
@@ -116,19 +116,23 @@
                     massed = massed + (MASS_BAND[offset] / SCALE) * both
                     stiffed = stiffed + (STIFF_BAND[offset] / SCALE) * both
             pieces = self.split(jnp.concatenate([massed, stiffed], axis=1))
-            pieces = jnp.concatenate(pieces + pieces[:2], axis=1)
+            pieces = jnp.concatenate(pieces + pieces[:1], axis=1)
             mixed = jnp.dot(pieces, self.pieces[...], preferred_element_type=jnp.float32)
-            a, b = 2 * (z % 2), 2 * (z % 2) + 1
-            self.near[a, PAD : PAD + LANES] = mixed[:, :LANES]
-            self.near[b, PAD : PAD + LANES] = mixed[:, LANES:]
-            stiff = STIFF_BAND[0] * mixed[:, :LANES] + MASS_BAND[0] * mixed[:, LANES:]
-            mass = MASS_BAND[0] * mixed[:, :LANES]
+            first, second = mixed[:, :LANES], mixed[:, LANES:]
+            at, inside = 4 * (z % 2), slice(PAD, PAD + LANES)
+            for o in (1, 2, 3):
+                self.near[at + o, inside] = STIFF_BAND[o] * first + MASS_BAND[o] * second
+            stiff = STIFF_BAND[0] * first + MASS_BAND[0] * second
             for o in (1, 2, 3):
                 low, high = slice(PAD - o, PAD - o + LANES), slice(PAD + o, PAD + o + LANES)
-                both = self.near[a, low] + self.near[a, high]
-                stiff = stiff + STIFF_BAND[o] * both
-                stiff = stiff + MASS_BAND[o] * (self.near[b, low] + self.near[b, high])
-                mass = mass + MASS_BAND[o] * both
+                stiff = stiff + (self.near[at + o, low] + self.near[at + o, high])
+            mass = None
+            if with_mass:
+                self.near[at, inside] = first
+                mass = MASS_BAND[0] * first
+                for o in (1, 2, 3):
+                    low, high = slice(PAD - o, PAD - o + LANES), slice(PAD + o, PAD + o + LANES)
+                    mass = mass + MASS_BAND[o] * (self.near[at, low] + self.near[at, high])
             finish(z, stiff, mass)
 
     def strips(self, field, slot=None, count=4):
@@ -401,7 +405,7 @@
         body.emit(v1, z, stiff, slot=1)
         m1[z] = mass
 
-    body.stiff0(lambda z: r0[z], image)
+    body.stiff0(lambda z: r0[z], image, True)
     trace, inner = body.traces(r0, 0), body.traces(v1, 1)
     tr[...], tv[...] = stack(trace), stack(inner)
     body.copies = 1
@@ -489,7 +493,7 @@
         for i, product in enumerate((a * a, a * b, b * b)):
             sums[i].append(jnp.sum(product, axis=0, keepdims=True))
 
-    body.stiff0(lambda z: y[z], again)
+    body.stiff0(lambda z: y[z], again, True)
     strips_y, strips = body.strips(y, 0), body.strips(v2, 1)
     trace, inner = [s[0] for s in strips_y], [s[0] for s in strips]
     ty[...], tv2[...] = stack(trace), stack(inner)
@@ -585,7 +589,7 @@
         for i, product in enumerate((a * a, a * x, a * b, x * x, x * b, energy)):
             sums[i] = sums[i] + jnp.sum(product.reshape(LANES // 8, 8, LANES), axis=0)
 
-    body.stiff0(lambda z: t[z], image)
+    body.stiff0(lambda z: t[z], image, True)
     moments = jnp.zeros((1, LANES), jnp.float32)
     lane = lax.broadcasted_iota(jnp.int32, (1, LANES), 1)
     for i, value in enumerate(sums):
@@ -689,7 +693,7 @@
         count, head = len(args), 3 + len(consts)
         inside = [pltpu.VMEM((depth, LANES, LANES), jnp.float32)] * fields
         shared = [
-            pltpu.VMEM((4, LANES + 2 * PAD, LANES), jnp.float32),
+            pltpu.VMEM((8, LANES + 2 * PAD, LANES), jnp.float32),
             pltpu.VMEM((2, -(-depth // 8), LANES, LANES), jnp.float32),
             pltpu.VMEM((LANES, LANES), jnp.float32),
             pltpu.VMEM((2, -(-depth // 8), LANES, LANES), jnp.float32),

time: 113 us -> 112 us (level)
  Pallas kernels: 31.6 us -> 30.2 us
    pallas_call x8, Pallas kernels: 30.6 us -> 29.1 us  [call(): pl.pallas_call(run, out_shape=outs, in_specs=[smem] * 3 + [vmem] * (len(c...]
where the time goes in v6:
time: 112 us
  blocking collectives  63.7 us (57%)
  Pallas kernels  30.2 us (27%)
  waiting for transfers between devices  8 us (7%)
  starting transfers between devices  7.86 us (7%)
  local copies, waits for them, and re-layouts  1.65 us (1%)
    all_to_all x6, blocking collectives, swap(): moved = lax.all_to_all(payload.reshape(parts, 1, rows * LANES), axes, 0, 0)  63.7 us
    pallas_call x8, Pallas kernels, call(): pl.pallas_call(run, out_shape=outs, in_specs=[smem] * 3 + [vmem] * (len(c...  29.1 us
    all_to_all x1, waiting for transfers between devices, swap(): moved = lax.all_to_all(payload.reshape(parts, 1, rows * LANES), axes, 0, 0)  8 us
    all_to_all x1, starting transfers between devices, swap(): moved = lax.all_to_all(payload.reshape(parts, 1, rows * LANES), axes, 0, 0)  4.89 us
    ppermute x1, starting transfers between devices, shards(): lax.ppermute(own, 'sec', [((i + k) % slabs, i) for i in range(slabs)])  2.97 us
  transfers between devices with their start and end apart: 2, of which 1 were waited for; matrix products, arithmetic and copies ran while one was open for 0% of the time, Pallas kernels for 3%

profile of v6, /device:TPU:0, one launch (start us, length us, event | category | flops | bytes accessed | tf_op | source)
XLA Modules:
  0.0 111.5 jit_solution(16021229968144347204)
XLA Ops:
  0.0 0.0 copy-start.3
  0.0 3.0 %collective-permute-start = (f32[4,128,128]{2,1,0:T(8,128)}, f32[4,128,128]{2,1,0:T(8,128)S(1)}, u32[]{:S(2)}, u32[]{:S(2)}) collective-permute-start(f32[4,128,128]{2,1,0:T(8,128)} %bitcast.58), channel_id=1, source_target_pairs={{1,0},{0,1},{3,2},{2,3},{5,4},{4,5},{7,6},{6,7},{9,8},{8,9},{11,10... | collective-permute-start | bytes 786440 | tf_op jit(solution)/shard_map/ppermute | solution.py:675
  3.0 0.0 copy-start.2
  3.0 0.0 copy-start.1
  3.0 0.0 copy-done.3
  3.0 0.7 copy-done.2
  3.7 0.0 copy-done.1
  3.7 0.0 copy-start.4
  3.7 0.9 copy-done.4
  4.6 0.0 copy-start
  4.6 1.7 %start_kernel.1 = f32[416,128]{1,0:T(8,128)} custom-call(s32[4,16]{1,0:T(4,128)S(1)} %bitcast.32, s32[4,16]{1,0:T(4,128)S(1)} %bitcast.40, s32[4,16]{1,0:T(4,128)S(1)} %bitcast.48, f32[4,128,128]{2,1,0:T(8,128)S(1)} %bitcast.59), custom_call_target="tpu_custom_call" | custom-call | flops 17179869184 | bytes 262144 | tf_op jit(solution)/shard_map/start_kernel/pallas_call | solution.py:707
  6.4 0.0 copy-start.5
  6.4 4.9 %all-to-all-start = ((f32[32,1,1664]{2,1,0:T(1,128)}), f32[32,1,1664]{2,1,0:T(1,128)S(1)}, u32[]{:S(2)}, u32[]{:S(2)}) async-start(f32[32,1,1664]{2,1,0:T(1,128)} %bitcast.4), calls=%async_computation | async-start | bytes 425984 | tf_op jit(solution)/shard_map/all_to_all | solution.py:720
  11.3 0.0 collective-permute-done.refs_5_
  11.3 0.0 copy-done
  11.3 0.0 copy-done.5
  11.3 1.9 %middle_kernel.1 = (f32[8,128,128]{2,1,0:T(8,128)S(1)}, f32[8,128,128]{2,1,0:T(8,128)S(1)}, f32[32,128]{1,0:T(8,128)S(1)}, f32[32,128]{1,0:T(8,128)S(1)}) custom-call(s32[4,16]{1,0:T(4,128)S(1)} %bitcast.33, s32[4,16]{1,0:T(4,128)S(1)} %bitcast.41, s32[4,16]{1,0:T(4,128)S(1)} %bitcast.49, bf16[1024,256]{1,0:T(8,128)(2,1)S(1)} %copy-done, ...), custom_call_target="tpu_custom_call" | custom-call | flops 17179869184 | bytes 262144 | tf_op jit(solution)/shard_map/middle_kernel/pallas_call | solution.py:707
  13.2 8.0 %all-to-all-done = f32[32,1,1664]{2,1,0:T(1,128)S(1)} async-done(((f32[32,1,1664]{2,1,0:T(1,128)}), f32[32,1,1664]{2,1,0:T(1,128)S(1)}, u32[]{:S(2)}, u32[]{:S(2)}) %all-to-all-start) | async-done | bytes 213024 | tf_op jit(solution)/shard_map/all_to_all | solution.py:720
  21.2 3.7 %first_kernel.1 = (f32[8,128,128]{2,1,0:T(8,128)S(1)}, f32[8,128,128]{2,1,0:T(8,128)S(1)}, f32[8,128,128]{2,1,0:T(8,128)S(1)}, f32[8,128,128]{2,1,0:T(8,128)S(1)...) custom-call(s32[4,16]{1,0:T(4,128)S(1)} %bitcast.34, ...), custom_call_target="tpu_custom_call" | custom-call | tf_op jit(solution)/shard_map/first_kernel/pallas_call | solution.py:707
  24.9 10.7 %all_to_all.35 = f32[16,1,2176]{2,1,0:T(1,128)S(1)} all-to-all(f32[16,1,2176]{2,1,0:T(1,128)S(1)} %bitcast.30), channel_id=1, replica_groups=mesh['patch'=16,'sec'=2] {'patch'}, dimensions={0} | all-to-all | bytes 278528 | tf_op jit(solution)/shard_map/all_to_all | solution.py:720
  35.5 4.2 %second_kernel.2 = (f32[8,128,128]{2,1,0:T(8,128)S(1)}, f32[8,128,128]{2,1,0:T(8,128)S(1)}, f32[8,128,128]{2,1,0:T(8,128)S(1)}, f32[8,128,128]{2,1,0:T(8,128)S(1...) custom-call(s32[4,16]{1,0:T(4,128)S(1)} %bitcast.35, ...), custom_call_target="tpu_custom_call" | custom-call | tf_op jit(solution)/shard_map/second_kernel/pallas_call | solution.py:707
  39.8 11.8 %all_to_all.36 = f32[16,1,3328]{2,1,0:T(1,128)S(1)} all-to-all(f32[16,1,3328]{2,1,0:T(1,128)S(1)} %bitcast.28), channel_id=1, replica_groups=mesh['patch'=16,'sec'=2] {'patch'}, dimensions={0} | all-to-all | bytes 425984 | tf_op jit(solution)/shard_map/all_to_all | solution.py:720
  51.6 4.5 %_lambda_.2 = (f32[8,128,128]{2,1,0:T(8,128)S(1)}, f32[8,128]{1,0:T(8,128)S(1)}, f32[8,128,128]{2,1,0:T(8,128)S(1)}, f32[8,128,128]{2,1,0:T(8,128)S(1)}, f32[32,...) custom-call(s32[4,16]{1,0:T(4,128)S(1)} %bitcast.36, ...), custom_call_target="tpu_custom_call" | custom-call | tf_op jit(solution)/shard_map/<lambda>/pallas_call | solution.py:707
  56.1 9.8 %all_to_all.37 = f32[16,1,1152]{2,1,0:T(1,128)S(1)} all-to-all(f32[16,1,1152]{2,1,0:T(1,128)S(1)} %bitcast.31), channel_id=1, replica_groups=mesh['patch'=16,'sec'=2] {'patch'}, dimensions={0} | all-to-all | bytes 147456 | tf_op jit(solution)/shard_map/all_to_all | solution.py:720
  65.9 3.8 %next_kernel.1 = (f32[8,128,128]{2,1,0:T(8,128)S(1)}, f32[8,128,128]{2,1,0:T(8,128)S(1)}, f32[8,128,128]{2,1,0:T(8,128)S(1)}, f32[8,128,128]{2,1,0:T(8,128)S(1)}...) custom-call(s32[4,16]{1,0:T(4,128)S(1)} %bitcast.37, s32[4,16]{1,0:T(4,128)S(1)} %bitcast.45, ...), custom_call_target="tpu_custom_call" | custom-call | tf_op jit(solution)/shard_map/next_kernel/pallas_call | solution.py:707
  69.7 10.7 %all_to_all.38 = f32[16,1,2176]{2,1,0:T(1,128)S(1)} all-to-all(f32[16,1,2176]{2,1,0:T(1,128)S(1)} %bitcast.29), channel_id=1, replica_groups=mesh['patch'=16,'sec'=2] {'patch'}, dimensions={0} | all-to-all | bytes 278528 | tf_op jit(solution)/shard_map/all_to_all | solution.py:720
  80.3 4.8 %second_kernel.3 = (f32[8,128,128]{2,1,0:T(8,128)}, f32[8,128,128]{2,1,0:T(8,128)S(1)}, f32[8,128,128]{2,1,0:T(8,128)S(1)}, f32[8,128,128]{2,1,0:T(8,128)S(1)}, ...) custom-call(s32[4,16]{1,0:T(4,128)S(1)} %bitcast.38, ...), custom_call_target="tpu_custom_call" | custom-call | tf_op jit(solution)/shard_map/second_kernel/pallas_call | solution.py:707
  85.2 11.8 %all_to_all.39 = f32[16,1,3328]{2,1,0:T(1,128)S(1)} all-to-all(f32[16,1,3328]{2,1,0:T(1,128)S(1)} %bitcast.27), channel_id=1, replica_groups=mesh['patch'=16,'sec'=2] {'patch'}, dimensions={0} | all-to-all | bytes 425984 | tf_op jit(solution)/shard_map/all_to_all | solution.py:720
  97.0 4.5 %_lambda_.3 = (f32[8,128,128]{2,1,0:T(8,128)S(1)}, f32[8,128]{1,0:T(8,128)S(1)}, f32[16,128]{1,0:T(8,128)S(1)}) custom-call(s32[4,16]{1,0:T(4,128)S(1)} %bitcast.39, s32[4,16]{1,0:T(4,128)S(1)} %bitcast.47, s32[4,16]{1,0:T(4,128)S(1)} %bitcast.55, bf16[1024,256]{1,0:T(8,128)(2,1)S(1)} %copy-done, f32[8,128,128]{2,1,0:T(8,128)S(1)} %get-tuple-element.84.refs_4_.r0, ...), custom_call_target="tpu_custom_call" | custom-call | tf_op jit(solution)/shard_map/<lambda>/pallas_call | solution.py:707
  101.5 9.0 %all_to_all.40 = f32[16,1,128]{2,1,0:T(1,128)S(1)} all-to-all(f32[16,1,128]{2,1,0:T(1,128)S(1)} %bitcast.57), channel_id=1, replica_groups=mesh['patch'=16,'sec'=2] {'patch'}, dimensions={0} | all-to-all | bytes 16384 | tf_op jit(solution)/shard_map/all_to_all | solution.py:720
  110.5 1.1 shard_map.55
Async XLA Ops:
  0.0 3.0 %copy-start.3 = (s32[16,4]{0,1:T(4,128)S(1)}, s32[16,4]{0,1:T(4,128)}, u32[]{:S(2)}) copy-start(s32[16,4]{0,1:T(4,128)} %param.8) | copy-start | bytes 772
  0.0 11.3 %collective-permute-start = (f32[4,128,128]{2,1,0:T(8,128)}, f32[4,128,128]{2,1,0:T(8,128)S(1)}, u32[]{:S(2)}, u32[]{:S(2)}) collective-permute-start(f32[4,128,128]{2,1,0:T(8,128)} %bitcast.58), channel_id=1, source_target_pairs={{1,0},{0,1},{3,2},{2,3},{5,4},{4,5},{7,6},{6,7},{9,8},{8,9},{11,10... | collective-permute-start | bytes 786440 | tf_op jit(solution)/shard_map/ppermute | solution.py:675
  3.0 0.7 copy-start.2
  3.0 0.7 copy-start.1
  3.7 0.9 copy-start.4
  4.6 6.7 %copy-start = (bf16[1024,256]{1,0:T(8,128)(2,1)S(1)}, bf16[1024,256]{1,0:T(8,128)(2,1)}, u32[]{:S(2)}) copy-start(bf16[1024,256]{1,0:T(8,128)(2,1)} %constant.2.clone.refs_3_) | copy-start | bytes 1572868
  6.4 4.9 %copy-start.5 = (f32[1,4,128,128]{3,2,1,0:T(8,128)S(1)}, f32[1,4,128,128]{3,2,1,0:T(8,128)}, u32[]{:S(2)}) copy-start(f32[1,4,128,128]{3,2,1,0:T(8,128)} %param.5) | copy-start | bytes 786436
  6.4 14.8 %all-to-all-start = ((f32[32,1,1664]{2,1,0:T(1,128)}), f32[32,1,1664]{2,1,0:T(1,128)S(1)}, u32[]{:S(2)}, u32[]{:S(2)}) async-start(f32[32,1,1664]{2,1,0:T(1,128)} %bitcast.4), calls=%async_computation | async-start | bytes 425984 | tf_op jit(solution)/shard_map/all_to_all | solution.py:720

commit v7 on v6

--- a/solution.py
+++ b/solution.py
@@ -67,19 +67,23 @@
         self.copies = copies
         self.tables, refs = refs[:3], refs[3:]
         self.near, self.strip, self.turned, self.stood = refs[-4:]
-        if len(refs) > 4:
-            self.pieces = refs[0]
+        self.pieces = refs[0] if len(refs) > 4 else None
         self.me = lax.axis_index("patch")
         self.lane = lax.broadcasted_iota(jnp.int32, (self.depth, LANES), 1)
         self.first, self.last = self.lane == 0, self.lane == LANES - 1
         self.wide = lax.broadcasted_iota(jnp.int32, (LANES, LANES), 1)
         self.edge = (self.wide == 0) | (self.wide == LANES - 1)
         row = lax.broadcasted_iota(jnp.int32, (LANES, LANES), 0)
-        self.reverse = jnp.where(row + self.wide == LANES - 1, 1.0, 0.0)
+        reverse = jnp.where(row + self.wide == LANES - 1, 1.0, 0.0).astype(jnp.bfloat16)
+        self.reverse = stack([reverse] * 3)
         distance = jnp.abs(row - self.wide)
-        self.plain = jnp.concatenate(
-            [banded(distance, MASS_BAND), banded(distance, STIFF_BAND)], axis=1
-        )
+        if self.pieces is None:
+            self.plain = jnp.concatenate(
+                [banded(distance, MASS_BAND), banded(distance, STIFF_BAND)], axis=1
+            )
+        else:
+            high = self.pieces[:LANES]
+            self.plain = stack([high, high, high, self.pieces[6 * LANES : 7 * LANES]])
 
     def partner(self, patch, face):
         return self.tables[0][face, patch]
@@ -210,6 +214,13 @@
             out.append(inner[f] + jump[f] + self.ends(*ends))
         return out
 
+    def lane_bands(self, value):
+        if self.pieces is None:
+            return dot(value, self.plain)
+        pieces = self.split(value * (1.0 / SCALE))
+        pieces = jnp.concatenate(pieces + pieces[:1], axis=1)
+        return jnp.dot(pieces, self.plain, preferred_element_type=jnp.float32)
+
     def third_axis(self, value, band):
         layer = lax.broadcasted_iota(jnp.int32, value.shape, 0)
         out = band[0] * value
@@ -222,7 +233,7 @@
     def slab(self, stiffs, masses, plain=None, arms=None):
         n = 4 * self.depth
         rows = [stack(x) for x in (masses, stiffs, plain, arms) if x is not None]
-        both = dot(stack(rows), self.plain)
+        both = self.lane_bands(stack(rows))
         lower = both[n : 2 * n, :LANES] + both[:n, LANES:]
         if plain is not None:
             lower = lower + both[2 * n : 3 * n, :LANES]
@@ -301,7 +312,8 @@
     def oriented(self, raw, count):
         depth = self.depth
         rows = count * depth
-        turned = dot(stack(raw), self.reverse)
+        pieces = jnp.concatenate(self.split(stack(raw)), axis=1)
+        turned = jnp.dot(pieces, self.reverse, preferred_element_type=jnp.float32)
         out = []
         for f in range(4):
             flipped = self.flip(self.me, f) == 1
@@ -458,8 +470,9 @@
     flux_tail(body, layer, mine_p, other_p, r0, v1, m1, tr, tv, payload)
 
 
-def second_kernel(sizes, r0, v1, m1, tr, tv, recv, u1, y, v2, m2, ty, tv2, tu, sides, payload,
-                  *refs):
+def second_kernel(sizes, last, r0, v1, m1, tr, tv, recv, y, v2, m2, ty, tv2, payload, u1, *refs):
+    if not last:
+        tu, sides, *refs = refs
     body = Body(sizes, refs)
     depth = body.depth
     other, inner = body.received(recv, 2)
@@ -474,8 +487,9 @@
     other_s = body.other_stiff(
         recv, 2 * depth, mine, other, inner, body.corners(), 1, NARROW
     )
-    tu[...] = stack(mine_s)
-    sides[0], sides[1] = stack(other), stack(other_s)
+    if not last:
+        tu[...] = stack(mine_s)
+        sides[0], sides[1] = stack(other), stack(other_s)
     jump = body.jumps(mine_s, other_s)
     body.stand(jump, 1)
 
@@ -712,7 +726,7 @@
             scratch_shapes=inside + shared,
             compiler_params=params,
             cost_estimate=cost,
-            name=kernel.__name__ if hasattr(kernel, "__name__") else "third_kernel",
+            name=kernel.__name__.strip("<>"),
         )(*tables, *consts, *args)
 
     def swap(payload, axes="patch", parts=patches):
@@ -741,12 +755,16 @@
         fields=1,
     )
     for step in range(STEPS):
-        u1, y, v2, m2, ty, tv2, tu, side_r, payload = call(
-            second_kernel,
-            [field] * 4 + [trace] * 3 + [sides(2), load(3 * depth + broad)],
+        last = step + 1 == STEPS
+        outs = [field] * 3 + [trace] * 2 + [load(3 * depth + broad)]
+        y, v2, m2, ty, tv2, payload, *rest = call(
+            lambda sizes, *refs, last=last: second_kernel(sizes, last, *refs),
+            outs + ([] if last else [field, trace, sides(2)]),
             r0, v1, m1, tr, tv, swap(payload),
+            fields=1 if last else 0,
         )
-        last = step + 1 == STEPS
+        if not last:
+            u1, tu, side_r = rest
         outs = [field, base]
         if last:
             outs += [load(1)]

time: 112 us -> 110 us (0.982)
  Pallas kernels: 30.2 us -> 28.8 us
    pallas_call x8, Pallas kernels: 29.1 us -> 27.7 us  [call(): pl.pallas_call(run, out_shape=outs, in_specs=[smem] * 3 + [vmem] * (len(c...]
where the time goes in v7:
time: 110 us
  blocking collectives  63.6 us (58%)
  Pallas kernels  28.8 us (26%)
  waiting for transfers between devices  8 us (7%)
  starting transfers between devices  7.86 us (7%)
  local copies, waits for them, and re-layouts  1.65 us (2%)
    all_to_all x6, blocking collectives, swap(): moved = lax.all_to_all(payload.reshape(parts, 1, rows * LANES), axes, 0, 0)  63.6 us
    pallas_call x8, Pallas kernels, call(): pl.pallas_call(run, out_shape=outs, in_specs=[smem] * 3 + [vmem] * (len(c...  27.7 us
    all_to_all x1, waiting for transfers between devices, swap(): moved = lax.all_to_all(payload.reshape(parts, 1, rows * LANES), axes, 0, 0)  8 us
    all_to_all x1, starting transfers between devices, swap(): moved = lax.all_to_all(payload.reshape(parts, 1, rows * LANES), axes, 0, 0)  4.89 us
    ppermute x1, starting transfers between devices, shards(): lax.ppermute(own, 'sec', [((i + k) % slabs, i) for i in range(slabs)])  2.97 us
  transfers between devices with their start and end apart: 2, of which 1 were waited for; matrix products, arithmetic and copies ran while one was open for 0% of the time, Pallas kernels for 3%

profile of v7, /device:TPU:0, one launch (start us, length us, event | category | flops | bytes accessed | tf_op | source)
XLA Modules:
  0.0 109.9 jit_solution(2633286883384573980)
XLA Ops:
  0.0 0.0 copy-start.3
  0.0 3.0 %collective-permute-start = (f32[4,128,128]{2,1,0:T(8,128)}, f32[4,128,128]{2,1,0:T(8,128)S(1)}, u32[]{:S(2)}, u32[]{:S(2)}) collective-permute-start(f32[4,128,128]{2,1,0:T(8,128)} %bitcast.58), channel_id=1, source_target_pairs={{1,0},{0,1},{3,2},{2,3},{5,4},{4,5},{7,6},{6,7},{9,8},{8,9},{11,10... | collective-permute-start | bytes 786440 | tf_op jit(solution)/shard_map/ppermute | solution.py:689
  3.0 0.0 copy-start.2
  3.0 0.0 copy-start.1
  3.0 0.0 copy-done.3
  3.0 0.7 copy-done.2
  3.7 0.0 copy-done.1
  3.7 0.0 copy-start.4
  3.7 0.9 copy-done.4
  4.6 0.0 copy-start
  4.6 1.7 %start_kernel.1 = f32[416,128]{1,0:T(8,128)} custom-call(s32[4,16]{1,0:T(4,128)S(1)} %bitcast.32, s32[4,16]{1,0:T(4,128)S(1)} %bitcast.40, s32[4,16]{1,0:T(4,128)S(1)} %bitcast.48, f32[4,128,128]{2,1,0:T(8,128)S(1)} %bitcast.59), custom_call_target="tpu_custom_call" | custom-call | flops 17179869184 | bytes 262144 | tf_op jit(solution)/shard_map/start_kernel/pallas_call | solution.py:721
  6.4 0.0 copy-start.5
  6.4 4.9 %all-to-all-start = ((f32[32,1,1664]{2,1,0:T(1,128)}), f32[32,1,1664]{2,1,0:T(1,128)S(1)}, u32[]{:S(2)}, u32[]{:S(2)}) async-start(f32[32,1,1664]{2,1,0:T(1,128)} %bitcast.4), calls=%async_computation | async-start | bytes 425984 | tf_op jit(solution)/shard_map/all_to_all | solution.py:734
  11.3 0.0 collective-permute-done.refs_5_
  11.3 0.0 copy-done
  11.3 0.0 copy-done.5
  11.3 1.9 %middle_kernel.1 = (f32[8,128,128]{2,1,0:T(8,128)S(1)}, f32[8,128,128]{2,1,0:T(8,128)S(1)}, f32[32,128]{1,0:T(8,128)S(1)}, f32[32,128]{1,0:T(8,128)S(1)}) custom-call(s32[4,16]{1,0:T(4,128)S(1)} %bitcast.33, s32[4,16]{1,0:T(4,128)S(1)} %bitcast.41, s32[4,16]{1,0:T(4,128)S(1)} %bitcast.49, bf16[1024,256]{1,0:T(8,128)(2,1)S(1)} %copy-done, ...), custom_call_target="tpu_custom_call" | custom-call | flops 17179869184 | bytes 262144 | tf_op jit(solution)/shard_map/middle_kernel/pallas_call | solution.py:721
  13.2 8.0 %all-to-all-done = f32[32,1,1664]{2,1,0:T(1,128)S(1)} async-done(((f32[32,1,1664]{2,1,0:T(1,128)}), f32[32,1,1664]{2,1,0:T(1,128)S(1)}, u32[]{:S(2)}, u32[]{:S(2)}) %all-to-all-start) | async-done | bytes 213024 | tf_op jit(solution)/shard_map/all_to_all | solution.py:734
  21.2 3.6 %first_kernel.1 = (f32[8,128,128]{2,1,0:T(8,128)S(1)}, f32[8,128,128]{2,1,0:T(8,128)S(1)}, f32[8,128,128]{2,1,0:T(8,128)S(1)}, f32[8,128,128]{2,1,0:T(8,128)S(1)...) custom-call(s32[4,16]{1,0:T(4,128)S(1)} %bitcast.34, ...), custom_call_target="tpu_custom_call" | custom-call | tf_op jit(solution)/shard_map/first_kernel/pallas_call | solution.py:721
  24.8 10.7 %all_to_all.35 = f32[16,1,2176]{2,1,0:T(1,128)S(1)} all-to-all(f32[16,1,2176]{2,1,0:T(1,128)S(1)} %bitcast.30), channel_id=1, replica_groups=mesh['patch'=16,'sec'=2] {'patch'}, dimensions={0} | all-to-all | bytes 278528 | tf_op jit(solution)/shard_map/all_to_all | solution.py:734
  35.4 3.9 %lambda.4 = (f32[8,128,128]{2,1,0:T(8,128)S(1)}, f32[8,128,128]{2,1,0:T(8,128)S(1)}, f32[8,128,128]{2,1,0:T(8,128)S(1)}, f32[32,128]{1,0:T(8,128)S(1)}, f32[32,1...) custom-call(s32[4,16]{1,0:T(4,128)S(1)} %bitcast.35, ...), custom_call_target="tpu_custom_call" | custom-call | tf_op jit(solution)/shard_map/lambda/pallas_call | solution.py:721
  39.4 11.8 %all_to_all.36 = f32[16,1,3328]{2,1,0:T(1,128)S(1)} all-to-all(f32[16,1,3328]{2,1,0:T(1,128)S(1)} %bitcast.27), channel_id=1, replica_groups=mesh['patch'=16,'sec'=2] {'patch'}, dimensions={0} | all-to-all | bytes 425984 | tf_op jit(solution)/shard_map/all_to_all | solution.py:734
  51.2 4.5 %lambda.5 = (f32[8,128,128]{2,1,0:T(8,128)S(1)}, f32[8,128]{1,0:T(8,128)S(1)}, f32[8,128,128]{2,1,0:T(8,128)S(1)}, f32[8,128,128]{2,1,0:T(8,128)S(1)}, f32[32,12...) custom-call(s32[4,16]{1,0:T(4,128)S(1)} %bitcast.36, ...), custom_call_target="tpu_custom_call" | custom-call | tf_op jit(solution)/shard_map/lambda/pallas_call | solution.py:721
  55.7 9.6 %all_to_all.37 = f32[16,1,1152]{2,1,0:T(1,128)S(1)} all-to-all(f32[16,1,1152]{2,1,0:T(1,128)S(1)} %bitcast.31), channel_id=1, replica_groups=mesh['patch'=16,'sec'=2] {'patch'}, dimensions={0} | all-to-all | bytes 147456 | tf_op jit(solution)/shard_map/all_to_all | solution.py:734
  65.3 3.7 %next_kernel.1 = (f32[8,128,128]{2,1,0:T(8,128)S(1)}, f32[8,128,128]{2,1,0:T(8,128)S(1)}, f32[8,128,128]{2,1,0:T(8,128)S(1)}, f32[8,128,128]{2,1,0:T(8,128)S(1)}...) custom-call(s32[4,16]{1,0:T(4,128)S(1)} %bitcast.37, s32[4,16]{1,0:T(4,128)S(1)} %bitcast.45, ...), custom_call_target="tpu_custom_call" | custom-call | tf_op jit(solution)/shard_map/next_kernel/pallas_call | solution.py:721
  69.0 10.7 %all_to_all.38 = f32[16,1,2176]{2,1,0:T(1,128)S(1)} all-to-all(f32[16,1,2176]{2,1,0:T(1,128)S(1)} %bitcast.29), channel_id=1, replica_groups=mesh['patch'=16,'sec'=2] {'patch'}, dimensions={0} | all-to-all | bytes 278528 | tf_op jit(solution)/shard_map/all_to_all | solution.py:734
  79.7 4.0 %lambda.6 = (f32[8,128,128]{2,1,0:T(8,128)S(1)}, f32[8,128,128]{2,1,0:T(8,128)S(1)}, f32[8,128,128]{2,1,0:T(8,128)S(1)}, f32[32,128]{1,0:T(8,128)S(1)}, f32[32,128]{1,0:T(8,128)S(1)}, /*index=5*/f32[416,128]{1,0:T(8,128)S(1)}) custom-call(s32[4,16]{1,0:T(4,128)S(1)} %bitcast.38, s32[4,16]{1,0:T(4,128)S(1)} %bitcast.46, s32[4,16]{1,0:T(4,128)S(1)} %bitcast.54, ...), custom_call_target="tpu_custom_call" | custom-call | tf_op jit(solution)/shard_map/lambda/pallas_call | solution.py:721
  83.7 11.8 %all_to_all.39 = f32[16,1,3328]{2,1,0:T(1,128)S(1)} all-to-all(f32[16,1,3328]{2,1,0:T(1,128)S(1)} %bitcast.28), channel_id=1, replica_groups=mesh['patch'=16,'sec'=2] {'patch'}, dimensions={0} | all-to-all | bytes 425984 | tf_op jit(solution)/shard_map/all_to_all | solution.py:734
  95.5 4.4 %lambda.7 = (f32[8,128,128]{2,1,0:T(8,128)S(1)}, f32[8,128]{1,0:T(8,128)S(1)}, f32[16,128]{1,0:T(8,128)S(1)}) custom-call(s32[4,16]{1,0:T(4,128)S(1)} %bitcast.39, s32[4,16]{1,0:T(4,128)S(1)} %bitcast.47, s32[4,16]{1,0:T(4,128)S(1)} %bitcast.55, bf16[1024,256]{1,0:T(8,128)(2,1)S(1)} %copy-done, f32[8,128,128]{2,1,0:T(8,128)S(1)} %get-tuple-element.84.refs_4_.r0, ...), custom_call_target="tpu_custom_call" | custom-call | tf_op jit(solution)/shard_map/lambda/pallas_call | solution.py:721
  99.9 9.0 %all_to_all.40 = f32[16,1,128]{2,1,0:T(1,128)S(1)} all-to-all(f32[16,1,128]{2,1,0:T(1,128)S(1)} %bitcast.57), channel_id=1, replica_groups=mesh['patch'=16,'sec'=2] {'patch'}, dimensions={0} | all-to-all | bytes 16384 | tf_op jit(solution)/shard_map/all_to_all | solution.py:734
  108.9 1.1 shard_map.55
Async XLA Ops:
  0.0 3.0 %copy-start.3 = (s32[16,4]{0,1:T(4,128)S(1)}, s32[16,4]{0,1:T(4,128)}, u32[]{:S(2)}) copy-start(s32[16,4]{0,1:T(4,128)} %param.8) | copy-start | bytes 772
  0.0 11.3 %collective-permute-start = (f32[4,128,128]{2,1,0:T(8,128)}, f32[4,128,128]{2,1,0:T(8,128)S(1)}, u32[]{:S(2)}, u32[]{:S(2)}) collective-permute-start(f32[4,128,128]{2,1,0:T(8,128)} %bitcast.58), channel_id=1, source_target_pairs={{1,0},{0,1},{3,2},{2,3},{5,4},{4,5},{7,6},{6,7},{9,8},{8,9},{11,10... | collective-permute-start | bytes 786440 | tf_op jit(solution)/shard_map/ppermute | solution.py:689
  3.0 0.7 copy-start.2
  3.0 0.7 copy-start.1
  3.7 0.9 copy-start.4
  4.6 6.7 %copy-start = (bf16[1024,256]{1,0:T(8,128)(2,1)S(1)}, bf16[1024,256]{1,0:T(8,128)(2,1)}, u32[]{:S(2)}) copy-start(bf16[1024,256]{1,0:T(8,128)(2,1)} %constant.2.clone.refs_3_) | copy-start | bytes 1572868
  6.4 4.9 %copy-start.5 = (f32[1,4,128,128]{3,2,1,0:T(8,128)S(1)}, f32[1,4,128,128]{3,2,1,0:T(8,128)}, u32[]{:S(2)}) copy-start(f32[1,4,128,128]{3,2,1,0:T(8,128)} %param.5) | copy-start | bytes 786436
  6.4 14.8 %all-to-all-start = ((f32[32,1,1664]{2,1,0:T(1,128)}), f32[32,1,1664]{2,1,0:T(1,128)S(1)}, u32[]{:S(2)}, u32[]{:S(2)}) async-start(f32[32,1,1664]{2,1,0:T(1,128)} %bitcast.4), calls=%async_computation | async-start | bytes 425984 | tf_op jit(solution)/shard_map/all_to_all | solution.py:734

commit v8 on v7

--- a/solution.py
+++ b/solution.py
@@ -404,6 +404,20 @@
     body.send(payload, [trace, inner], body.pack(table, NARROW))
 
 
+def fetch_kernel(sizes, partner, face_id, flip, own, payload, *refs):
+    here, sems, refs = refs[:4], refs[4], refs[5:]
+    sources = (partner, face_id, flip, own)
+    copies = [
+        pltpu.make_async_copy(source, target, sems.at[i])
+        for i, (source, target) in enumerate(zip(sources, here))
+    ]
+    for copy in copies:
+        copy.start()
+    for copy in copies:
+        copy.wait()
+    start_kernel(sizes, here[3], payload, *here[:3], *refs)
+
+
 def flux_tail(body, layer, mine, other, r0, v1, m1, tr, tv, payload):
     jump = body.jumps(mine, other)
     body.stand(jump, 1)
@@ -703,16 +717,16 @@
     def load(count):
         return shape(patches * count, LANES)
 
+    shared = [
+        pltpu.VMEM((8, LANES + 2 * PAD, LANES), jnp.float32),
+        pltpu.VMEM((2, -(-depth // 8), LANES, LANES), jnp.float32),
+        pltpu.VMEM((LANES, LANES), jnp.float32),
+        pltpu.VMEM((2, -(-depth // 8), LANES, LANES), jnp.float32),
+    ]
+
     def call(kernel, outs, *args, fields=0, consts=matrices, cost=None):
         count, head = len(args), 3 + len(consts)
         inside = [pltpu.VMEM((depth, LANES, LANES), jnp.float32)] * fields
-        shared = [
-            pltpu.VMEM((8, LANES + 2 * PAD, LANES), jnp.float32),
-            pltpu.VMEM((2, -(-depth // 8), LANES, LANES), jnp.float32),
-            pltpu.VMEM((LANES, LANES), jnp.float32),
-            pltpu.VMEM((2, -(-depth // 8), LANES, LANES), jnp.float32),
-        ]
-
         def run(*refs):
             common, rest = refs[:head], refs[head:]
             cut = len(rest) - len(shared)
@@ -734,14 +748,20 @@
         moved = lax.all_to_all(payload.reshape(parts, 1, rows * LANES), axes, 0, 0)
         return moved.reshape(parts * rows, LANES)
 
+    cost = pl.CostEstimate(flops=COST, bytes_accessed=4 * own.size, transcendentals=0)
     narrow, broad = depth * NARROW // LANES, depth * BROAD // LANES
-    (payload,) = call(
-        start_kernel,
-        [load(slabs * (rows + depth + narrow))],
-        own,
-        consts=[],
-        cost=pl.CostEstimate(flops=COST, bytes_accessed=4 * own.size, transcendentals=0),
-    )
+    payload = pl.pallas_call(
+        functools.partial(fetch_kernel, (depth, patches, slabs)),
+        out_shape=load(slabs * (rows + depth + narrow)),
+        in_specs=[pl.BlockSpec(memory_space=pltpu.HBM)] * 4,
+        out_specs=vmem,
+        scratch_shapes=[pltpu.SMEM((4, patches), jnp.int32)] * 3
+        + [pltpu.VMEM(own.shape, jnp.float32), pltpu.SemaphoreType.DMA((4,))]
+        + shared,
+        compiler_params=params,
+        cost_estimate=cost,
+        name="start_kernel",
+    )(*[pltpu.with_memory_space_constraint(x, pltpu.HBM) for x in (*tables, own)])
     c, v0, tc, tv0 = call(
         middle_kernel,
         [field, field, trace, trace],

time: 110 us -> 109 us (level)
  local copies, waits for them, and re-layouts: 1.65 us -> 0.03 us
    pallas_call x0 -> x1, Pallas kernels: none -> 2.16 us  [shards(): pl.pallas_call(functools.partial(fetch_kernel, (depth, patches, slabs)),...]
    pallas_call x8 -> x7, Pallas kernels: 27.7 us -> 26 us  [call(): pl.pallas_call(run, out_shape=outs, in_specs=[smem] * 3 + [vmem] * (len(c...]
    unnamed x12 -> x10, local copies, waits for them, and re-layouts: 1.65 us -> 0.03 us
  transfers between devices with their start and end apart: 2 -> 2, of which waited for: 1 -> 1; matrix products, arithmetic and copies ran while one was open for 0% -> 0% of each run, Pallas kernels for 3% -> 4%
where the time goes in v8:
time: 109 us
  blocking collectives  63.6 us (58%)
  Pallas kernels  29.2 us (27%)
  waiting for transfers between devices  7.97 us (7%)
  starting transfers between devices  7.87 us (7%)
    all_to_all x6, blocking collectives, swap(): moved = lax.all_to_all(payload.reshape(parts, 1, rows * LANES), axes, 0, 0)  63.6 us
    pallas_call x7, Pallas kernels, call(): pl.pallas_call(run, out_shape=outs, in_specs=[smem] * 3 + [vmem] * (len(c...  26 us
    all_to_all x1, waiting for transfers between devices, swap(): moved = lax.all_to_all(payload.reshape(parts, 1, rows * LANES), axes, 0, 0)  7.96 us
    all_to_all x1, starting transfers between devices, swap(): moved = lax.all_to_all(payload.reshape(parts, 1, rows * LANES), axes, 0, 0)  4.9 us
    ppermute x1, starting transfers between devices, shards(): lax.ppermute(own, 'sec', [((i + k) % slabs, i) for i in range(slabs)])  2.97 us
  transfers between devices with their start and end apart: 2, of which 1 were waited for; matrix products, arithmetic and copies ran while one was open for 0% of the time, Pallas kernels for 4%

profile of v8, /device:TPU:0, one launch (start us, length us, event | category | flops | bytes accessed | tf_op | source)
XLA Modules:
  0.0 108.8 jit_solution(10847075237356243700)
XLA Ops:
  0.0 3.0 %collective-permute-start = (f32[4,128,128]{2,1,0:T(8,128)}, f32[4,128,128]{2,1,0:T(8,128)S(1)}, u32[]{:S(2)}, u32[]{:S(2)}) collective-permute-start(f32[4,128,128]{2,1,0:T(8,128)} %bitcast.58), channel_id=1, source_target_pairs={{1,0},{0,1},{3,2},{2,3},{5,4},{4,5},{7,6},{6,7},{9,8},{8,9},{11,10... | collective-permute-start | bytes 786440 | tf_op jit(solution)/shard_map/ppermute | solution.py:703
  3.0 0.0 copy-start
  3.0 2.2 %start_kernel.1 = f32[416,128]{1,0:T(8,128)} custom-call(s32[4,16]{1,0:T(4,128)} %bitcast.32, s32[4,16]{1,0:T(4,128)} %bitcast.40, s32[4,16]{1,0:T(4,128)} %bitcast.48, f32[4,128,128]{2,1,0:T(8,128)} %bitcast.59), custom_call_target="tpu_custom_call" | custom-call | flops 17179869184 | bytes 262144 | tf_op jit(solution)/shard_map/start_kernel/pallas_call | solution.py:753
  5.1 0.0 copy-start.4
  5.1 0.0 copy-start.1
  5.2 0.0 copy-start.2
  5.2 0.0 copy-start.3
  5.2 4.9 %all-to-all-start = ((f32[32,1,1664]{2,1,0:T(1,128)}), f32[32,1,1664]{2,1,0:T(1,128)S(1)}, u32[]{:S(2)}, u32[]{:S(2)}) async-start(f32[32,1,1664]{2,1,0:T(1,128)} %bitcast.4), calls=%async_computation | async-start | bytes 425984 | tf_op jit(solution)/shard_map/all_to_all | solution.py:748
  10.1 0.0 collective-permute-done.refs_5_
  10.1 0.0 copy-done
  10.1 0.0 copy-done.4
  10.1 0.0 copy-done.1
  10.1 0.0 copy-done.2
  10.1 0.0 copy-done.3
  10.2 1.9 %middle_kernel.1 = (f32[8,128,128]{2,1,0:T(8,128)S(1)}, f32[8,128,128]{2,1,0:T(8,128)S(1)}, f32[32,128]{1,0:T(8,128)S(1)}, f32[32,128]{1,0:T(8,128)S(1)}) custom-call(s32[4,16]{1,0:T(4,128)S(1)} %bitcast.33, s32[4,16]{1,0:T(4,128)S(1)} %bitcast.41, s32[4,16]{1,0:T(4,128)S(1)} %bitcast.49, bf16[1024,256]{1,0:T(8,128)(2,1)S(1)} %copy-done, ...), custom_call_target="tpu_custom_call" | custom-call | flops 17179869184 | bytes 262144 | tf_op jit(solution)/shard_map/middle_kernel/pallas_call | solution.py:735
  12.1 8.0 %all-to-all-done = f32[32,1,1664]{2,1,0:T(1,128)S(1)} async-done(((f32[32,1,1664]{2,1,0:T(1,128)}), f32[32,1,1664]{2,1,0:T(1,128)S(1)}, u32[]{:S(2)}, u32[]{:S(2)}) %all-to-all-start) | async-done | bytes 213024 | tf_op jit(solution)/shard_map/all_to_all | solution.py:748
  20.0 3.6 %first_kernel.1 = (f32[8,128,128]{2,1,0:T(8,128)S(1)}, f32[8,128,128]{2,1,0:T(8,128)S(1)}, f32[8,128,128]{2,1,0:T(8,128)S(1)}, f32[8,128,128]{2,1,0:T(8,128)S(1)...) custom-call(s32[4,16]{1,0:T(4,128)S(1)} %bitcast.34, ...), custom_call_target="tpu_custom_call" | custom-call | tf_op jit(solution)/shard_map/first_kernel/pallas_call | solution.py:735
  23.6 10.7 %all_to_all.35 = f32[16,1,2176]{2,1,0:T(1,128)S(1)} all-to-all(f32[16,1,2176]{2,1,0:T(1,128)S(1)} %bitcast.30), channel_id=1, replica_groups=mesh['patch'=16,'sec'=2] {'patch'}, dimensions={0} | all-to-all | bytes 278528 | tf_op jit(solution)/shard_map/all_to_all | solution.py:748
  34.2 3.9 %lambda.4 = (f32[8,128,128]{2,1,0:T(8,128)S(1)}, f32[8,128,128]{2,1,0:T(8,128)S(1)}, f32[8,128,128]{2,1,0:T(8,128)S(1)}, f32[32,128]{1,0:T(8,128)S(1)}, f32[32,1...) custom-call(s32[4,16]{1,0:T(4,128)S(1)} %bitcast.35, ...), custom_call_target="tpu_custom_call" | custom-call | tf_op jit(solution)/shard_map/lambda/pallas_call | solution.py:735
  38.2 11.8 %all_to_all.36 = f32[16,1,3328]{2,1,0:T(1,128)S(1)} all-to-all(f32[16,1,3328]{2,1,0:T(1,128)S(1)} %bitcast.27), channel_id=1, replica_groups=mesh['patch'=16,'sec'=2] {'patch'}, dimensions={0} | all-to-all | bytes 425984 | tf_op jit(solution)/shard_map/all_to_all | solution.py:748
  50.0 4.5 %lambda.5 = (f32[8,128,128]{2,1,0:T(8,128)S(1)}, f32[8,128]{1,0:T(8,128)S(1)}, f32[8,128,128]{2,1,0:T(8,128)S(1)}, f32[8,128,128]{2,1,0:T(8,128)S(1)}, f32[32,12...) custom-call(s32[4,16]{1,0:T(4,128)S(1)} %bitcast.36, ...), custom_call_target="tpu_custom_call" | custom-call | tf_op jit(solution)/shard_map/lambda/pallas_call | solution.py:735
  54.6 9.6 %all_to_all.37 = f32[16,1,1152]{2,1,0:T(1,128)S(1)} all-to-all(f32[16,1,1152]{2,1,0:T(1,128)S(1)} %bitcast.31), channel_id=1, replica_groups=mesh['patch'=16,'sec'=2] {'patch'}, dimensions={0} | all-to-all | bytes 147456 | tf_op jit(solution)/shard_map/all_to_all | solution.py:748
  64.2 3.7 %next_kernel.1 = (f32[8,128,128]{2,1,0:T(8,128)S(1)}, f32[8,128,128]{2,1,0:T(8,128)S(1)}, f32[8,128,128]{2,1,0:T(8,128)S(1)}, f32[8,128,128]{2,1,0:T(8,128)S(1)}...) custom-call(s32[4,16]{1,0:T(4,128)S(1)} %bitcast.37, s32[4,16]{1,0:T(4,128)S(1)} %bitcast.45, ...), custom_call_target="tpu_custom_call" | custom-call | tf_op jit(solution)/shard_map/next_kernel/pallas_call | solution.py:735
  67.9 10.7 %all_to_all.38 = f32[16,1,2176]{2,1,0:T(1,128)S(1)} all-to-all(f32[16,1,2176]{2,1,0:T(1,128)S(1)} %bitcast.29), channel_id=1, replica_groups=mesh['patch'=16,'sec'=2] {'patch'}, dimensions={0} | all-to-all | bytes 278528 | tf_op jit(solution)/shard_map/all_to_all | solution.py:748
  78.5 4.0 %lambda.6 = (f32[8,128,128]{2,1,0:T(8,128)S(1)}, f32[8,128,128]{2,1,0:T(8,128)S(1)}, f32[8,128,128]{2,1,0:T(8,128)S(1)}, f32[32,128]{1,0:T(8,128)S(1)}, f32[32,128]{1,0:T(8,128)S(1)}, /*index=5*/f32[416,128]{1,0:T(8,128)S(1)}) custom-call(s32[4,16]{1,0:T(4,128)S(1)} %bitcast.38, s32[4,16]{1,0:T(4,128)S(1)} %bitcast.46, s32[4,16]{1,0:T(4,128)S(1)} %bitcast.54, ...), custom_call_target="tpu_custom_call" | custom-call | tf_op jit(solution)/shard_map/lambda/pallas_call | solution.py:735
  82.5 11.8 %all_to_all.39 = f32[16,1,3328]{2,1,0:T(1,128)S(1)} all-to-all(f32[16,1,3328]{2,1,0:T(1,128)S(1)} %bitcast.28), channel_id=1, replica_groups=mesh['patch'=16,'sec'=2] {'patch'}, dimensions={0} | all-to-all | bytes 425984 | tf_op jit(solution)/shard_map/all_to_all | solution.py:748
  94.4 4.4 %lambda.7 = (f32[8,128,128]{2,1,0:T(8,128)S(1)}, f32[8,128]{1,0:T(8,128)S(1)}, f32[16,128]{1,0:T(8,128)S(1)}) custom-call(s32[4,16]{1,0:T(4,128)S(1)} %bitcast.39, s32[4,16]{1,0:T(4,128)S(1)} %bitcast.47, s32[4,16]{1,0:T(4,128)S(1)} %bitcast.55, bf16[1024,256]{1,0:T(8,128)(2,1)S(1)} %copy-done, f32[8,128,128]{2,1,0:T(8,128)S(1)} %get-tuple-element.84.refs_4_.r0, ...), custom_call_target="tpu_custom_call" | custom-call | tf_op jit(solution)/shard_map/lambda/pallas_call | solution.py:735
  98.8 9.0 %all_to_all.40 = f32[16,1,128]{2,1,0:T(1,128)S(1)} all-to-all(f32[16,1,128]{2,1,0:T(1,128)S(1)} %bitcast.57), channel_id=1, replica_groups=mesh['patch'=16,'sec'=2] {'patch'}, dimensions={0} | all-to-all | bytes 16384 | tf_op jit(solution)/shard_map/all_to_all | solution.py:748
  107.7 1.1 shard_map.55
Async XLA Ops:
  0.0 10.1 %collective-permute-start = (f32[4,128,128]{2,1,0:T(8,128)}, f32[4,128,128]{2,1,0:T(8,128)S(1)}, u32[]{:S(2)}, u32[]{:S(2)}) collective-permute-start(f32[4,128,128]{2,1,0:T(8,128)} %bitcast.58), channel_id=1, source_target_pairs={{1,0},{0,1},{3,2},{2,3},{5,4},{4,5},{7,6},{6,7},{9,8},{8,9},{11,10... | collective-permute-start | bytes 786440 | tf_op jit(solution)/shard_map/ppermute | solution.py:703
  3.0 7.1 %copy-start = (bf16[1024,256]{1,0:T(8,128)(2,1)S(1)}, bf16[1024,256]{1,0:T(8,128)(2,1)}, u32[]{:S(2)}) copy-start(bf16[1024,256]{1,0:T(8,128)(2,1)} %constant.2.clone.refs_3_) | copy-start | bytes 1572868
  5.1 5.0 %copy-start.4 = (f32[1,4,128,128]{3,2,1,0:T(8,128)S(1)}, f32[1,4,128,128]{3,2,1,0:T(8,128)}, u32[]{:S(2)}) copy-start(f32[1,4,128,128]{3,2,1,0:T(8,128)} %param.5) | copy-start | bytes 786436
  5.1 5.0 %copy-start.1 = (s32[16,4]{0,1:T(4,128)S(1)}, s32[16,4]{0,1:T(4,128)}, u32[]{:S(2)}) copy-start(s32[16,4]{0,1:T(4,128)} %param.6) | copy-start | bytes 772
  5.2 5.0 %copy-start.2 = (s32[16,4]{0,1:T(4,128)S(1)}, s32[16,4]{0,1:T(4,128)}, u32[]{:S(2)}) copy-start(s32[16,4]{0,1:T(4,128)} %param.7) | copy-start | bytes 772
  5.2 5.0 %copy-start.3 = (s32[16,4]{0,1:T(4,128)S(1)}, s32[16,4]{0,1:T(4,128)}, u32[]{:S(2)}) copy-start(s32[16,4]{0,1:T(4,128)} %param.8) | copy-start | bytes 772
  5.2 14.8 %all-to-all-start = ((f32[32,1,1664]{2,1,0:T(1,128)}), f32[32,1,1664]{2,1,0:T(1,128)S(1)}, u32[]{:S(2)}, u32[]{:S(2)}) async-start(f32[32,1,1664]{2,1,0:T(1,128)} %bitcast.4), calls=%async_computation | async-start | bytes 425984 | tf_op jit(solution)/shard_map/all_to_all | solution.py:748

commit v9 on v8

--- a/solution.py
+++ b/solution.py
@@ -64,7 +64,7 @@
 class Body:
     def __init__(self, sizes, refs, copies=1):
         self.depth, self.patches, self.slabs = sizes
-        self.copies = copies
+        self.copies, self.spread = copies, {}
         self.tables, refs = refs[:3], refs[3:]
         self.near, self.strip, self.turned, self.stood = refs[-4:]
         self.pieces = refs[0] if len(refs) > 4 else None
@@ -345,6 +345,9 @@
     def look(self, recv, at, patch, lane, side, width):
         count = width // NARROW
         shift = (side * (LANES - 1) + LANES - lane) & (LANES - 1)
+        known = self.spread.get(id(patch))
+        if known is not None:
+            return pltpu.roll(known[1], shift, 1)
         packed = self.take(recv, patch, at, self.depth // 8 * count)
         odd = (lax.broadcasted_iota(jnp.int32, (8, LANES), 0) & 1) == 1
         out = []
@@ -353,7 +356,9 @@
             if count == 2:
                 spread = jnp.where(odd, packed[k + 1 : k + 2], spread)
             out.append(pltpu.roll(spread, 0, 1, stride=NARROW, stride_axis=0))
-        return pltpu.roll(stack(out) if len(out) > 1 else out[0], shift, 1)
+        spread = stack(out) if len(out) > 1 else out[0]
+        self.spread[id(patch)] = (patch, spread)
+        return pltpu.roll(spread, shift, 1)
 
     def ends(self, low, high):
         return jnp.where(self.first, low, jnp.where(self.last, high, 0.0))

time: 109 us -> 109 us (level)
  no operation moved by 1% of the time
where the time goes in v9:
time: 109 us
  blocking collectives  63.6 us (58%)
  Pallas kernels  29.2 us (27%)
  waiting for transfers between devices  7.97 us (7%)
  starting transfers between devices  7.87 us (7%)
    all_to_all x6, blocking collectives, swap(): moved = lax.all_to_all(payload.reshape(parts, 1, rows * LANES), axes, 0, 0)  63.6 us
    pallas_call x7, Pallas kernels, call(): pl.pallas_call(run, out_shape=outs, in_specs=[smem] * 3 + [vmem] * (len(c...  26 us
    all_to_all x1, waiting for transfers between devices, swap(): moved = lax.all_to_all(payload.reshape(parts, 1, rows * LANES), axes, 0, 0)  7.96 us
    all_to_all x1, starting transfers between devices, swap(): moved = lax.all_to_all(payload.reshape(parts, 1, rows * LANES), axes, 0, 0)  4.9 us
    ppermute x1, starting transfers between devices, shards(): lax.ppermute(own, 'sec', [((i + k) % slabs, i) for i in range(slabs)])  2.97 us
  transfers between devices with their start and end apart: 2, of which 1 were waited for; matrix products, arithmetic and copies ran while one was open for 0% of the time, Pallas kernels for 4%

profile of v9, /device:TPU:0, one launch (start us, length us, event | category | flops | bytes accessed | tf_op | source)
XLA Modules:
  0.0 108.8 jit_solution(10847075237356243700)
XLA Ops:
  0.0 3.0 %collective-permute-start = (f32[4,128,128]{2,1,0:T(8,128)}, f32[4,128,128]{2,1,0:T(8,128)S(1)}, u32[]{:S(2)}, u32[]{:S(2)}) collective-permute-start(f32[4,128,128]{2,1,0:T(8,128)} %bitcast.58), channel_id=1, source_target_pairs={{1,0},{0,1},{3,2},{2,3},{5,4},{4,5},{7,6},{6,7},{9,8},{8,9},{11,10... | collective-permute-start | bytes 786440 | tf_op jit(solution)/shard_map/ppermute | solution.py:708
  3.0 0.0 copy-start
  3.0 2.2 %start_kernel.1 = f32[416,128]{1,0:T(8,128)} custom-call(s32[4,16]{1,0:T(4,128)} %bitcast.32, s32[4,16]{1,0:T(4,128)} %bitcast.40, s32[4,16]{1,0:T(4,128)} %bitcast.48, f32[4,128,128]{2,1,0:T(8,128)} %bitcast.59), custom_call_target="tpu_custom_call" | custom-call | flops 17179869184 | bytes 262144 | tf_op jit(solution)/shard_map/start_kernel/pallas_call | solution.py:758
  5.1 0.0 copy-start.4
  5.1 0.0 copy-start.1
  5.2 0.0 copy-start.2
  5.2 0.0 copy-start.3
  5.2 4.9 %all-to-all-start = ((f32[32,1,1664]{2,1,0:T(1,128)}), f32[32,1,1664]{2,1,0:T(1,128)S(1)}, u32[]{:S(2)}, u32[]{:S(2)}) async-start(f32[32,1,1664]{2,1,0:T(1,128)} %bitcast.4), calls=%async_computation | async-start | bytes 425984 | tf_op jit(solution)/shard_map/all_to_all | solution.py:753
  10.1 0.0 collective-permute-done.refs_5_
  10.1 0.0 copy-done
  10.1 0.0 copy-done.4
  10.1 0.0 copy-done.1
  10.1 0.0 copy-done.2
  10.1 0.0 copy-done.3
  10.2 1.9 %middle_kernel.1 = (f32[8,128,128]{2,1,0:T(8,128)S(1)}, f32[8,128,128]{2,1,0:T(8,128)S(1)}, f32[32,128]{1,0:T(8,128)S(1)}, f32[32,128]{1,0:T(8,128)S(1)}) custom-call(s32[4,16]{1,0:T(4,128)S(1)} %bitcast.33, s32[4,16]{1,0:T(4,128)S(1)} %bitcast.41, s32[4,16]{1,0:T(4,128)S(1)} %bitcast.49, bf16[1024,256]{1,0:T(8,128)(2,1)S(1)} %copy-done, ...), custom_call_target="tpu_custom_call" | custom-call | flops 17179869184 | bytes 262144 | tf_op jit(solution)/shard_map/middle_kernel/pallas_call | solution.py:740
  12.1 8.0 %all-to-all-done = f32[32,1,1664]{2,1,0:T(1,128)S(1)} async-done(((f32[32,1,1664]{2,1,0:T(1,128)}), f32[32,1,1664]{2,1,0:T(1,128)S(1)}, u32[]{:S(2)}, u32[]{:S(2)}) %all-to-all-start) | async-done | bytes 213024 | tf_op jit(solution)/shard_map/all_to_all | solution.py:753
  20.0 3.6 %first_kernel.1 = (f32[8,128,128]{2,1,0:T(8,128)S(1)}, f32[8,128,128]{2,1,0:T(8,128)S(1)}, f32[8,128,128]{2,1,0:T(8,128)S(1)}, f32[8,128,128]{2,1,0:T(8,128)S(1)...) custom-call(s32[4,16]{1,0:T(4,128)S(1)} %bitcast.34, ...), custom_call_target="tpu_custom_call" | custom-call | tf_op jit(solution)/shard_map/first_kernel/pallas_call | solution.py:740
  23.6 10.7 %all_to_all.35 = f32[16,1,2176]{2,1,0:T(1,128)S(1)} all-to-all(f32[16,1,2176]{2,1,0:T(1,128)S(1)} %bitcast.30), channel_id=1, replica_groups=mesh['patch'=16,'sec'=2] {'patch'}, dimensions={0} | all-to-all | bytes 278528 | tf_op jit(solution)/shard_map/all_to_all | solution.py:753
  34.2 4.0 %lambda.4 = (f32[8,128,128]{2,1,0:T(8,128)S(1)}, f32[8,128,128]{2,1,0:T(8,128)S(1)}, f32[8,128,128]{2,1,0:T(8,128)S(1)}, f32[32,128]{1,0:T(8,128)S(1)}, f32[32,1...) custom-call(s32[4,16]{1,0:T(4,128)S(1)} %bitcast.35, ...), custom_call_target="tpu_custom_call" | custom-call | tf_op jit(solution)/shard_map/lambda/pallas_call | solution.py:740
  38.2 11.8 %all_to_all.36 = f32[16,1,3328]{2,1,0:T(1,128)S(1)} all-to-all(f32[16,1,3328]{2,1,0:T(1,128)S(1)} %bitcast.27), channel_id=1, replica_groups=mesh['patch'=16,'sec'=2] {'patch'}, dimensions={0} | all-to-all | bytes 425984 | tf_op jit(solution)/shard_map/all_to_all | solution.py:753
  50.0 4.5 %lambda.5 = (f32[8,128,128]{2,1,0:T(8,128)S(1)}, f32[8,128]{1,0:T(8,128)S(1)}, f32[8,128,128]{2,1,0:T(8,128)S(1)}, f32[8,128,128]{2,1,0:T(8,128)S(1)}, f32[32,12...) custom-call(s32[4,16]{1,0:T(4,128)S(1)} %bitcast.36, ...), custom_call_target="tpu_custom_call" | custom-call | tf_op jit(solution)/shard_map/lambda/pallas_call | solution.py:740
  54.6 9.6 %all_to_all.37 = f32[16,1,1152]{2,1,0:T(1,128)S(1)} all-to-all(f32[16,1,1152]{2,1,0:T(1,128)S(1)} %bitcast.31), channel_id=1, replica_groups=mesh['patch'=16,'sec'=2] {'patch'}, dimensions={0} | all-to-all | bytes 147456 | tf_op jit(solution)/shard_map/all_to_all | solution.py:753
  64.2 3.7 %next_kernel.1 = (f32[8,128,128]{2,1,0:T(8,128)S(1)}, f32[8,128,128]{2,1,0:T(8,128)S(1)}, f32[8,128,128]{2,1,0:T(8,128)S(1)}, f32[8,128,128]{2,1,0:T(8,128)S(1)}...) custom-call(s32[4,16]{1,0:T(4,128)S(1)} %bitcast.37, s32[4,16]{1,0:T(4,128)S(1)} %bitcast.45, ...), custom_call_target="tpu_custom_call" | custom-call | tf_op jit(solution)/shard_map/next_kernel/pallas_call | solution.py:740
  67.9 10.7 %all_to_all.38 = f32[16,1,2176]{2,1,0:T(1,128)S(1)} all-to-all(f32[16,1,2176]{2,1,0:T(1,128)S(1)} %bitcast.29), channel_id=1, replica_groups=mesh['patch'=16,'sec'=2] {'patch'}, dimensions={0} | all-to-all | bytes 278528 | tf_op jit(solution)/shard_map/all_to_all | solution.py:753
  78.5 4.0 %lambda.6 = (f32[8,128,128]{2,1,0:T(8,128)S(1)}, f32[8,128,128]{2,1,0:T(8,128)S(1)}, f32[8,128,128]{2,1,0:T(8,128)S(1)}, f32[32,128]{1,0:T(8,128)S(1)}, f32[32,128]{1,0:T(8,128)S(1)}, /*index=5*/f32[416,128]{1,0:T(8,128)S(1)}) custom-call(s32[4,16]{1,0:T(4,128)S(1)} %bitcast.38, s32[4,16]{1,0:T(4,128)S(1)} %bitcast.46, s32[4,16]{1,0:T(4,128)S(1)} %bitcast.54, ...), custom_call_target="tpu_custom_call" | custom-call | tf_op jit(solution)/shard_map/lambda/pallas_call | solution.py:740
  82.5 11.8 %all_to_all.39 = f32[16,1,3328]{2,1,0:T(1,128)S(1)} all-to-all(f32[16,1,3328]{2,1,0:T(1,128)S(1)} %bitcast.28), channel_id=1, replica_groups=mesh['patch'=16,'sec'=2] {'patch'}, dimensions={0} | all-to-all | bytes 425984 | tf_op jit(solution)/shard_map/all_to_all | solution.py:753
  94.3 4.4 %lambda.7 = (f32[8,128,128]{2,1,0:T(8,128)S(1)}, f32[8,128]{1,0:T(8,128)S(1)}, f32[16,128]{1,0:T(8,128)S(1)}) custom-call(s32[4,16]{1,0:T(4,128)S(1)} %bitcast.39, s32[4,16]{1,0:T(4,128)S(1)} %bitcast.47, s32[4,16]{1,0:T(4,128)S(1)} %bitcast.55, bf16[1024,256]{1,0:T(8,128)(2,1)S(1)} %copy-done, f32[8,128,128]{2,1,0:T(8,128)S(1)} %get-tuple-element.84.refs_4_.r0, ...), custom_call_target="tpu_custom_call" | custom-call | tf_op jit(solution)/shard_map/lambda/pallas_call | solution.py:740
  98.7 9.0 %all_to_all.40 = f32[16,1,128]{2,1,0:T(1,128)S(1)} all-to-all(f32[16,1,128]{2,1,0:T(1,128)S(1)} %bitcast.57), channel_id=1, replica_groups=mesh['patch'=16,'sec'=2] {'patch'}, dimensions={0} | all-to-all | bytes 16384 | tf_op jit(solution)/shard_map/all_to_all | solution.py:753
  107.7 1.1 shard_map.55
Async XLA Ops:
  0.0 10.1 %collective-permute-start = (f32[4,128,128]{2,1,0:T(8,128)}, f32[4,128,128]{2,1,0:T(8,128)S(1)}, u32[]{:S(2)}, u32[]{:S(2)}) collective-permute-start(f32[4,128,128]{2,1,0:T(8,128)} %bitcast.58), channel_id=1, source_target_pairs={{1,0},{0,1},{3,2},{2,3},{5,4},{4,5},{7,6},{6,7},{9,8},{8,9},{11,10... | collective-permute-start | bytes 786440 | tf_op jit(solution)/shard_map/ppermute | solution.py:708
  3.0 7.1 %copy-start = (bf16[1024,256]{1,0:T(8,128)(2,1)S(1)}, bf16[1024,256]{1,0:T(8,128)(2,1)}, u32[]{:S(2)}) copy-start(bf16[1024,256]{1,0:T(8,128)(2,1)} %constant.2.clone.refs_3_) | copy-start | bytes 1572868
  5.1 5.0 %copy-start.4 = (f32[1,4,128,128]{3,2,1,0:T(8,128)S(1)}, f32[1,4,128,128]{3,2,1,0:T(8,128)}, u32[]{:S(2)}) copy-start(f32[1,4,128,128]{3,2,1,0:T(8,128)} %param.5) | copy-start | bytes 786436
  5.1 5.0 %copy-start.1 = (s32[16,4]{0,1:T(4,128)S(1)}, s32[16,4]{0,1:T(4,128)}, u32[]{:S(2)}) copy-start(s32[16,4]{0,1:T(4,128)} %param.6) | copy-start | bytes 772
  5.2 5.0 %copy-start.2 = (s32[16,4]{0,1:T(4,128)S(1)}, s32[16,4]{0,1:T(4,128)}, u32[]{:S(2)}) copy-start(s32[16,4]{0,1:T(4,128)} %param.7) | copy-start | bytes 772
  5.2 5.0 %copy-start.3 = (s32[16,4]{0,1:T(4,128)S(1)}, s32[16,4]{0,1:T(4,128)}, u32[]{:S(2)}) copy-start(s32[16,4]{0,1:T(4,128)} %param.8) | copy-start | bytes 772
  5.2 14.8 %all-to-all-start = ((f32[32,1,1664]{2,1,0:T(1,128)}), f32[32,1,1664]{2,1,0:T(1,128)S(1)}, u32[]{:S(2)}, u32[]{:S(2)}) async-start(f32[32,1,1664]{2,1,0:T(1,128)} %bitcast.4), calls=%async_computation | async-start | bytes 425984 | tf_op jit(solution)/shard_map/all_to_all | solution.py:753
